TPU v7x, 256 devices: a whole 4x4x8 slice. The times are simulated.
256 devices in a mesh: segment: 8 (over x, core), expert: 32 (over y, z).
Axes of the slice: x: 4, y: 4, z: 8, core: 2. Of those that a mesh axis runs over, the one named last changes fastest.
Arguments:
- states: bfloat16 [8, 128, 7168], P('segment', 'expert'), may hold values from -6 to 6
- routing: int32 [8, 2, 128, 2], P('segment', None, 'expert'), may hold values from 0 to 7, all different within a row; in each aligned block of 4 rows (0 to 3, 4 to 7, ..., all dimensions but the last counted through in order) at most 2 rows name the same one
- route_weight: bfloat16 [8, 2, 128, 2], P('segment', None, 'expert'), may hold values from 0.19921875 to 1
- norm_gain: float32 [8, 7168], P('segment'), may hold values from 0.1 to 1.9
- gate_proj: bfloat16 [8, 7168, 8192], P('segment', None, 'expert'), may hold values from -0.0625 to 0.0625
- up_proj: bfloat16 [8, 7168, 8192], P('segment', None, 'expert'), may hold values from -0.0625 to 0.0625
- down_proj: bfloat16 [8, 8192, 7168], P('segment', 'expert'), may hold values from -0.1875 to 0.1875
Outputs:
- new_states: bfloat16 [8, 128, 7168], P('segment', 'expert')
Inputs may be any that keep to these rules, and one draw needn't show every extreme that they name: `routing`: in each aligned block of 4 rows (the rows of one device for one layer and pass) no expert is named by more than 2 rows, and some block reaches 2; each row names 2 different experts.
All inputs are finite; a program needn't handle non-finite values.
Results may differ from a plain program's by a relative error of at most 0.015.
Values may be sent and summed in bfloat16 or wider, within the bound.
A program may use at most 64 MiB of HBM per device.

v0:
```python
import jax
import jax.numpy as jnp
from jax import lax
from jax.sharding import PartitionSpec as P

GROUP = 4


def shifted(value, axis, steps):
    count = lax.axis_size(axis)
    pairs = [(source, (source + steps) % count) for source in range(count)]
    return lax.ppermute(value, axis, pairs)


def on_device(states, routing, route_weight, norm_gain, gate_proj, up_proj, down_proj):
    owners = lax.axis_size("expert")
    experts = owners // GROUP
    row_dev = states.shape[1]
    model_dim = states.shape[2]
    passes_count = routing.shape[1]
    top_k = routing.shape[3]
    capacity = max(2, min(row_dev, 2 * row_dev * top_k // experts))
    gain_row = norm_gain[0]
    gate_mat = gate_proj[0]
    up_mat = up_proj[0]
    down_mat = down_proj[0]
    expert_ids = jnp.arange(experts, dtype=jnp.int32)
    slot_ids = jnp.arange(capacity, dtype=jnp.int32)

    def expert_terms(slot_rows, slot_weight):
        lead_shape = slot_rows.shape[:2]
        flat_rows = slot_rows.reshape(-1, model_dim)
        gated = jnp.dot(flat_rows, gate_mat, preferred_element_type=jnp.float32)
        up_part = jnp.dot(flat_rows, up_mat, preferred_element_type=jnp.float32)
        inner_act = (jax.nn.silu(gated) * up_part).astype(jnp.bfloat16)
        partial_out = jnp.dot(inner_act, down_mat, preferred_element_type=jnp.float32)
        scaled = slot_weight.reshape(-1, 1).astype(jnp.float32) * partial_out
        return scaled.astype(jnp.bfloat16).reshape(lead_shape + (model_dim,))

    def advance(step_no, current):
        chosen = lax.dynamic_index_in_dim(routing[0], step_no, 0, keepdims=False)
        weights_now = lax.dynamic_index_in_dim(route_weight[0], step_no, 0, keepdims=False)
        picked = chosen[:, :, None] == expert_ids[None, None, :]
        dense_weight = jnp.sum(
            jnp.where(picked, weights_now[:, :, None].astype(jnp.float32), jnp.float32(0.0)), axis=1
        )
        current_f = current.astype(jnp.float32)
        inv_rms = lax.rsqrt(jnp.mean(current_f * current_f, axis=1, keepdims=True) + 1e-06)
        normed = (current_f * inv_rms * gain_row).astype(jnp.bfloat16)
        gathered, gathered_weight = (
            lax.all_gather(normed, "expert", axis=0, tiled=True),
            lax.all_gather(dense_weight.astype(jnp.bfloat16), "expert", axis=0, tiled=True),
        )
        own_expert = lax.axis_index("expert") // GROUP
        own_weight = lax.dynamic_index_in_dim(
            gathered_weight, own_expert, 1, keepdims=False
        ).reshape(owners, row_dev)
        member = own_weight > 0
        slot_rank = jnp.cumsum(member.astype(jnp.int32), axis=1) - 1
        placer = (member[:, None, :] & (slot_rank[:, None, :] == slot_ids[None, :, None])).astype(
            jnp.bfloat16
        )
        packed = jnp.einsum(
            "scr,srd->scd",
            placer,
            gathered.reshape(owners, row_dev, model_dim),
            preferred_element_type=jnp.float32,
        ).astype(jnp.bfloat16)
        packed_weight = jnp.sum(
            placer.astype(jnp.float32) * own_weight[:, None, :].astype(jnp.float32), axis=2
        ).astype(jnp.bfloat16)
        term_rows = expert_terms(packed, packed_weight)
        spread = jnp.einsum("scr,scd->srd", placer, term_rows, preferred_element_type=jnp.float32)
        branch_sum = (
            lax.psum_scatter(spread.astype(jnp.bfloat16), "expert", scatter_dimension=0, tiled=True)
            .astype(jnp.float32)
            .reshape(row_dev, model_dim)
        )
        updated = (current_f + branch_sum).astype(jnp.bfloat16)
        return shifted(updated, "segment", 1)

    finished = lax.fori_loop(0, passes_count, advance, states[0])
    return finished[None]


def solution(mesh):
    return jax.shard_map(
        on_device,
        mesh=mesh,
        in_specs=(
            P("segment", "expert", None),
            P("segment", None, "expert", None),
            P("segment", None, "expert", None),
            P("segment", None),
            P("segment", None, "expert"),
            P("segment", None, "expert"),
            P("segment", "expert", None),
        ),
        out_specs=P("segment", "expert", None),
        check_vma=False,
    )
```

profile of v0, /device:TPU:32, one launch (start us, length us, event | category | flops | bytes accessed | tf_op | source)
XLA Modules:
  0.0 515.3 jit_solution(18351627865680173956)
XLA Ops:
  6.5 0.8 copy.30
  7.4 500.8 %while.17 = (s32[]{:T(128)}, bf16[4,7168]{1,0:T(4,128)(2,1)S(1)}, s32[1,2,4,2]{2,3,1,0:T(2,128)}, bf16[1,2,4,2]{2,3,1,0:T(2,128)(2,1)}, f32[1,7168]{1,0:T(1,128)...) while((s32[]{:T(128)}, bf16[4,7168]{1,0:T(4,128)(2,1)S(1)}, ...), condition=%wide.region_6.7_spmd.clone, body=%wide.region_0.6_spmd.clone.sunk | while | flops 715611648 | bytes 40374308 | solution.py:82
  7.5 1.5 fusion.49
  9.1 0.7 dynamic-slice_bitcast_fusion.2
  10.5 45.3 %all-gather.7 = bf16[32,4,8]{2,1,0:T(4,128)(2,1)S(1)} all-gather(bf16[1,4,8]{2,1,0:T(4,128)(2,1)S(1)} %bitcast.67), channel_id=1, replica_groups=mesh['segment'=8,'expert'=32] {'expert'}, dimensions={0}, use_global_device_ids=true | all-gather | bytes 2112 | tf_op jit(solution)/shard_map/while/body/eval_jaxpr/all_gather | solution.py:52
  56.7 33.2 %all-gather.10.cloned.1.call-done = bf16[32,4,7168]{2,1,0:T(4,128)(2,1)} async-done(((bf16[1,4,7168]{2,1,0:T(4,128)(2,1)}), bf16[32,4,7168]{2,1,0:T(4,128)(2,1)}) %all-gather.10.cloned.1.call-update) | async-done | bytes 1835024 | tf_op jit(solution)/shard_map/while/body/eval_jaxpr/all_gather | solution.py:51
  89.9 2.6 convolution_convert_fusion.4
  92.9 2.8 fusion.51
  95.6 5.5 %fusion.52 = bf16[64,7168]{1,0:T(8,128)(2,1)S(1)} fusion(bf16[256,7168]{1,0:T(8,128)(2,1)} %get-tuple-element.402, bf16[64,7168]{1,0:T(8,128)(2,1)S(1)} %reshape.200, bf16[7168,256]{1,0:T(8,128)(2,1)} %get-tuple-element.401, f32[64]{0:T(128)S(1)} %reshape.202, f32[64,256]{1,0:T(8,128)S(1)} %fusion.51), kind=kOutput, calls=%fused_computation.4.clone.1 | convolution fusion | flops 470777856 | bytes 9240832 | tf_op jit(solution)/shard_map/while/body/eval_jaxpr/dot_general | solution.py:36
  101.4 2.5 convolution_convert_fusion.5
  104.6 149.6 %all-reduce.5.cloned.1.call-done = bf16[32,4,7168]{2,1,0:T(4,128)(2,1)} async-done(((bf16[32,4,7168]{2,1,0:T(4,128)(2,1)}), bf16[32,4,7168]{2,1,0:T(4,128)(2,1)}) %all-reduce.5.cloned.1.call-update) | async-done | bytes 1835024 | tf_op jit(solution)/shard_map/while
  254.2 1.5 fusion.53
  255.7 4.8 collective-permute-done
  260.7 1.5 fusion.49
  262.3 0.7 dynamic-slice_bitcast_fusion.2
  263.7 41.4 %all-gather.7 = bf16[32,4,8]{2,1,0:T(4,128)(2,1)S(1)} all-gather(bf16[1,4,8]{2,1,0:T(4,128)(2,1)S(1)} %bitcast.67), channel_id=1, replica_groups=mesh['segment'=8,'expert'=32] {'expert'}, dimensions={0}, use_global_device_ids=true | all-gather | bytes 2112 | tf_op jit(solution)/shard_map/while/body/eval_jaxpr/all_gather | solution.py:52
  306.0 31.5 %all-gather.10.cloned.1.call-done = bf16[32,4,7168]{2,1,0:T(4,128)(2,1)} async-done(((bf16[1,4,7168]{2,1,0:T(4,128)(2,1)}), bf16[32,4,7168]{2,1,0:T(4,128)(2,1)}) %all-gather.10.cloned.1.call-update) | async-done | bytes 1835024 | tf_op jit(solution)/shard_map/while/body/eval_jaxpr/all_gather | solution.py:51
  337.5 2.6 convolution_convert_fusion.4
  340.5 2.8 fusion.51
  343.2 5.5 %fusion.52 = bf16[64,7168]{1,0:T(8,128)(2,1)S(1)} fusion(bf16[256,7168]{1,0:T(8,128)(2,1)} %get-tuple-element.402, bf16[64,7168]{1,0:T(8,128)(2,1)S(1)} %reshape.200, bf16[7168,256]{1,0:T(8,128)(2,1)} %get-tuple-element.401, f32[64]{0:T(128)S(1)} %reshape.202, f32[64,256]{1,0:T(8,128)S(1)} %fusion.51), kind=kOutput, calls=%fused_computation.4.clone.1 | convolution fusion | flops 470777856 | bytes 9240832 | tf_op jit(solution)/shard_map/while/body/eval_jaxpr/dot_general | solution.py:36
  349.1 2.5 convolution_convert_fusion.5
  352.2 149.6 %all-reduce.5.cloned.1.call-done = bf16[32,4,7168]{2,1,0:T(4,128)(2,1)} async-done(((bf16[32,4,7168]{2,1,0:T(4,128)(2,1)}), bf16[32,4,7168]{2,1,0:T(4,128)(2,1)}) %all-reduce.5.cloned.1.call-update) | async-done | bytes 1835024 | tf_op jit(solution)/shard_map/while
  501.8 1.5 fusion.53
  503.4 4.8 collective-permute-done
  (51 shorter events, 6.9 us)
Async XLA Ops:
  7.4 82.5 %all-gather.10.cloned.1.call-start = ((), (), s32[]{:S(2)}) async-start(), calls=%async_computation | async-start | bytes 1892352 | tf_op jit(solution)/shard_map/while/body/eval_jaxpr/all_gather | solution.py:51
  9.0 245.2 %all-reduce.5.cloned.1.call-start = ((), (), s32[]{:S(2)}) async-start(), calls=%async_computation.1 | async-start | bytes 3670016 | tf_op jit(solution)/shard_map/while
  101.1 2.9 copy-start
  255.7 4.8 collective-permute-start
  260.5 77.0 %all-gather.10.cloned.1.call-start = ((), (), s32[]{:S(2)}) async-start(), calls=%async_computation | async-start | bytes 1892352 | tf_op jit(solution)/shard_map/while/body/eval_jaxpr/all_gather | solution.py:51
  262.2 239.6 %all-reduce.5.cloned.1.call-start = ((), (), s32[]{:S(2)}) async-start(), calls=%async_computation.1 | async-start | bytes 3670016 | tf_op jit(solution)/shard_map/while
  348.7 2.9 copy-start
  503.3 4.8 collective-permute-start
Sparse Core Ops, SparseCore 0:
  10.8 79.0 all-gather.9
  104.1 150.0 all-reduce.4
  263.9 73.5 all-gather.9
  351.7 150.0 all-reduce.4
where the time goes:
time: 517 us; the launch traced here: 515 us
  waiting for transfers between devices  374 us (72%)
  blocking collectives  86.7 us (17%)
  matrix products  26.7 us (5%)
  between operations  13.1 us (3%)
  other arithmetic  8.48 us (2%)
  local copies, waits for them, and re-layouts  6.36 us (1%)
    while x6, waiting for transfers between devices  299 us
    all_gather x2, blocking collectives, advance(): lax.all_gather(dense_weight.astype(jnp.bfloat16), 'expert', axis=0, tiled...  86.7 us
    all_gather x2, waiting for transfers between devices, advance(): lax.all_gather(normed, 'expert', axis=0, tiled=True)  64.7 us
    dot_general x2, matrix products, expert_terms(): jnp.dot(inner_act, down_mat, preferred_element_type=jnp.float32)  10.9 us
  transfers between devices with their start and end apart: 6, of which 6 were waited for; matrix products, arithmetic and copies ran while one was open for 1% of the time, Pallas kernels for 0%

commit v1 on v0

v1 whole, which is shorter than its diff:
```python
import jax
import jax.numpy as jnp
from jax import lax
from jax.sharding import PartitionSpec as P

GROUP = 4


def shifted(value, axis, steps):
    count = lax.axis_size(axis)
    pairs = [(source, (source + steps) % count) for source in range(count)]
    return lax.ppermute(value, axis, pairs)


def on_device(states, routing, route_weight, norm_gain, gate_proj, up_proj, down_proj):
    owners = lax.axis_size("expert")
    experts = owners // GROUP
    passes_count = routing.shape[1]
    row_dev = states.shape[1]
    capacity = 2
    gain_row = norm_gain[0]
    gate_mat = gate_proj[0]
    up_mat = up_proj[0]
    down_mat = down_proj[0]
    expert_ids = jnp.arange(experts, dtype=jnp.int32)
    slot_ids = jnp.arange(capacity, dtype=jnp.int32)
    owner_expert = jnp.arange(owners, dtype=jnp.int32) // GROUP

    current = states[0]
    for step_no in range(passes_count):
        chosen = routing[0, step_no]
        weights_now = route_weight[0, step_no]
        picked = chosen[:, :, None] == expert_ids[None, None, :]
        member = jnp.any(picked, axis=1)
        dense_weight = jnp.sum(
            jnp.where(picked, weights_now[:, :, None].astype(jnp.float32), jnp.float32(0.0)), axis=1
        )
        slot_rank = jnp.cumsum(member.astype(jnp.int32), axis=0) - 1
        placer = member.T[:, None, :] & (slot_rank.T[:, None, :] == slot_ids[None, :, None])
        placer_f = placer.astype(jnp.bfloat16)

        current_f = current.astype(jnp.float32)
        inv_rms = lax.rsqrt(jnp.mean(current_f * current_f, axis=1, keepdims=True) + 1e-06)
        normed = (current_f * inv_rms * gain_row).astype(jnp.bfloat16)

        packed = jnp.einsum(
            "jcr,rd->jcd", placer_f, normed, preferred_element_type=jnp.float32
        ).astype(jnp.bfloat16)
        packed_weight = jnp.sum(
            jnp.where(placer, dense_weight.T[:, None, :], jnp.float32(0.0)), axis=2
        ).astype(jnp.bfloat16)
        send_rows = packed[owner_expert]
        send_weight = packed_weight[owner_expert]
        got_rows = lax.all_to_all(send_rows, "expert", 0, 0, tiled=True)
        got_weight = lax.all_to_all(send_weight, "expert", 0, 0, tiled=True)

        flat_rows = got_rows.reshape(owners * capacity, -1)
        gated = jnp.dot(flat_rows, gate_mat, preferred_element_type=jnp.float32)
        up_part = jnp.dot(flat_rows, up_mat, preferred_element_type=jnp.float32)
        inner_act = (jax.nn.silu(gated) * up_part).astype(jnp.bfloat16)
        partial_out = jnp.dot(inner_act, down_mat, preferred_element_type=jnp.float32)
        scaled = got_weight.reshape(-1, 1).astype(jnp.float32) * partial_out
        terms = scaled.astype(jnp.bfloat16).reshape(owners, capacity, -1)

        back = lax.all_to_all(terms, "expert", 0, 0, tiled=True)
        back_placer = placer_f[owner_expert]
        summed = jnp.einsum(
            "ocr,ocd->rd", back_placer, back, preferred_element_type=jnp.float32
        )
        updated = (current_f + summed).astype(jnp.bfloat16)
        current = shifted(updated, "segment", 1)
    return current[None]


def solution(mesh):
    return jax.shard_map(
        on_device,
        mesh=mesh,
        in_specs=(
            P("segment", "expert", None),
            P("segment", None, "expert", None),
            P("segment", None, "expert", None),
            P("segment", None),
            P("segment", None, "expert"),
            P("segment", None, "expert"),
            P("segment", "expert", None),
        ),
        out_specs=P("segment", "expert", None),
        check_vma=False,
    )
```

time: 517 us -> 190 us (0.37)
  waiting for transfers between devices: 374 us -> 114 us
  blocking collectives: 86.7 us -> 0 us
  starting transfers between devices: 0.12 us -> 38.8 us
  between operations: 13.1 us -> 0.2 us
  local copies, waits for them, and re-layouts: 6.36 us -> 15.9 us
  matrix products: 26.7 us -> 18.4 us
  other arithmetic: 8.48 us -> 2.43 us
    while x6 -> x0, waiting for transfers between devices: 299 us -> none
    all_to_all x0 -> x6, waiting for transfers between devices: none -> 109 us  [the longest x2 51.8 us: on_device(): got_rows = lax.all_to_all(send_rows, 'expert', 0, 0, tiled=True)]
    all_gather x2 -> x0, blocking collectives: 86.7 us -> none  [advance(): lax.all_gather(dense_weight.astype(jnp.bfloat16), 'expert', axis=0, tiled...]
    all_gather x2 -> x0, waiting for transfers between devices: 64.7 us -> none  [advance(): lax.all_gather(normed, 'expert', axis=0, tiled=True)]
    all_to_all x0 -> x6, starting transfers between devices: none -> 38.8 us  [the longest x2 16.4 us: on_device(): got_weight = lax.all_to_all(send_weight, 'expert', 0, 0, tiled=True)]
    gather x0 -> x6, local copies, waits for them, and re-layouts: none -> 8.91 us  [the longest x2 6.52 us: on_device(): send_rows = packed[owner_expert]]
    dot_general x8, matrix products: 26.7 us -> 18.4 us  [the longest x2 10.9 us: on_device(): jnp.dot(inner_act, down_mat, preferred_element_type=jnp.float32)]
  transfers between devices with their start and end apart: 6 -> 8, of which waited for: 6 -> 7; matrix products, arithmetic and copies ran while one was open for 1% -> 7% of each run, Pallas kernels for 0% -> 0%
where the time goes in v1:
time: 190 us
  waiting for transfers between devices  114 us (60%)
  starting transfers between devices  38.8 us (20%)
  matrix products  18.4 us (10%)
  local copies, waits for them, and re-layouts  15.9 us (8%)
  other arithmetic  2.43 us (1%)
    all_to_all x2, waiting for transfers between devices, on_device(): got_rows = lax.all_to_all(send_rows, 'expert', 0, 0, tiled=True)  51.8 us
    all_to_all x2, waiting for transfers between devices, on_device(): back = lax.all_to_all(terms, 'expert', 0, 0, tiled=True)  49.9 us
    all_to_all x2, starting transfers between devices, on_device(): got_weight = lax.all_to_all(send_weight, 'expert', 0, 0, tiled=True)  16.4 us
    all_to_all x2, starting transfers between devices, on_device(): got_rows = lax.all_to_all(send_rows, 'expert', 0, 0, tiled=True)  12.1 us
    dot_general x2, matrix products, on_device(): jnp.dot(inner_act, down_mat, preferred_element_type=jnp.float32)  10.9 us
    all_to_all x2, starting transfers between devices, on_device(): back = lax.all_to_all(terms, 'expert', 0, 0, tiled=True)  10.3 us
    all_to_all x2, waiting for transfers between devices, on_device(): got_weight = lax.all_to_all(send_weight, 'expert', 0, 0, tiled=True)  7.51 us
    gather x2, local copies, waits for them, and re-layouts, on_device(): send_rows = packed[owner_expert]  6.52 us
  transfers between devices with their start and end apart: 8, of which 7 were waited for; matrix products, arithmetic and copies ran while one was open for 7% of the time, Pallas kernels for 0%

profile of v1, /device:TPU:32, one launch (start us, length us, event | category | flops | bytes accessed | tf_op | source)
XLA Modules:
  0.0 189.7 jit_solution(14911144798844311469)
XLA Ops:
  0.0 0.7 slice_bitcast_fusion.1
  3.2 11.4 %all-to-all-start = ((bf16[32,1,2]{2,1,0:T(2,128)(2,1)}), bf16[32,1,2]{2,1,0:T(2,128)(2,1)S(1)}, u32[]{:S(2)}, u32[]{:S(2)}) async-start(bf16[32,1,2]{2,1,0:T(2,128)(2,1)} %copy.54), calls=%async_computation | async-start | bytes 32768 | tf_op jit(solution)/shard_map/all_to_all | solution.py:55
  14.6 1.0 fusion.37
  15.6 1.1 convolution_convert_fusion.1
  16.9 3.3 %gather_fusion.2 = bf16[32,2,7168]{2,1,0:T(2,128)(2,1)} fusion(bf16[8,2,7168]{2,1,0:T(2,128)(2,1)S(1)} %copy.56, s32[1024]{0:T(1024)S(1)} %pad_clamp_fusion), kind=kCustom, calls=%fused_computation.2 | custom fusion | bytes 1835136 | tf_op jit(solution)/shard_map/gather | solution.py:52
  20.2 2.9 %all-to-all-done = bf16[32,1,2]{2,1,0:T(2,128)(2,1)S(1)} async-done(((bf16[32,1,2]{2,1,0:T(2,128)(2,1)}), bf16[32,1,2]{2,1,0:T(2,128)(2,1)S(1)}, u32[]{:S(2)}, u32[]{:S(2)}) %all-to-all-start) | async-done | bytes 160 | tf_op jit(solution)/shard_map/all_to_all | solution.py:55
  23.1 6.8 %all-to-all-start.1 = ((bf16[32,2,7168]{2,1,0:T(2,128)(2,1)}), bf16[32,2,7168]{2,1,0:T(2,128)(2,1)S(1)}, u32[]{:S(2)}, u32[]{:S(2)}) async-start(bf16[32,2,7168]{2,1,0:T(2,128)(2,1)} %gather_fusion.2), calls=%async_computation.1 | async-start | bytes 1835008 | tf_op jit(solution)/shard_map/all_to_all | solution.py:54
  30.1 25.1 %all-to-all-done.1 = bf16[32,2,7168]{2,1,0:T(2,128)(2,1)S(1)} async-done(((bf16[32,2,7168]{2,1,0:T(2,128)(2,1)}), bf16[32,2,7168]{2,1,0:T(2,128)(2,1)S(1)}, u32[]{:S(2)}, u32[]{:S(2)}) %all-to-all-start.1) | async-done | bytes 917536 | tf_op jit(solution)/shard_map/all_to_all | solution.py:54
  55.6 2.8 %fusion.14 = f32[64,256]{1,0:T(8,128)S(1)} fusion(bf16[64,7168]{1,0:T(8,128)(2,1)S(1)} %reshape.125, bf16[1,7168,256]{2,1,0:T(8,128)(2,1)} %param.11), kind=kOutput, calls=%fused_computation.26 | convolution fusion | flops 234881024 | bytes 4653056 | tf_op jit(solution)/shard_map/dot_general | solution.py:58
  58.3 5.5 %fusion = bf16[64,7168]{1,0:T(8,128)(2,1)S(1)} fusion(bf16[1,256,7168]{2,1,0:T(8,128)(2,1)} %param.13, f32[64]{0:T(128)S(1)} %reshape.131, bf16[64,7168]{1,0:T(8,128)(2,1)S(1)} %reshape.125, bf16[1,7168,256]{2,1,0:T(8,128)(2,1)} %param.12, f32[64,256]{1,0:T(8,128)S(1)} %fusion.14), kind=kOutput, calls=%fused_computation.8 | convolution fusion | flops 470777856 | bytes 9240832 | tf_op jit(solution)/shard_map/dot_general | solution.py:61
  63.8 1.3 reshape.126
  65.1 5.1 %all-to-all-start.2 = ((bf16[32,2,7168]{2,1,0:T(2,128)(2,1)}), bf16[32,2,7168]{2,1,0:T(2,128)(2,1)S(1)}, u32[]{:S(2)}, u32[]{:S(2)}) async-start(bf16[32,2,7168]{2,1,0:T(2,128)(2,1)} %reshape.126), calls=%async_computation.2 | async-start | bytes 1835008 | tf_op jit(solution)/shard_map/all_to_all | solution.py:65
  71.1 24.4 %all-to-all-done.2 = bf16[32,2,7168]{2,1,0:T(2,128)(2,1)S(1)} async-done(((bf16[32,2,7168]{2,1,0:T(2,128)(2,1)}), bf16[32,2,7168]{2,1,0:T(2,128)(2,1)S(1)}, u32[]{:S(2)}, u32[]{:S(2)}) %all-to-all-start.2) | async-done | bytes 917536 | tf_op jit(solution)/shard_map/all_to_all | solution.py:65
  97.1 5.1 %all-to-all-start.3 = ((bf16[32,1,2]{2,1,0:T(2,128)(2,1)}), bf16[32,1,2]{2,1,0:T(2,128)(2,1)S(1)}, u32[]{:S(2)}, u32[]{:S(2)}) async-start(bf16[32,1,2]{2,1,0:T(2,128)(2,1)} %copy.63), calls=%async_computation.3 | async-start | bytes 32768 | tf_op jit(solution)/shard_map/all_to_all | solution.py:55
  102.9 3.3 %gather_fusion.5 = bf16[32,2,7168]{2,1,0:T(2,128)(2,1)} fusion(bf16[8,2,7168]{2,1,0:T(2,128)(2,1)S(1)} %copy.65, s32[1024]{0:T(1024)S(1)} %pad_clamp_fusion), kind=kCustom, calls=%fused_computation.5 | custom fusion | bytes 1835136 | tf_op jit(solution)/shard_map/gather | solution.py:52
  106.1 4.6 %all-to-all-done.3 = bf16[32,1,2]{2,1,0:T(2,128)(2,1)S(1)} async-done(((bf16[32,1,2]{2,1,0:T(2,128)(2,1)}), bf16[32,1,2]{2,1,0:T(2,128)(2,1)S(1)}, u32[]{:S(2)}, u32[]{:S(2)}) %all-to-all-start.3) | async-done | bytes 160 | tf_op jit(solution)/shard_map/all_to_all | solution.py:55
  110.7 5.2 %all-to-all-start.4 = ((bf16[32,2,7168]{2,1,0:T(2,128)(2,1)}), bf16[32,2,7168]{2,1,0:T(2,128)(2,1)S(1)}, u32[]{:S(2)}, u32[]{:S(2)}) async-start(bf16[32,2,7168]{2,1,0:T(2,128)(2,1)} %gather_fusion.5), calls=%async_computation.4 | async-start | bytes 1835008 | tf_op jit(solution)/shard_map/all_to_all | solution.py:54
  116.1 26.7 %all-to-all-done.4 = bf16[32,2,7168]{2,1,0:T(2,128)(2,1)S(1)} async-done(((bf16[32,2,7168]{2,1,0:T(2,128)(2,1)}), bf16[32,2,7168]{2,1,0:T(2,128)(2,1)S(1)}, u32[]{:S(2)}, u32[]{:S(2)}) %all-to-all-start.4) | async-done | bytes 917536 | tf_op jit(solution)/shard_map/all_to_all | solution.py:54
  143.1 2.8 %fusion.12 = f32[64,256]{1,0:T(8,128)S(1)} fusion(bf16[64,7168]{1,0:T(8,128)(2,1)S(1)} %reshape.127, bf16[1,7168,256]{2,1,0:T(8,128)(2,1)} %param.11), kind=kOutput, calls=%fused_computation.24 | convolution fusion | flops 234881024 | bytes 4653056 | tf_op jit(solution)/shard_map/dot_general | solution.py:58
  145.9 5.5 %fusion.1 = bf16[64,7168]{1,0:T(8,128)(2,1)S(1)} fusion(bf16[1,256,7168]{2,1,0:T(8,128)(2,1)} %param.13, f32[64]{0:T(128)S(1)} %reshape.133, bf16[64,7168]{1,0:T(8,128)(2,1)S(1)} %reshape.127, bf16[1,7168,256]{2,1,0:T(8,128)(2,1)} %param.12, f32[64,256]{1,0:T(8,128)S(1)} %fusion.12), kind=kOutput, calls=%fused_computation.9 | convolution fusion | flops 470777856 | bytes 9240832 | tf_op jit(solution)/shard_map/dot_general | solution.py:61
  151.3 1.3 reshape.128
  152.6 5.3 %all-to-all-start.5 = ((bf16[32,2,7168]{2,1,0:T(2,128)(2,1)}), bf16[32,2,7168]{2,1,0:T(2,128)(2,1)S(1)}, u32[]{:S(2)}, u32[]{:S(2)}) async-start(bf16[32,2,7168]{2,1,0:T(2,128)(2,1)} %reshape.128), calls=%async_computation.5 | async-start | bytes 1835008 | tf_op jit(solution)/shard_map/all_to_all | solution.py:65
  158.5 25.5 %all-to-all-done.5 = bf16[32,2,7168]{2,1,0:T(2,128)(2,1)S(1)} async-done(((bf16[32,2,7168]{2,1,0:T(2,128)(2,1)}), bf16[32,2,7168]{2,1,0:T(2,128)(2,1)S(1)}, u32[]{:S(2)}, u32[]{:S(2)}) %all-to-all-start.5) | async-done | bytes 917536 | tf_op jit(solution)/shard_map/all_to_all | solution.py:65
  184.3 4.8 %collective-permute-done.1 = bf16[4,7168]{1,0:T(4,128)(2,1)S(1)} collective-permute-done((bf16[4,7168]{1,0:T(4,128)(2,1)S(1)}, bf16[4,7168]{1,0:T(4,128)(2,1)S(1)}, u32[]{:S(2)}, u32[]{:S(2)}) %collective-permute-start.1) | collective-permute-done | bytes 57376 | tf_op jit(solution)/shard_map/ppermute | solution.py:12
  (47 shorter events, 8.5 us)
Async XLA Ops:
  3.2 19.9 %all-to-all-start = ((bf16[32,1,2]{2,1,0:T(2,128)(2,1)}), bf16[32,1,2]{2,1,0:T(2,128)(2,1)S(1)}, u32[]{:S(2)}, u32[]{:S(2)}) async-start(bf16[32,1,2]{2,1,0:T(2,128)(2,1)} %copy.54), calls=%async_computation | async-start | bytes 32768 | tf_op jit(solution)/shard_map/all_to_all | solution.py:55
  23.1 32.1 %all-to-all-start.1 = ((bf16[32,2,7168]{2,1,0:T(2,128)(2,1)}), bf16[32,2,7168]{2,1,0:T(2,128)(2,1)S(1)}, u32[]{:S(2)}, u32[]{:S(2)}) async-start(bf16[32,2,7168]{2,1,0:T(2,128)(2,1)} %gather_fusion.2), calls=%async_computation.1 | async-start | bytes 1835008 | tf_op jit(solution)/shard_map/all_to_all | solution.py:54
  63.8 31.7 %copy-start = (bf16[1,4,7168]{2,1,0:T(4,128)(2,1)S(1)}, bf16[1,4,7168]{2,1,0:T(4,128)(2,1)}, u32[]{:S(2)}) copy-start(bf16[1,4,7168]{2,1,0:T(4,128)(2,1)} %param.7) | copy-start | bytes 172036
  63.8 38.5 %copy-start.1 = (f32[1,7168]{1,0:T(1,128)S(1)}, f32[1,7168]{1,0:T(1,128)}, u32[]{:S(2)}) copy-start(f32[1,7168]{1,0:T(1,128)} %param.10) | copy-start | bytes 86020
  65.1 30.4 %all-to-all-start.2 = ((bf16[32,2,7168]{2,1,0:T(2,128)(2,1)}), bf16[32,2,7168]{2,1,0:T(2,128)(2,1)S(1)}, u32[]{:S(2)}, u32[]{:S(2)}) async-start(bf16[32,2,7168]{2,1,0:T(2,128)(2,1)} %reshape.126), calls=%async_computation.2 | async-start | bytes 1835008 | tf_op jit(solution)/shard_map/all_to_all | solution.py:65
  95.8 6.4 %collective-permute-start = (bf16[4,7168]{1,0:T(4,128)(2,1)S(1)}, bf16[4,7168]{1,0:T(4,128)(2,1)S(1)}, u32[]{:S(2)}, u32[]{:S(2)}) collective-permute-start(bf16[4,7168]{1,0:T(4,128)(2,1)S(1)} %fusion.4), channel_id=1, source_target_pairs={{0,32},{32,64},{64,96},{96,128},{128,160},{160,192},{192,224},{224... | collective-permute-start | bytes 172040 | tf_op jit(solution)/shard_map/ppermute | solution.py:12
  97.1 13.6 %all-to-all-start.3 = ((bf16[32,1,2]{2,1,0:T(2,128)(2,1)}), bf16[32,1,2]{2,1,0:T(2,128)(2,1)S(1)}, u32[]{:S(2)}, u32[]{:S(2)}) async-start(bf16[32,1,2]{2,1,0:T(2,128)(2,1)} %copy.63), calls=%async_computation.3 | async-start | bytes 32768 | tf_op jit(solution)/shard_map/all_to_all | solution.py:55
  110.7 32.1 %all-to-all-start.4 = ((bf16[32,2,7168]{2,1,0:T(2,128)(2,1)}), bf16[32,2,7168]{2,1,0:T(2,128)(2,1)S(1)}, u32[]{:S(2)}, u32[]{:S(2)}) async-start(bf16[32,2,7168]{2,1,0:T(2,128)(2,1)} %gather_fusion.5), calls=%async_computation.4 | async-start | bytes 1835008 | tf_op jit(solution)/shard_map/all_to_all | solution.py:54
  152.6 31.4 %all-to-all-start.5 = ((bf16[32,2,7168]{2,1,0:T(2,128)(2,1)}), bf16[32,2,7168]{2,1,0:T(2,128)(2,1)S(1)}, u32[]{:S(2)}, u32[]{:S(2)}) async-start(bf16[32,2,7168]{2,1,0:T(2,128)(2,1)} %reshape.128), calls=%async_computation.5 | async-start | bytes 1835008 | tf_op jit(solution)/shard_map/all_to_all | solution.py:65
  184.3 4.8 %collective-permute-start.1 = (bf16[4,7168]{1,0:T(4,128)(2,1)S(1)}, bf16[4,7168]{1,0:T(4,128)(2,1)S(1)}, u32[]{:S(2)}, u32[]{:S(2)}) collective-permute-start(bf16[4,7168]{1,0:T(4,128)(2,1)S(1)} %fusion.5), channel_id=1, source_target_pairs={{0,32},{32,64},{64,96},{96,128},{128,160},{160,192},{192,224},{224... | collective-permute-start | bytes 172040 | tf_op jit(solution)/shard_map/ppermute | solution.py:12

commit v2 on v1

--- a/solution.py
+++ b/solution.py
@@ -1,9 +1,84 @@
+import functools
+
 import jax
 import jax.numpy as jnp
 from jax import lax
+from jax.experimental import pallas as pl
+from jax.experimental.pallas import tpu as pltpu
 from jax.sharding import PartitionSpec as P
 
 GROUP = 4
+LANES = 128
+
+
+def exchange_kernel(count, x_ref, y_ref, send_sem, recv_sem, own_sem):
+    me = lax.axis_index("expert")
+    seg = lax.axis_index("segment")
+
+    barrier = pltpu.get_barrier_semaphore()
+
+    def greet(d, carry):
+        peer = lax.rem(me + d, count)
+        pl.semaphore_signal(
+            barrier, inc=1, device_id=(seg, peer), device_id_type=pl.DeviceIdType.MESH
+        )
+        return carry
+
+    lax.fori_loop(1, count, greet, 0)
+    pl.semaphore_wait(barrier, count - 1)
+
+    own = pltpu.make_async_copy(x_ref.at[me], y_ref.at[me], own_sem)
+    own.start()
+
+    def outgoing(peer):
+        return pltpu.make_async_remote_copy(
+            src_ref=x_ref.at[peer],
+            dst_ref=y_ref.at[me],
+            send_sem=send_sem.at[peer],
+            recv_sem=recv_sem.at[me],
+            device_id=(seg, peer),
+            device_id_type=pl.DeviceIdType.MESH,
+        )
+
+    def incoming(peer):
+        return pltpu.make_async_remote_copy(
+            src_ref=x_ref.at[me],
+            dst_ref=y_ref.at[peer],
+            send_sem=send_sem.at[peer],
+            recv_sem=recv_sem.at[peer],
+            device_id=(seg, peer),
+            device_id_type=pl.DeviceIdType.MESH,
+        )
+
+    def send(d, carry):
+        outgoing(lax.rem(me + d, count)).start()
+        return carry
+
+    lax.fori_loop(1, count, send, 0)
+
+    def finish(d, carry):
+        outgoing(lax.rem(me + d, count)).wait_send()
+        incoming(lax.rem(me + count - d, count)).wait_recv()
+        return carry
+
+    lax.fori_loop(1, count, finish, 0)
+    own.wait()
+
+
+def exchange(x, collective_id):
+    count = x.shape[0]
+    return pl.pallas_call(
+        functools.partial(exchange_kernel, count),
+        out_shape=jax.ShapeDtypeStruct(x.shape, x.dtype),
+        in_specs=[pl.BlockSpec(memory_space=pl.ANY)],
+        out_specs=pl.BlockSpec(memory_space=pl.ANY),
+        scratch_shapes=[
+            pltpu.SemaphoreType.DMA((count,)),
+            pltpu.SemaphoreType.DMA((count,)),
+            pltpu.SemaphoreType.DMA,
+        ],
+        compiler_params=pltpu.CompilerParams(collective_id=collective_id, has_side_effects=True),
+    )(x)
 
 
 def shifted(value, axis, steps):
@@ -49,12 +124,15 @@
         packed_weight = jnp.sum(
             jnp.where(placer, dense_weight.T[:, None, :], jnp.float32(0.0)), axis=2
         ).astype(jnp.bfloat16)
-        send_rows = packed[owner_expert]
-        send_weight = packed_weight[owner_expert]
-        got_rows = lax.all_to_all(send_rows, "expert", 0, 0, tiled=True)
-        got_weight = lax.all_to_all(send_weight, "expert", 0, 0, tiled=True)
-
-        flat_rows = got_rows.reshape(owners * capacity, -1)
+        weight_block = jnp.broadcast_to(packed_weight[:, :, None], packed_weight.shape + (LANES,))
+        with_weight = jnp.concatenate([packed, weight_block], axis=2)
+        send_rows = jnp.broadcast_to(
+            with_weight[:, None], (experts, GROUP) + with_weight.shape[1:]
+        ).reshape((owners,) + with_weight.shape[1:])
+        got = exchange(send_rows, 0)
+        model_dim = normed.shape[1]
+        flat_rows = got[:, :, :model_dim].reshape(owners * capacity, model_dim)
+        got_weight = got[:, :, model_dim]
         gated = jnp.dot(flat_rows, gate_mat, preferred_element_type=jnp.float32)
         up_part = jnp.dot(flat_rows, up_mat, preferred_element_type=jnp.float32)
         inner_act = (jax.nn.silu(gated) * up_part).astype(jnp.bfloat16)
@@ -62,7 +140,7 @@
         scaled = got_weight.reshape(-1, 1).astype(jnp.float32) * partial_out
         terms = scaled.astype(jnp.bfloat16).reshape(owners, capacity, -1)
 
-        back = lax.all_to_all(terms, "expert", 0, 0, tiled=True)
+        back = exchange(terms, 1)
         back_placer = placer_f[owner_expert]
         summed = jnp.einsum(
             "ocr,ocd->rd", back_placer, back, preferred_element_type=jnp.float32

time: 190 us -> 161 us (0.85)
  Pallas kernels: 0 us -> 112 us
  waiting for transfers between devices: 114 us -> 8.49 us
  starting transfers between devices: 38.8 us -> 0.02 us
  matrix products: 18.4 us -> 20.7 us
  local copies, waits for them, and re-layouts: 15.9 us -> 13.7 us
    pallas_call x0 -> x4, Pallas kernels: none -> 112 us  [exchange(): pl.pallas_call(functools.partial(exchange_kernel, count), out_shape=jax.S...]
    all_to_all x6 -> x0, waiting for transfers between devices: 109 us -> none  [the longest x2 51.8 us: on_device(): got_rows = lax.all_to_all(send_rows, 'expert', 0, 0, tiled=True)]
    all_to_all x6 -> x0, starting transfers between devices: 38.8 us -> none  [the longest x2 16.4 us: on_device(): got_weight = lax.all_to_all(send_weight, 'expert', 0, 0, tiled=True)]
    gather x4 -> x0, local copies, waits for them, and re-layouts: 7.71 us -> none  [the longest x2 6.52 us: on_device(): send_rows = packed[owner_expert]]
    ppermute x2, waiting for transfers between devices: 4.8 us -> 8.49 us  [shifted(): return lax.ppermute(value, axis, pairs)]
    slice x0 -> x2, local copies, waits for them, and re-layouts: none -> 3.62 us  [on_device(): flat_rows = got[:, :, :model_dim].reshape(owners * capacity, model_dim)]
    broadcast_in_dim x0 -> x4, local copies, waits for them, and re-layouts: none -> 2.98 us  [the longest x2 2.84 us: on_device(): jnp.broadcast_to(with_weight[:, None], (experts, GROUP) + with_weight.sha...]
    dot_general x2, matrix products: 0.59 us -> 2.95 us  [on_device(): jnp.einsum('ocr,ocd->rd', back_placer, back, preferred_element_type=jnp.f...]
  transfers between devices with their start and end apart: 8 -> 2, of which waited for: 7 -> 2; matrix products, arithmetic and copies ran while one was open for 7% -> 1% of each run, Pallas kernels for 0% -> 0%
where the time goes in v2:
time: 161 us; the launch traced here: 160 us
  Pallas kernels  112 us (70%)
  matrix products  20.7 us (13%)
  local copies, waits for them, and re-layouts  13.7 us (9%)
  waiting for transfers between devices  8.49 us (5%)
  other arithmetic  4.03 us (3%)
    pallas_call x4, Pallas kernels, exchange(): pl.pallas_call(functools.partial(exchange_kernel, count), out_shape=jax.S...  112 us
    dot_general x2, matrix products, on_device(): jnp.dot(inner_act, down_mat, preferred_element_type=jnp.float32)  10.9 us
    ppermute x2, waiting for transfers between devices, shifted(): return lax.ppermute(value, axis, pairs)  8.49 us
    dot_general x2, matrix products, on_device(): gated = jnp.dot(flat_rows, gate_mat, preferred_element_type=jnp.float32)  5.5 us
    slice x2, local copies, waits for them, and re-layouts, on_device(): flat_rows = got[:, :, :model_dim].reshape(owners * capacity, model_dim)  3.62 us
  transfers between devices with their start and end apart: 2, of which 2 were waited for; matrix products, arithmetic and copies ran while one was open for 1% of the time, Pallas kernels for 0%

profile of v2, /device:TPU:32, one launch (start us, length us, event | category | flops | bytes accessed | tf_op | source)
XLA Modules:
  0.0 159.5 jit_solution(2782057015196230185)
XLA Ops:
  0.0 0.7 bitcast_convert_fusion.1
  0.7 0.7 slice_bitcast_fusion.1
  2.1 1.0 fusion.37
  3.1 1.1 convolution_convert_fusion.1
  4.4 1.4 broadcast_in_dim.82
  5.9 31.4 %shard_map.73 = bf16[32,2,7296]{2,1,0:T(2,128)(2,1)} custom-call(bf16[32,2,7296]{2,1,0:T(2,128)(2,1)} %bitcast.81), custom_call_target="tpu_custom_call" | custom-call | tf_op jit(solution)/shard_map/pallas_call | solution.py:70
  37.3 0.8 convert_reduce_fusion.1
  38.1 1.8 %slice.27 = bf16[32,2,7168]{2,1,0:T(2,128)(2,1)S(1)} slice(bf16[32,2,7296]{2,1,0:T(2,128)(2,1)} %shard_map.73), slice={[0:32], [0:2], [0:7168]} | slice | bytes 1835008 | tf_op jit(solution)/shard_map/slice | solution.py:134
  40.4 2.8 %fusion.14 = f32[64,256]{1,0:T(8,128)S(1)} fusion(bf16[64,7168]{1,0:T(8,128)(2,1)S(1)} %reshape.132, bf16[1,7168,256]{2,1,0:T(8,128)(2,1)} %param.11), kind=kOutput, calls=%fused_computation.22 | convolution fusion | flops 234881024 | bytes 4653056 | tf_op jit(solution)/shard_map/dot_general | solution.py:136
  43.1 5.5 %fusion = bf16[64,7168]{1,0:T(8,128)(2,1)S(1)} fusion(bf16[1,256,7168]{2,1,0:T(8,128)(2,1)} %param.13, f32[64]{0:T(128)S(1)} %reshape.139, bf16[64,7168]{1,0:T(8,128)(2,1)S(1)} %reshape.132, bf16[1,7168,256]{2,1,0:T(8,128)(2,1)} %param.12, f32[64,256]{1,0:T(8,128)S(1)} %fusion.14), kind=kOutput, calls=%fused_computation.4 | convolution fusion | flops 470777856 | bytes 9240832 | tf_op jit(solution)/shard_map/dot_general | solution.py:139
  48.6 1.3 reshape.133.x_ref
  49.9 26.9 %shard_map.74 = bf16[32,2,7168]{2,1,0:T(2,128)(2,1)} custom-call(bf16[32,2,7168]{2,1,0:T(2,128)(2,1)} %reshape.133.x_ref), custom_call_target="tpu_custom_call" | custom-call | tf_op jit(solution)/shard_map/pallas_call | solution.py:70
  77.5 1.5 fusion.4
  80.1 3.7 %collective-permute-done = bf16[4,7168]{1,0:T(4,128)(2,1)S(1)} collective-permute-done((bf16[4,7168]{1,0:T(4,128)(2,1)S(1)}, bf16[4,7168]{1,0:T(4,128)(2,1)S(1)}, u32[]{:S(2)}, u32[]{:S(2)}) %collective-permute-start) | collective-permute-done | bytes 57376 | tf_op jit(solution)/shard_map/ppermute | solution.py:87
  84.5 1.4 broadcast_in_dim.86
  85.9 27.1 %shard_map.75 = bf16[32,2,7296]{2,1,0:T(2,128)(2,1)} custom-call(bf16[32,2,7296]{2,1,0:T(2,128)(2,1)} %bitcast.82), custom_call_target="tpu_custom_call" | custom-call | tf_op jit(solution)/shard_map/pallas_call | solution.py:70
  113.0 0.8 convert_reduce_fusion
  113.8 1.8 %slice.31 = bf16[32,2,7168]{2,1,0:T(2,128)(2,1)S(1)} slice(bf16[32,2,7296]{2,1,0:T(2,128)(2,1)} %shard_map.75), slice={[0:32], [0:2], [0:7168]} | slice | bytes 1835008 | tf_op jit(solution)/shard_map/slice | solution.py:134
  116.1 2.8 %fusion.12 = f32[64,256]{1,0:T(8,128)S(1)} fusion(bf16[64,7168]{1,0:T(8,128)(2,1)S(1)} %reshape.135, bf16[1,7168,256]{2,1,0:T(8,128)(2,1)} %param.11), kind=kOutput, calls=%fused_computation.20 | convolution fusion | flops 234881024 | bytes 4653056 | tf_op jit(solution)/shard_map/dot_general | solution.py:136
  118.9 5.5 %fusion.1 = bf16[64,7168]{1,0:T(8,128)(2,1)S(1)} fusion(bf16[1,256,7168]{2,1,0:T(8,128)(2,1)} %param.13, f32[64]{0:T(128)S(1)} %reshape.141, bf16[64,7168]{1,0:T(8,128)(2,1)S(1)} %reshape.135, bf16[1,7168,256]{2,1,0:T(8,128)(2,1)} %param.12, f32[64,256]{1,0:T(8,128)S(1)} %fusion.12), kind=kOutput, calls=%fused_computation.5 | convolution fusion | flops 470777856 | bytes 9240832 | tf_op jit(solution)/shard_map/dot_general | solution.py:139
  124.3 1.3 reshape.136.x_ref
  125.6 27.0 %shard_map.76 = bf16[32,2,7168]{2,1,0:T(2,128)(2,1)} custom-call(bf16[32,2,7168]{2,1,0:T(2,128)(2,1)} %reshape.136.x_ref), custom_call_target="tpu_custom_call" | custom-call | tf_op jit(solution)/shard_map/pallas_call | solution.py:70
  152.6 1.5 fusion.5
  154.1 4.8 %collective-permute-done.1 = bf16[4,7168]{1,0:T(4,128)(2,1)S(1)} collective-permute-done((bf16[4,7168]{1,0:T(4,128)(2,1)S(1)}, bf16[4,7168]{1,0:T(4,128)(2,1)S(1)}, u32[]{:S(2)}, u32[]{:S(2)}) %collective-permute-start.1) | collective-permute-done | bytes 57376 | tf_op jit(solution)/shard_map/ppermute | solution.py:87
  (43 shorter events, 5.0 us)
Async XLA Ops:
  48.6 28.9 %copy-start = (bf16[1,4,7168]{2,1,0:T(4,128)(2,1)S(1)}, bf16[1,4,7168]{2,1,0:T(4,128)(2,1)}, u32[]{:S(2)}) copy-start(bf16[1,4,7168]{2,1,0:T(4,128)(2,1)} %param.7) | copy-start | bytes 172036
  48.6 35.3 %copy-start.1 = (f32[1,7168]{1,0:T(1,128)S(1)}, f32[1,7168]{1,0:T(1,128)}, u32[]{:S(2)}) copy-start(f32[1,7168]{1,0:T(1,128)} %param.10) | copy-start | bytes 86020
  79.0 4.8 %collective-permute-start = (bf16[4,7168]{1,0:T(4,128)(2,1)S(1)}, bf16[4,7168]{1,0:T(4,128)(2,1)S(1)}, u32[]{:S(2)}, u32[]{:S(2)}) collective-permute-start(bf16[4,7168]{1,0:T(4,128)(2,1)S(1)} %fusion.4), channel_id=1, source_target_pairs={{0,32},{32,64},{64,96},{96,128},{128,160},{160,192},{192,224},{224... | collective-permute-start | bytes 172040 | tf_op jit(solution)/shard_map/ppermute | solution.py:87
  154.1 4.8 %collective-permute-start.1 = (bf16[4,7168]{1,0:T(4,128)(2,1)S(1)}, bf16[4,7168]{1,0:T(4,128)(2,1)S(1)}, u32[]{:S(2)}, u32[]{:S(2)}) collective-permute-start(bf16[4,7168]{1,0:T(4,128)(2,1)S(1)} %fusion.5), channel_id=1, source_target_pairs={{0,32},{32,64},{64,96},{96,128},{128,160},{160,192},{192,224},{224... | collective-permute-start | bytes 172040 | tf_op jit(solution)/shard_map/ppermute | solution.py:87

commit v3 on v2

--- a/solution.py
+++ b/solution.py
@@ -8,10 +8,9 @@
 from jax.sharding import PartitionSpec as P
 
 GROUP = 4
-LANES = 128
 
 
-def exchange_kernel(count, x_ref, y_ref, send_sem, recv_sem, own_sem):
+def exchange_kernel(count, spread, x_ref, y_ref, send_sem, recv_sem, own_sem):
     me = lax.axis_index("expert")
     seg = lax.axis_index("segment")
 
@@ -27,12 +26,12 @@
     lax.fori_loop(1, count, greet, 0)
     pl.semaphore_wait(barrier, count - 1)
 
-    own = pltpu.make_async_copy(x_ref.at[me], y_ref.at[me], own_sem)
+    own = pltpu.make_async_copy(x_ref.at[me // spread], y_ref.at[me], own_sem)
     own.start()
 
     def outgoing(peer):
         return pltpu.make_async_remote_copy(
-            src_ref=x_ref.at[peer],
+            src_ref=x_ref.at[peer // spread],
             dst_ref=y_ref.at[me],
             send_sem=send_sem.at[peer],
             recv_sem=recv_sem.at[me],
@@ -42,7 +41,7 @@
 
     def incoming(peer):
         return pltpu.make_async_remote_copy(
-            src_ref=x_ref.at[me],
+            src_ref=x_ref.at[me // spread],
             dst_ref=y_ref.at[peer],
             send_sem=send_sem.at[peer],
             recv_sem=recv_sem.at[peer],
@@ -65,11 +64,11 @@
     own.wait()
 
 
-def exchange(x, collective_id):
-    count = x.shape[0]
+def exchange(x, count, collective_id):
+    spread = count // x.shape[0]
     return pl.pallas_call(
-        functools.partial(exchange_kernel, count),
-        out_shape=jax.ShapeDtypeStruct(x.shape, x.dtype),
+        functools.partial(exchange_kernel, count, spread),
+        out_shape=jax.ShapeDtypeStruct((count,) + x.shape[1:], x.dtype),
         in_specs=[pl.BlockSpec(memory_space=pl.ANY)],
         out_specs=pl.BlockSpec(memory_space=pl.ANY),
         scratch_shapes=[
@@ -123,27 +122,20 @@
         ).astype(jnp.bfloat16)
         packed_weight = jnp.sum(
             jnp.where(placer, dense_weight.T[:, None, :], jnp.float32(0.0)), axis=2
-        ).astype(jnp.bfloat16)
-        weight_block = jnp.broadcast_to(packed_weight[:, :, None], packed_weight.shape + (LANES,))
-        with_weight = jnp.concatenate([packed, weight_block], axis=2)
-        send_rows = jnp.broadcast_to(
-            with_weight[:, None], (experts, GROUP) + with_weight.shape[1:]
-        ).reshape((owners,) + with_weight.shape[1:])
-        got = exchange(send_rows, 0)
-        model_dim = normed.shape[1]
-        flat_rows = got[:, :, :model_dim].reshape(owners * capacity, model_dim)
-        got_weight = got[:, :, model_dim]
+        )
+        got = exchange(packed, owners, 0)
+        flat_rows = got.reshape(owners * capacity, -1)
         gated = jnp.dot(flat_rows, gate_mat, preferred_element_type=jnp.float32)
         up_part = jnp.dot(flat_rows, up_mat, preferred_element_type=jnp.float32)
         inner_act = (jax.nn.silu(gated) * up_part).astype(jnp.bfloat16)
         partial_out = jnp.dot(inner_act, down_mat, preferred_element_type=jnp.float32)
-        scaled = got_weight.reshape(-1, 1).astype(jnp.float32) * partial_out
-        terms = scaled.astype(jnp.bfloat16).reshape(owners, capacity, -1)
+        terms = partial_out.astype(jnp.bfloat16).reshape(owners, capacity, -1)
 
-        back = exchange(terms, 1)
-        back_placer = placer_f[owner_expert]
+        back = exchange(terms, owners, 1)
+        slot_weight = jnp.where(placer, packed_weight[:, :, None], jnp.float32(0.0))
+        back_weight = slot_weight[owner_expert].astype(jnp.bfloat16)
         summed = jnp.einsum(
-            "ocr,ocd->rd", back_placer, back, preferred_element_type=jnp.float32
+            "ocr,ocd->rd", back_weight, back, preferred_element_type=jnp.float32
         )
         updated = (current_f + summed).astype(jnp.bfloat16)
         current = shifted(updated, "segment", 1)

time: 161 us -> 157 us (0.975)
  other arithmetic: 4.03 us -> 2.34 us
    reshape x4, local copies, waits for them, and re-layouts: 3.24 us -> 7.5 us  [the longest x2 4.96 us: on_device(): flat_rows = got.reshape(owners * capacity, -1)]
    slice x2 -> x0, local copies, waits for them, and re-layouts: 3.62 us -> none  [on_device(): flat_rows = got[:, :, :model_dim].reshape(owners * capacity, model_dim)]
    broadcast_in_dim x4 -> x0, local copies, waits for them, and re-layouts: 2.98 us -> none  [the longest x2 2.84 us: on_device(): jnp.broadcast_to(with_weight[:, None], (experts, GROUP) + with_weight.sha...]
    dot_general x0 -> x2, local copies, waits for them, and re-layouts: none -> 1.86 us  [on_device(): jnp.einsum('jcr,rd->jcd', placer_f, normed, preferred_element_type=jnp.fl...]
    convert_element_type x2 -> x0, other arithmetic: 1.65 us -> none  [on_device(): scaled = got_weight.reshape(-1, 1).astype(jnp.float32) * partial_out]
where the time goes in v3:
time: 157 us; the launch traced here: 156 us
  Pallas kernels  112 us (71%)
  matrix products  20.7 us (13%)
  local copies, waits for them, and re-layouts  12.6 us (8%)
  waiting for transfers between devices  8.48 us (5%)
  other arithmetic  2.34 us (1%)
    pallas_call x4, Pallas kernels, exchange(): pl.pallas_call(functools.partial(exchange_kernel, count, spread), out_sha...  112 us
    dot_general x2, matrix products, on_device(): jnp.dot(inner_act, down_mat, preferred_element_type=jnp.float32)  10.9 us
    ppermute x2, waiting for transfers between devices, shifted(): return lax.ppermute(value, axis, pairs)  8.48 us
    dot_general x2, matrix products, on_device(): gated = jnp.dot(flat_rows, gate_mat, preferred_element_type=jnp.float32)  5.5 us
    reshape x2, local copies, waits for them, and re-layouts, on_device(): flat_rows = got.reshape(owners * capacity, -1)  4.96 us
  transfers between devices with their start and end apart: 2, of which 2 were waited for; matrix products, arithmetic and copies ran while one was open for 1% of the time, Pallas kernels for 0%

profile of v3, /device:TPU:32, one launch (start us, length us, event | category | flops | bytes accessed | tf_op | source)
XLA Modules:
  0.0 156.0 jit_solution(15612682731336302382)
XLA Ops:
  0.0 1.0 fusion.39
  1.0 0.7 slice_bitcast_fusion
  2.0 0.7 bitcast_convert_fusion
  3.0 0.6 gather_fusion
  3.7 1.1 fusion.53
  4.8 0.9 copy.67.x_ref
  5.7 31.1 %shard_map.73 = bf16[32,2,7168]{2,1,0:T(2,128)(2,1)} custom-call(bf16[8,2,7168]{2,1,0:T(2,128)(2,1)} %copy.67.x_ref), custom_call_target="tpu_custom_call" | custom-call | tf_op jit(solution)/shard_map/pallas_call | solution.py:69
  36.8 2.5 %reshape.101 = bf16[64,7168]{1,0:T(8,128)(2,1)S(1)} reshape(bf16[32,2,7168]{2,1,0:T(2,128)(2,1)} %shard_map.73) | data formatting | bytes 1835008 | tf_op jit(solution)/shard_map/reshape | solution.py:127
  39.3 2.8 %fusion.14 = f32[64,256]{1,0:T(8,128)S(1)} fusion(bf16[64,7168]{1,0:T(8,128)(2,1)S(1)} %reshape.101, bf16[1,7168,256]{2,1,0:T(8,128)(2,1)} %param.11), kind=kOutput, calls=%fused_computation.20 | convolution fusion | flops 234881024 | bytes 4653056 | tf_op jit(solution)/shard_map/dot_general | solution.py:128
  42.1 5.5 %convolution_convert_fusion.1 = bf16[64,7168]{1,0:T(8,128)(2,1)S(1)} fusion(bf16[1,256,7168]{2,1,0:T(8,128)(2,1)} %param.13, bf16[64,7168]{1,0:T(8,128)(2,1)S(1)} %reshape.101, bf16[1,7168,256]{2,1,0:T(8,128)(2,1)} %param.12, f32[64,256]{1,0:T(8,128)S(1)} %fusion.14), kind=kOutput, calls=%fused_computation.5 | convolution fusion | flops 470319104 | bytes 9240576 | tf_op jit(solution)/shard_map/dot_general | solution.py:131
  47.5 1.3 reshape.102.x_ref
  48.8 26.9 %shard_map.74 = bf16[32,2,7168]{2,1,0:T(2,128)(2,1)} custom-call(bf16[32,2,7168]{2,1,0:T(2,128)(2,1)} %reshape.102.x_ref), custom_call_target="tpu_custom_call" | custom-call | tf_op jit(solution)/shard_map/pallas_call | solution.py:69
  75.8 1.5 fusion.4
  78.4 3.7 %collective-permute-done = bf16[4,7168]{1,0:T(4,128)(2,1)S(1)} collective-permute-done((bf16[4,7168]{1,0:T(4,128)(2,1)S(1)}, bf16[4,7168]{1,0:T(4,128)(2,1)S(1)}, u32[]{:S(2)}, u32[]{:S(2)}) %collective-permute-start) | collective-permute-done | bytes 57376 | tf_op jit(solution)/shard_map/ppermute | solution.py:86
  82.5 0.9 copy.66.x_ref
  83.5 26.7 %shard_map.75 = bf16[32,2,7168]{2,1,0:T(2,128)(2,1)} custom-call(bf16[8,2,7168]{2,1,0:T(2,128)(2,1)} %copy.66.x_ref), custom_call_target="tpu_custom_call" | custom-call | tf_op jit(solution)/shard_map/pallas_call | solution.py:69
  110.2 2.5 %reshape.103 = bf16[64,7168]{1,0:T(8,128)(2,1)S(1)} reshape(bf16[32,2,7168]{2,1,0:T(2,128)(2,1)} %shard_map.75) | data formatting | bytes 1835008 | tf_op jit(solution)/shard_map/reshape | solution.py:127
  112.6 2.8 %fusion.12 = f32[64,256]{1,0:T(8,128)S(1)} fusion(bf16[64,7168]{1,0:T(8,128)(2,1)S(1)} %reshape.103, bf16[1,7168,256]{2,1,0:T(8,128)(2,1)} %param.11), kind=kOutput, calls=%fused_computation.18 | convolution fusion | flops 234881024 | bytes 4653056 | tf_op jit(solution)/shard_map/dot_general | solution.py:128
  115.4 5.5 %convolution_convert_fusion = bf16[64,7168]{1,0:T(8,128)(2,1)S(1)} fusion(bf16[1,256,7168]{2,1,0:T(8,128)(2,1)} %param.13, bf16[64,7168]{1,0:T(8,128)(2,1)S(1)} %reshape.103, bf16[1,7168,256]{2,1,0:T(8,128)(2,1)} %param.12, f32[64,256]{1,0:T(8,128)S(1)} %fusion.12), kind=kOutput, calls=%fused_computation.4 | convolution fusion | flops 470319104 | bytes 9240576 | tf_op jit(solution)/shard_map/dot_general | solution.py:131
  120.9 1.3 reshape.104.x_ref
  122.1 27.0 %shard_map.76 = bf16[32,2,7168]{2,1,0:T(2,128)(2,1)} custom-call(bf16[32,2,7168]{2,1,0:T(2,128)(2,1)} %reshape.104.x_ref), custom_call_target="tpu_custom_call" | custom-call | tf_op jit(solution)/shard_map/pallas_call | solution.py:69
  149.1 1.5 fusion.5
  150.6 4.8 %collective-permute-done.1 = bf16[4,7168]{1,0:T(4,128)(2,1)S(1)} collective-permute-done((bf16[4,7168]{1,0:T(4,128)(2,1)S(1)}, bf16[4,7168]{1,0:T(4,128)(2,1)S(1)}, u32[]{:S(2)}, u32[]{:S(2)}) %collective-permute-start.1) | collective-permute-done | bytes 57376 | tf_op jit(solution)/shard_map/ppermute | solution.py:86
  155.4 0.6 copy.69
  (33 shorter events, 2.3 us)
Async XLA Ops:
  47.5 28.3 %copy-start = (bf16[1,4,7168]{2,1,0:T(4,128)(2,1)S(1)}, bf16[1,4,7168]{2,1,0:T(4,128)(2,1)}, u32[]{:S(2)}) copy-start(bf16[1,4,7168]{2,1,0:T(4,128)(2,1)} %param.7) | copy-start | bytes 172036
  47.5 34.7 %copy-start.1 = (f32[1,7168]{1,0:T(1,128)S(1)}, f32[1,7168]{1,0:T(1,128)}, u32[]{:S(2)}) copy-start(f32[1,7168]{1,0:T(1,128)} %param.10) | copy-start | bytes 86020
  77.3 4.8 %collective-permute-start = (bf16[4,7168]{1,0:T(4,128)(2,1)S(1)}, bf16[4,7168]{1,0:T(4,128)(2,1)S(1)}, u32[]{:S(2)}, u32[]{:S(2)}) collective-permute-start(bf16[4,7168]{1,0:T(4,128)(2,1)S(1)} %fusion.4), channel_id=1, source_target_pairs={{0,32},{32,64},{64,96},{96,128},{128,160},{160,192},{192,224},{224... | collective-permute-start | bytes 172040 | tf_op jit(solution)/shard_map/ppermute | solution.py:86
  150.6 4.8 %collective-permute-start.1 = (bf16[4,7168]{1,0:T(4,128)(2,1)S(1)}, bf16[4,7168]{1,0:T(4,128)(2,1)S(1)}, u32[]{:S(2)}, u32[]{:S(2)}) collective-permute-start(bf16[4,7168]{1,0:T(4,128)(2,1)S(1)} %fusion.5), channel_id=1, source_target_pairs={{0,32},{32,64},{64,96},{96,128},{128,160},{160,192},{192,224},{224... | collective-permute-start | bytes 172040 | tf_op jit(solution)/shard_map/ppermute | solution.py:86

commit v4 on v3

--- a/solution.py
+++ b/solution.py
@@ -10,24 +10,33 @@
 GROUP = 4
 
 
-def exchange_kernel(count, spread, x_ref, y_ref, send_sem, recv_sem, own_sem):
+def exchange_kernel(count, spread, shift, x_ref, y_ref, send_sem, recv_sem, own_sem):
     me = lax.axis_index("expert")
     seg = lax.axis_index("segment")
+    sections = lax.axis_size("segment")
+    ahead = lax.rem(seg + shift, sections)
+    behind = lax.rem(seg + sections - shift, sections)
+    first = 1 if shift == 0 else 0
 
     barrier = pltpu.get_barrier_semaphore()
 
     def greet(d, carry):
         peer = lax.rem(me + d, count)
         pl.semaphore_signal(
-            barrier, inc=1, device_id=(seg, peer), device_id_type=pl.DeviceIdType.MESH
+            barrier, inc=1, device_id=(ahead, peer), device_id_type=pl.DeviceIdType.MESH
         )
+        if shift != 0:
+            pl.semaphore_signal(
+                barrier, inc=1, device_id=(behind, peer), device_id_type=pl.DeviceIdType.MESH
+            )
         return carry
 
-    lax.fori_loop(1, count, greet, 0)
-    pl.semaphore_wait(barrier, count - 1)
+    lax.fori_loop(first, count, greet, 0)
+    pl.semaphore_wait(barrier, (count - first) * (1 if shift == 0 else 2))
 
-    own = pltpu.make_async_copy(x_ref.at[me // spread], y_ref.at[me], own_sem)
-    own.start()
+    if shift == 0:
+        own = pltpu.make_async_copy(x_ref.at[me // spread], y_ref.at[me], own_sem)
+        own.start()
 
     def outgoing(peer):
         return pltpu.make_async_remote_copy(
@@ -35,7 +44,7 @@
             dst_ref=y_ref.at[me],
             send_sem=send_sem.at[peer],
             recv_sem=recv_sem.at[me],
-            device_id=(seg, peer),
+            device_id=(ahead, peer),
             device_id_type=pl.DeviceIdType.MESH,
         )
 
@@ -45,7 +54,7 @@
             dst_ref=y_ref.at[peer],
             send_sem=send_sem.at[peer],
             recv_sem=recv_sem.at[peer],
-            device_id=(seg, peer),
+            device_id=(behind, peer),
             device_id_type=pl.DeviceIdType.MESH,
         )
 
@@ -53,21 +62,22 @@
         outgoing(lax.rem(me + d, count)).start()
         return carry
 
-    lax.fori_loop(1, count, send, 0)
+    lax.fori_loop(first, count, send, 0)
 
     def finish(d, carry):
         outgoing(lax.rem(me + d, count)).wait_send()
         incoming(lax.rem(me + count - d, count)).wait_recv()
         return carry
 
-    lax.fori_loop(1, count, finish, 0)
-    own.wait()
+    lax.fori_loop(first, count, finish, 0)
+    if shift == 0:
+        own.wait()
 
 
-def exchange(x, count, collective_id):
+def exchange(x, count, shift, collective_id):
     spread = count // x.shape[0]
     return pl.pallas_call(
-        functools.partial(exchange_kernel, count, spread),
+        functools.partial(exchange_kernel, count, spread, shift),
         out_shape=jax.ShapeDtypeStruct((count,) + x.shape[1:], x.dtype),
         in_specs=[pl.BlockSpec(memory_space=pl.ANY)],
         out_specs=pl.BlockSpec(memory_space=pl.ANY),
@@ -123,7 +133,7 @@
         packed_weight = jnp.sum(
             jnp.where(placer, dense_weight.T[:, None, :], jnp.float32(0.0)), axis=2
         )
-        got = exchange(packed, owners, 0)
+        got = exchange(packed, owners, 0, 0)
         flat_rows = got.reshape(owners * capacity, -1)
         gated = jnp.dot(flat_rows, gate_mat, preferred_element_type=jnp.float32)
         up_part = jnp.dot(flat_rows, up_mat, preferred_element_type=jnp.float32)
@@ -131,14 +141,14 @@
         partial_out = jnp.dot(inner_act, down_mat, preferred_element_type=jnp.float32)
         terms = partial_out.astype(jnp.bfloat16).reshape(owners, capacity, -1)
 
-        back = exchange(terms, owners, 1)
+        back = exchange(terms, owners, 1, 1 + step_no)
         slot_weight = jnp.where(placer, packed_weight[:, :, None], jnp.float32(0.0))
-        back_weight = slot_weight[owner_expert].astype(jnp.bfloat16)
+        back_weight = shifted(slot_weight[owner_expert].astype(jnp.bfloat16), "segment", 1)
+        moved = shifted(current, "segment", 1)
         summed = jnp.einsum(
             "ocr,ocd->rd", back_weight, back, preferred_element_type=jnp.float32
         )
-        updated = (current_f + summed).astype(jnp.bfloat16)
-        current = shifted(updated, "segment", 1)
+        current = (moved.astype(jnp.float32) + summed).astype(jnp.bfloat16)
     return current[None]
 
 

time: 157 us -> 161 us (1.025)
  Pallas kernels: 112 us -> 123 us
  waiting for transfers between devices: 8.48 us -> 0.01 us
    pallas_call x4, Pallas kernels: 112 us -> 123 us  [exchange(): pl.pallas_call(functools.partial(exchange_kernel, count, spread, shift),...]
    ppermute x2 -> x4, waiting for transfers between devices: 8.48 us -> 0.01 us  [shifted(): return lax.ppermute(value, axis, pairs)]
  transfers between devices with their start and end apart: 2 -> 4, of which waited for: 2 -> 0; matrix products, arithmetic and copies ran while one was open for 1% -> 19% of each run, Pallas kernels for 0% -> 77%
where the time goes in v4:
time: 161 us; the launch traced here: 160 us
  Pallas kernels  123 us (76%)
  matrix products  21.5 us (13%)
  local copies, waits for them, and re-layouts  12 us (7%)
  other arithmetic  2.16 us (1%)
  starting transfers between devices  1.63 us (1%)
    pallas_call x4, Pallas kernels, exchange(): pl.pallas_call(functools.partial(exchange_kernel, count, spread, shift),...  123 us
    dot_general x2, matrix products, on_device(): jnp.dot(inner_act, down_mat, preferred_element_type=jnp.float32)  10.9 us
    dot_general x2, matrix products, on_device(): gated = jnp.dot(flat_rows, gate_mat, preferred_element_type=jnp.float32)  5.5 us
    reshape x2, local copies, waits for them, and re-layouts, on_device(): flat_rows = got.reshape(owners * capacity, -1)  4.96 us
    dot_general x2, matrix products, on_device(): jnp.einsum('ocr,ocd->rd', back_weight, back, preferred_element_type=jnp.f...  3.7 us
  transfers between devices with their start and end apart: 4, of which 0 were waited for; matrix products, arithmetic and copies ran while one was open for 19% of the time, Pallas kernels for 77%

profile of v4, /device:TPU:32, one launch (start us, length us, event | category | flops | bytes accessed | tf_op | source)
XLA Modules:
  0.0 160.2 jit_solution(12209789278694608634)
XLA Ops:
  0.0 0.7 slice_bitcast_fusion.1
  1.0 0.7 bitcast_convert_fusion.1
  2.0 0.6 gather_fusion
  3.1 0.6 gather_fusion.1
  3.8 1.6 %collective-permute-start.3 = (bf16[32,2,4]{0,2,1:T(4,128)(2,1)S(1)}, bf16[32,2,4]{0,2,1:T(4,128)(2,1)S(1)}, u32[]{:S(2)}, u32[]{:S(2)}) collective-permute-start(bf16[32,2,4]{0,2,1:T(4,128)(2,1)S(1)} %copy.38), channel_id=1, source_target_pairs={{0,32},{32,64},{64,96},{96,128},{128,160},{160,192},{192,224},{224... | collective-permute-start | bytes 1544 | tf_op jit(solution)/shard_map/ppermute | solution.py:96
  5.4 1.0 fusion.32
  6.4 1.1 fusion.53
  7.5 0.9 copy.53.x_ref
  8.5 31.9 %shard_map.73 = bf16[32,2,7168]{2,1,0:T(2,128)(2,1)} custom-call(bf16[8,2,7168]{2,1,0:T(2,128)(2,1)} %copy.53.x_ref), custom_call_target="tpu_custom_call" | custom-call | tf_op jit(solution)/shard_map/pallas_call | solution.py:79
  40.3 2.5 %reshape.99 = bf16[64,7168]{1,0:T(8,128)(2,1)S(1)} reshape(bf16[32,2,7168]{2,1,0:T(2,128)(2,1)} %shard_map.73) | data formatting | bytes 1835008 | tf_op jit(solution)/shard_map/reshape | solution.py:137
  42.8 2.8 %fusion.10 = f32[64,256]{1,0:T(8,128)S(1)} fusion(bf16[64,7168]{1,0:T(8,128)(2,1)S(1)} %reshape.99, bf16[1,7168,256]{2,1,0:T(8,128)(2,1)} %param.11), kind=kOutput, calls=%fused_computation.16 | convolution fusion | flops 234881024 | bytes 4653056 | tf_op jit(solution)/shard_map/dot_general | solution.py:138
  45.6 5.5 %convolution_convert_fusion.1 = bf16[64,7168]{1,0:T(8,128)(2,1)S(1)} fusion(bf16[1,256,7168]{2,1,0:T(8,128)(2,1)} %param.13, bf16[64,7168]{1,0:T(8,128)(2,1)S(1)} %reshape.99, bf16[1,7168,256]{2,1,0:T(8,128)(2,1)} %param.12, f32[64,256]{1,0:T(8,128)S(1)} %fusion.10), kind=kOutput, calls=%fused_computation.5 | convolution fusion | flops 470319104 | bytes 9240576 | tf_op jit(solution)/shard_map/dot_general | solution.py:141
  51.1 1.3 reshape.100.x_ref
  52.3 30.3 %shard_map.74 = bf16[32,2,7168]{2,1,0:T(2,128)(2,1)} custom-call(bf16[32,2,7168]{2,1,0:T(2,128)(2,1)} %reshape.100.x_ref), custom_call_target="tpu_custom_call" | custom-call | tf_op jit(solution)/shard_map/pallas_call | solution.py:79
  82.7 1.6 fusion.35
  84.3 0.3 fusion.50
  84.6 0.9 copy.52.x_ref
  85.5 29.0 %shard_map.75 = bf16[32,2,7168]{2,1,0:T(2,128)(2,1)} custom-call(bf16[8,2,7168]{2,1,0:T(2,128)(2,1)} %copy.52.x_ref), custom_call_target="tpu_custom_call" | custom-call | tf_op jit(solution)/shard_map/pallas_call | solution.py:79
  114.5 2.5 %reshape.101 = bf16[64,7168]{1,0:T(8,128)(2,1)S(1)} reshape(bf16[32,2,7168]{2,1,0:T(2,128)(2,1)} %shard_map.75) | data formatting | bytes 1835008 | tf_op jit(solution)/shard_map/reshape | solution.py:137
  117.0 2.8 %fusion.8 = f32[64,256]{1,0:T(8,128)S(1)} fusion(bf16[64,7168]{1,0:T(8,128)(2,1)S(1)} %reshape.101, bf16[1,7168,256]{2,1,0:T(8,128)(2,1)} %param.11), kind=kOutput, calls=%fused_computation.14 | convolution fusion | flops 234881024 | bytes 4653056 | tf_op jit(solution)/shard_map/dot_general | solution.py:138
  119.7 5.5 %convolution_convert_fusion = bf16[64,7168]{1,0:T(8,128)(2,1)S(1)} fusion(bf16[1,256,7168]{2,1,0:T(8,128)(2,1)} %param.13, bf16[64,7168]{1,0:T(8,128)(2,1)S(1)} %reshape.101, bf16[1,7168,256]{2,1,0:T(8,128)(2,1)} %param.12, f32[64,256]{1,0:T(8,128)S(1)} %fusion.8), kind=kOutput, calls=%fused_computation.4 | convolution fusion | flops 470319104 | bytes 9240576 | tf_op jit(solution)/shard_map/dot_general | solution.py:141
  125.2 1.3 reshape.102.x_ref
  126.5 31.6 %shard_map.76 = bf16[32,2,7168]{2,1,0:T(2,128)(2,1)} custom-call(bf16[32,2,7168]{2,1,0:T(2,128)(2,1)} %reshape.102.x_ref), custom_call_target="tpu_custom_call" | custom-call | tf_op jit(solution)/shard_map/pallas_call | solution.py:79
  158.1 2.1 %fusion.48 = bf16[1,4,7168]{2,1,0:T(4,128)(2,1)} fusion(bf16[4,7168]{1,0:T(4,128)(2,1)S(1)} %collective-permute-done.2, bf16[32,2,4]{0,2,1:T(4,128)(2,1)S(1)} %collective-permute-done.3, bf16[32,2,7168]{2,1,0:T(2,128)(2,1)} %shard_map.76), kind=kOutput, calls=%fused_computation.50 | convolution fusion | flops 3756032 | bytes 1032704 | tf_op jit(solution)/shard_map/ocr,ocd->rd/dot_general | solution.py:148
  (33 shorter events, 1.3 us)
Async XLA Ops:
  2.7 80.0 %collective-permute-start.1 = (bf16[32,2,4]{0,2,1:T(4,128)(2,1)S(1)}, bf16[32,2,4]{0,2,1:T(4,128)(2,1)S(1)}, u32[]{:S(2)}, u32[]{:S(2)}) collective-permute-start(bf16[32,2,4]{0,2,1:T(4,128)(2,1)S(1)} %copy.31), channel_id=1, source_target_pairs={{0,32},{32,64},{64,96},{96,128},{128,160},{160,192},{192,224},{224... | collective-permute-start | bytes 1544 | tf_op jit(solution)/shard_map/ppermute | solution.py:96
  3.8 154.3 %collective-permute-start.3 = (bf16[32,2,4]{0,2,1:T(4,128)(2,1)S(1)}, bf16[32,2,4]{0,2,1:T(4,128)(2,1)S(1)}, u32[]{:S(2)}, u32[]{:S(2)}) collective-permute-start(bf16[32,2,4]{0,2,1:T(4,128)(2,1)S(1)} %copy.38), channel_id=1, source_target_pairs={{0,32},{32,64},{64,96},{96,128},{128,160},{160,192},{192,224},{224... | collective-permute-start | bytes 1544 | tf_op jit(solution)/shard_map/ppermute | solution.py:96
  5.4 77.2 %collective-permute-start = (bf16[4,7168]{1,0:T(4,128)(2,1)}, bf16[4,7168]{1,0:T(4,128)(2,1)S(1)}, u32[]{:S(2)}, u32[]{:S(2)}) collective-permute-start(bf16[4,7168]{1,0:T(4,128)(2,1)} %bitcast.74), channel_id=1, source_target_pairs={{0,32},{32,64},{64,96},{96,128},{128,160},{160,192},{192,224},{224... | collective-permute-start | bytes 172040 | tf_op jit(solution)/shard_map/ppermute | solution.py:96
  51.1 33.2 %copy-start = (f32[1,7168]{1,0:T(1,128)S(1)}, f32[1,7168]{1,0:T(1,128)}, u32[]{:S(2)}) copy-start(f32[1,7168]{1,0:T(1,128)} %param.10) | copy-start | bytes 86020
  84.3 73.9 %collective-permute-start.2 = (bf16[4,7168]{1,0:T(4,128)(2,1)S(1)}, bf16[4,7168]{1,0:T(4,128)(2,1)S(1)}, u32[]{:S(2)}, u32[]{:S(2)}) collective-permute-start(bf16[4,7168]{1,0:T(4,128)(2,1)S(1)} %get-tuple-element.6), channel_id=1, source_target_pairs={{0,32},{32,64},{64,96},{96,128},{128,160},{160,192},{192,224},{224... | collective-permute-start | bytes 172040 | tf_op jit(solution)/shard_map/ppermute | solution.py:96

commit v5 on v3

--- a/solution.py
+++ b/solution.py
@@ -80,6 +80,57 @@
     )(x)
 
 
+def ffn_kernel(x_ref, g_ref, u_ref, d_ref, o_ref, acc_g, acc_u):
+    k = pl.program_id(0)
+
+    @pl.when(k == 0)
+    def _():
+        acc_g[...] = jnp.zeros_like(acc_g)
+        acc_u[...] = jnp.zeros_like(acc_u)
+
+    for c in range(x_ref.shape[1]):
+        xc = x_ref[:, c, :]
+        acc_g[c] += jnp.dot(xc, g_ref[...], preferred_element_type=jnp.float32)
+        acc_u[c] += jnp.dot(xc, u_ref[...], preferred_element_type=jnp.float32)
+
+    @pl.when(k == pl.num_programs(0) - 1)
+    def _():
+        for c in range(x_ref.shape[1]):
+            g = acc_g[c]
+            inner = (g / (1.0 + jnp.exp(-g)) * acc_u[c]).astype(jnp.bfloat16)
+            o_ref[:, c, :] = jnp.dot(
+                inner, d_ref[...], preferred_element_type=jnp.float32
+            ).astype(o_ref.dtype)
+
+
+def expert_ffn(x, gate_mat, up_mat, down_mat):
+    sources, slots, model_dim = x.shape
+    hidden = gate_mat.shape[1]
+    chunk = 1024
+    rows = sources * slots
+    return pl.pallas_call(
+        ffn_kernel,
+        grid=(model_dim // chunk,),
+        in_specs=[
+            pl.BlockSpec((sources, slots, chunk), lambda k: (0, 0, k)),
+            pl.BlockSpec((chunk, hidden), lambda k: (k, 0)),
+            pl.BlockSpec((chunk, hidden), lambda k: (k, 0)),
+            pl.BlockSpec((hidden, model_dim), lambda k: (0, 0)),
+        ],
+        out_specs=pl.BlockSpec((sources, slots, model_dim), lambda k: (0, 0, 0)),
+        out_shape=jax.ShapeDtypeStruct(x.shape, jnp.bfloat16),
+        scratch_shapes=[
+            pltpu.VMEM((slots, sources, hidden), jnp.float32),
+            pltpu.VMEM((slots, sources, hidden), jnp.float32),
+        ],
+        cost_estimate=pl.CostEstimate(
+            flops=6 * rows * model_dim * hidden,
+            transcendentals=rows * hidden,
+            bytes_accessed=3 * model_dim * hidden * 2 + 2 * rows * model_dim * 2,
+        ),
+    )(x, gate_mat, up_mat, down_mat)
+
+
 def shifted(value, axis, steps):
     count = lax.axis_size(axis)
     pairs = [(source, (source + steps) % count) for source in range(count)]
@@ -124,12 +175,7 @@
             jnp.where(placer, dense_weight.T[:, None, :], jnp.float32(0.0)), axis=2
         )
         got = exchange(packed, owners, 0)
-        flat_rows = got.reshape(owners * capacity, -1)
-        gated = jnp.dot(flat_rows, gate_mat, preferred_element_type=jnp.float32)
-        up_part = jnp.dot(flat_rows, up_mat, preferred_element_type=jnp.float32)
-        inner_act = (jax.nn.silu(gated) * up_part).astype(jnp.bfloat16)
-        partial_out = jnp.dot(inner_act, down_mat, preferred_element_type=jnp.float32)
-        terms = partial_out.astype(jnp.bfloat16).reshape(owners, capacity, -1)
+        terms = expert_ffn(got, gate_mat, up_mat, down_mat)
 
         back = exchange(terms, owners, 1)
         slot_weight = jnp.where(placer, packed_weight[:, :, None], jnp.float32(0.0))

time: 157 us -> 155 us (0.987)
  Pallas kernels: 112 us -> 134 us
  matrix products: 20.7 us -> 4.31 us
  local copies, waits for them, and re-layouts: 12.6 us -> 5.12 us
    pallas_call x0 -> x2, Pallas kernels: none -> 21.9 us  [expert_ffn(): pl.pallas_call(ffn_kernel, grid=(model_dim // chunk,), in_specs=[pl.Block...]
    dot_general x4 -> x0, matrix products: 16.4 us -> none  [the longest x2 10.9 us: on_device(): jnp.dot(inner_act, down_mat, preferred_element_type=jnp.float32)]
    reshape x4 -> x0, local copies, waits for them, and re-layouts: 7.5 us -> none  [the longest x2 4.96 us: on_device(): flat_rows = got.reshape(owners * capacity, -1)]
where the time goes in v5:
time: 155 us; the launch traced here: 154 us
  Pallas kernels  134 us (86%)
  waiting for transfers between devices  8.48 us (5%)
  local copies, waits for them, and re-layouts  5.12 us (3%)
  matrix products  4.31 us (3%)
  other arithmetic  2.34 us (2%)
    pallas_call x4, Pallas kernels, exchange(): pl.pallas_call(functools.partial(exchange_kernel, count, spread), out_sha...  112 us
    pallas_call x2, Pallas kernels, expert_ffn(): pl.pallas_call(ffn_kernel, grid=(model_dim // chunk,), in_specs=[pl.Block...  21.9 us
    ppermute x2, waiting for transfers between devices, shifted(): return lax.ppermute(value, axis, pairs)  8.48 us
  transfers between devices with their start and end apart: 2, of which 2 were waited for; matrix products, arithmetic and copies ran while one was open for 1% of the time, Pallas kernels for 0%

profile of v5, /device:TPU:32, one launch (start us, length us, event | category | flops | bytes accessed | tf_op | source)
XLA Modules:
  0.0 154.2 jit_solution(1162637517715251581)
XLA Ops:
  0.0 1.0 fusion.13
  1.0 0.7 slice_bitcast_fusion
  2.0 0.7 bitcast_convert_fusion
  3.0 0.6 gather_fusion
  3.6 0.1 copy.43
  3.7 1.1 fusion.17
  4.8 0.9 copy.65.x_ref
  5.7 31.1 %shard_map.73.x_ref = bf16[32,2,7168]{2,1,0:T(2,128)(2,1)} custom-call(bf16[8,2,7168]{2,1,0:T(2,128)(2,1)} %copy.65.x_ref), custom_call_target="tpu_custom_call" | custom-call | tf_op jit(solution)/shard_map/pallas_call | solution.py:69
  36.8 10.9 %shard_map.74.x_ref = bf16[32,2,7168]{2,1,0:T(2,128)(2,1)} custom-call(bf16[32,2,7168]{2,1,0:T(2,128)(2,1)} %shard_map.73.x_ref, bf16[7168,256]{1,0:T(8,128)(2,1)} %bitcast.53, bf16[7168,256]{1,0:T(8,128)(2,1)} %bitcast.55, bf16[256,7168]{1,0:T(8,128)(2,1)} %bitcast.57), custom_call_target="tpu_custom_call" | custom-call | flops 704643072 | bytes 12845056 | tf_op jit(solution)/shard_map/pallas_call | solution.py:111
  47.8 26.9 %shard_map.75 = bf16[32,2,7168]{2,1,0:T(2,128)(2,1)} custom-call(bf16[32,2,7168]{2,1,0:T(2,128)(2,1)} %shard_map.74.x_ref), custom_call_target="tpu_custom_call" | custom-call | tf_op jit(solution)/shard_map/pallas_call | solution.py:69
  74.7 1.5 fusion.4
  76.2 0.1 copy.47
  76.7 0.6 gather_fusion.1
  77.3 0.1 copy.50
  77.4 3.7 %collective-permute-done = bf16[4,7168]{1,0:T(4,128)(2,1)S(1)} collective-permute-done((bf16[4,7168]{1,0:T(4,128)(2,1)S(1)}, bf16[4,7168]{1,0:T(4,128)(2,1)S(1)}, u32[]{:S(2)}, u32[]{:S(2)}) %collective-permute-start) | collective-permute-done | bytes 57376 | tf_op jit(solution)/shard_map/ppermute | solution.py:137
  81.0 0.2 fusion.10
  81.2 0.3 fusion.20
  81.5 0.9 copy.64.x_ref
  82.4 26.8 %shard_map.76.x_ref = bf16[32,2,7168]{2,1,0:T(2,128)(2,1)} custom-call(bf16[8,2,7168]{2,1,0:T(2,128)(2,1)} %copy.64.x_ref), custom_call_target="tpu_custom_call" | custom-call | tf_op jit(solution)/shard_map/pallas_call | solution.py:69
  109.2 10.9 %shard_map.77.x_ref = bf16[32,2,7168]{2,1,0:T(2,128)(2,1)} custom-call(bf16[32,2,7168]{2,1,0:T(2,128)(2,1)} %shard_map.76.x_ref, bf16[7168,256]{1,0:T(8,128)(2,1)} %bitcast.54, bf16[7168,256]{1,0:T(8,128)(2,1)} %bitcast.56, bf16[256,7168]{1,0:T(8,128)(2,1)} %bitcast.58), custom_call_target="tpu_custom_call" | custom-call | flops 704643072 | bytes 12845056 | tf_op jit(solution)/shard_map/pallas_call | solution.py:111
  120.1 27.1 %shard_map.78 = bf16[32,2,7168]{2,1,0:T(2,128)(2,1)} custom-call(bf16[32,2,7168]{2,1,0:T(2,128)(2,1)} %shard_map.77.x_ref), custom_call_target="tpu_custom_call" | custom-call | tf_op jit(solution)/shard_map/pallas_call | solution.py:69
  147.3 1.5 fusion.5
  148.8 4.8 %collective-permute-done.1 = bf16[4,7168]{1,0:T(4,128)(2,1)S(1)} collective-permute-done((bf16[4,7168]{1,0:T(4,128)(2,1)S(1)}, bf16[4,7168]{1,0:T(4,128)(2,1)S(1)}, u32[]{:S(2)}, u32[]{:S(2)}) %collective-permute-start.1) | collective-permute-done | bytes 57376 | tf_op jit(solution)/shard_map/ppermute | solution.py:137
  153.6 0.6 copy.67
  (27 shorter events, 1.0 us)
Async XLA Ops:
  36.8 37.9 %copy-start = (bf16[1,4,7168]{2,1,0:T(4,128)(2,1)S(1)}, bf16[1,4,7168]{2,1,0:T(4,128)(2,1)}, u32[]{:S(2)}) copy-start(bf16[1,4,7168]{2,1,0:T(4,128)(2,1)} %param.7) | copy-start | bytes 172036
  36.8 44.4 %copy-start.1 = (f32[1,7168]{1,0:T(1,128)S(1)}, f32[1,7168]{1,0:T(1,128)}, u32[]{:S(2)}) copy-start(f32[1,7168]{1,0:T(1,128)} %param.10) | copy-start | bytes 86020
  76.2 4.8 %collective-permute-start = (bf16[4,7168]{1,0:T(4,128)(2,1)S(1)}, bf16[4,7168]{1,0:T(4,128)(2,1)S(1)}, u32[]{:S(2)}, u32[]{:S(2)}) collective-permute-start(bf16[4,7168]{1,0:T(4,128)(2,1)S(1)} %fusion.4), channel_id=1, source_target_pairs={{0,32},{32,64},{64,96},{96,128},{128,160},{160,192},{192,224},{224... | collective-permute-start | bytes 172040 | tf_op jit(solution)/shard_map/ppermute | solution.py:137
  148.7 4.8 %collective-permute-start.1 = (bf16[4,7168]{1,0:T(4,128)(2,1)S(1)}, bf16[4,7168]{1,0:T(4,128)(2,1)S(1)}, u32[]{:S(2)}, u32[]{:S(2)}) collective-permute-start(bf16[4,7168]{1,0:T(4,128)(2,1)S(1)} %fusion.5), channel_id=1, source_target_pairs={{0,32},{32,64},{64,96},{96,128},{128,160},{160,192},{192,224},{224... | collective-permute-start | bytes 172040 | tf_op jit(solution)/shard_map/ppermute | solution.py:137

commit v6 on v5

--- a/solution.py
+++ b/solution.py
@@ -80,26 +80,33 @@
     )(x)
 
 
-def ffn_kernel(x_ref, g_ref, u_ref, d_ref, o_ref, acc_g, acc_u):
+def ffn_kernel(steps, x_ref, g_ref, u_ref, d_ref, o_ref, acc_g, acc_u, inner):
     k = pl.program_id(0)
+    slots = x_ref.shape[1]
 
     @pl.when(k == 0)
     def _():
         acc_g[...] = jnp.zeros_like(acc_g)
         acc_u[...] = jnp.zeros_like(acc_u)
 
-    for c in range(x_ref.shape[1]):
-        xc = x_ref[:, c, :]
-        acc_g[c] += jnp.dot(xc, g_ref[...], preferred_element_type=jnp.float32)
-        acc_u[c] += jnp.dot(xc, u_ref[...], preferred_element_type=jnp.float32)
-
-    @pl.when(k == pl.num_programs(0) - 1)
-    def _():
-        for c in range(x_ref.shape[1]):
+    @pl.when(k < steps)
+    def _():
+        for c in range(slots):
+            xc = x_ref[:, c, :]
+            acc_g[c] += jnp.dot(xc, g_ref[...], preferred_element_type=jnp.float32)
+            acc_u[c] += jnp.dot(xc, u_ref[...], preferred_element_type=jnp.float32)
+
+    @pl.when(k == steps)
+    def _():
+        for c in range(slots):
             g = acc_g[c]
-            inner = (g / (1.0 + jnp.exp(-g)) * acc_u[c]).astype(jnp.bfloat16)
+            inner[c] = (g / (1.0 + jnp.exp(-g)) * acc_u[c]).astype(jnp.bfloat16)
+
+    @pl.when(k >= steps)
+    def _():
+        for c in range(slots):
             o_ref[:, c, :] = jnp.dot(
-                inner, d_ref[...], preferred_element_type=jnp.float32
+                inner[c], d_ref[...], preferred_element_type=jnp.float32
             ).astype(o_ref.dtype)
 
 
@@ -107,21 +114,30 @@
     sources, slots, model_dim = x.shape
     hidden = gate_mat.shape[1]
     chunk = 1024
+    steps = model_dim // chunk
     rows = sources * slots
+
+    def first(k):
+        return jnp.minimum(k, steps - 1)
+
+    def second(k):
+        return jnp.maximum(k - steps, 0)
+
     return pl.pallas_call(
-        ffn_kernel,
-        grid=(model_dim // chunk,),
+        functools.partial(ffn_kernel, steps),
+        grid=(2 * steps,),
         in_specs=[
-            pl.BlockSpec((sources, slots, chunk), lambda k: (0, 0, k)),
-            pl.BlockSpec((chunk, hidden), lambda k: (k, 0)),
-            pl.BlockSpec((chunk, hidden), lambda k: (k, 0)),
-            pl.BlockSpec((hidden, model_dim), lambda k: (0, 0)),
+            pl.BlockSpec((sources, slots, chunk), lambda k: (0, 0, first(k))),
+            pl.BlockSpec((chunk, hidden), lambda k: (first(k), 0)),
+            pl.BlockSpec((chunk, hidden), lambda k: (first(k), 0)),
+            pl.BlockSpec((hidden, chunk), lambda k: (0, second(k))),
         ],
-        out_specs=pl.BlockSpec((sources, slots, model_dim), lambda k: (0, 0, 0)),
+        out_specs=pl.BlockSpec((sources, slots, chunk), lambda k: (0, 0, second(k))),
         out_shape=jax.ShapeDtypeStruct(x.shape, jnp.bfloat16),
         scratch_shapes=[
             pltpu.VMEM((slots, sources, hidden), jnp.float32),
             pltpu.VMEM((slots, sources, hidden), jnp.float32),
+            pltpu.VMEM((slots, sources, hidden), jnp.bfloat16),
         ],
         cost_estimate=pl.CostEstimate(
             flops=6 * rows * model_dim * hidden,

time: 155 us -> 159 us (1.026)
  Pallas kernels: 134 us -> 138 us
    pallas_call x2, Pallas kernels: 21.9 us -> 25.7 us  [expert_ffn(): pl.pallas_call(functools.partial(ffn_kernel, steps), grid=(2 * steps,), i...]
where the time goes in v6:
time: 159 us; the launch traced here: 158 us
  Pallas kernels  138 us (87%)
  waiting for transfers between devices  8.48 us (5%)
  local copies, waits for them, and re-layouts  5.12 us (3%)
  matrix products  4.31 us (3%)
  other arithmetic  2.34 us (1%)
    pallas_call x4, Pallas kernels, exchange(): pl.pallas_call(functools.partial(exchange_kernel, count, spread), out_sha...  112 us
    pallas_call x2, Pallas kernels, expert_ffn(): pl.pallas_call(functools.partial(ffn_kernel, steps), grid=(2 * steps,), i...  25.7 us
    ppermute x2, waiting for transfers between devices, shifted(): return lax.ppermute(value, axis, pairs)  8.48 us
  transfers between devices with their start and end apart: 2, of which 2 were waited for; matrix products, arithmetic and copies ran while one was open for 1% of the time, Pallas kernels for 0%

profile of v6, /device:TPU:32, one launch (start us, length us, event | category | flops | bytes accessed | tf_op | source)
XLA Modules:
  0.0 158.0 jit_solution(10227289335074459917)
XLA Ops:
  0.0 1.0 fusion.13
  1.0 0.7 slice_bitcast_fusion
  2.0 0.7 bitcast_convert_fusion
  3.0 0.6 gather_fusion
  3.6 0.1 copy.43
  3.7 1.1 fusion.17
  4.8 0.9 copy.65.x_ref
  5.7 31.1 %shard_map.73.x_ref = bf16[32,2,7168]{2,1,0:T(2,128)(2,1)} custom-call(bf16[8,2,7168]{2,1,0:T(2,128)(2,1)} %copy.65.x_ref), custom_call_target="tpu_custom_call" | custom-call | tf_op jit(solution)/shard_map/pallas_call | solution.py:69
  36.8 12.8 %shard_map.74.x_ref = bf16[32,2,7168]{2,1,0:T(2,128)(2,1)} custom-call(bf16[32,2,7168]{2,1,0:T(2,128)(2,1)} %shard_map.73.x_ref, bf16[7168,256]{1,0:T(8,128)(2,1)} %bitcast.53, bf16[7168,256]{1,0:T(8,128)(2,1)} %bitcast.55, bf16[256,7168]{1,0:T(8,128)(2,1)} %bitcast.57), custom_call_target="tpu_custom_call" | custom-call | flops 704643072 | bytes 12845056 | tf_op jit(solution)/shard_map/pallas_call | solution.py:126
  49.7 26.9 %shard_map.75 = bf16[32,2,7168]{2,1,0:T(2,128)(2,1)} custom-call(bf16[32,2,7168]{2,1,0:T(2,128)(2,1)} %shard_map.74.x_ref), custom_call_target="tpu_custom_call" | custom-call | tf_op jit(solution)/shard_map/pallas_call | solution.py:69
  76.6 1.5 fusion.4
  78.2 0.1 copy.47
  78.6 0.6 gather_fusion.1
  79.2 0.1 copy.50
  79.3 3.7 %collective-permute-done = bf16[4,7168]{1,0:T(4,128)(2,1)S(1)} collective-permute-done((bf16[4,7168]{1,0:T(4,128)(2,1)S(1)}, bf16[4,7168]{1,0:T(4,128)(2,1)S(1)}, u32[]{:S(2)}, u32[]{:S(2)}) %collective-permute-start) | collective-permute-done | bytes 57376 | tf_op jit(solution)/shard_map/ppermute | solution.py:153
  82.9 0.2 fusion.10
  83.1 0.3 fusion.20
  83.4 0.9 copy.64.x_ref
  84.3 26.8 %shard_map.76.x_ref = bf16[32,2,7168]{2,1,0:T(2,128)(2,1)} custom-call(bf16[8,2,7168]{2,1,0:T(2,128)(2,1)} %copy.64.x_ref), custom_call_target="tpu_custom_call" | custom-call | tf_op jit(solution)/shard_map/pallas_call | solution.py:69
  111.1 12.8 %shard_map.77.x_ref = bf16[32,2,7168]{2,1,0:T(2,128)(2,1)} custom-call(bf16[32,2,7168]{2,1,0:T(2,128)(2,1)} %shard_map.76.x_ref, bf16[7168,256]{1,0:T(8,128)(2,1)} %bitcast.54, bf16[7168,256]{1,0:T(8,128)(2,1)} %bitcast.56, bf16[256,7168]{1,0:T(8,128)(2,1)} %bitcast.58), custom_call_target="tpu_custom_call" | custom-call | flops 704643072 | bytes 12845056 | tf_op jit(solution)/shard_map/pallas_call | solution.py:126
  124.0 27.1 %shard_map.78 = bf16[32,2,7168]{2,1,0:T(2,128)(2,1)} custom-call(bf16[32,2,7168]{2,1,0:T(2,128)(2,1)} %shard_map.77.x_ref), custom_call_target="tpu_custom_call" | custom-call | tf_op jit(solution)/shard_map/pallas_call | solution.py:69
  151.1 1.5 fusion.5
  152.6 4.8 %collective-permute-done.1 = bf16[4,7168]{1,0:T(4,128)(2,1)S(1)} collective-permute-done((bf16[4,7168]{1,0:T(4,128)(2,1)S(1)}, bf16[4,7168]{1,0:T(4,128)(2,1)S(1)}, u32[]{:S(2)}, u32[]{:S(2)}) %collective-permute-start.1) | collective-permute-done | bytes 57376 | tf_op jit(solution)/shard_map/ppermute | solution.py:153
  157.4 0.6 copy.67
  (27 shorter events, 1.0 us)
Async XLA Ops:
  36.8 39.8 %copy-start = (bf16[1,4,7168]{2,1,0:T(4,128)(2,1)S(1)}, bf16[1,4,7168]{2,1,0:T(4,128)(2,1)}, u32[]{:S(2)}) copy-start(bf16[1,4,7168]{2,1,0:T(4,128)(2,1)} %param.7) | copy-start | bytes 172036
  36.8 46.3 %copy-start.1 = (f32[1,7168]{1,0:T(1,128)S(1)}, f32[1,7168]{1,0:T(1,128)}, u32[]{:S(2)}) copy-start(f32[1,7168]{1,0:T(1,128)} %param.10) | copy-start | bytes 86020
  78.1 4.8 %collective-permute-start = (bf16[4,7168]{1,0:T(4,128)(2,1)S(1)}, bf16[4,7168]{1,0:T(4,128)(2,1)S(1)}, u32[]{:S(2)}, u32[]{:S(2)}) collective-permute-start(bf16[4,7168]{1,0:T(4,128)(2,1)S(1)} %fusion.4), channel_id=1, source_target_pairs={{0,32},{32,64},{64,96},{96,128},{128,160},{160,192},{192,224},{224... | collective-permute-start | bytes 172040 | tf_op jit(solution)/shard_map/ppermute | solution.py:153
  152.6 4.8 %collective-permute-start.1 = (bf16[4,7168]{1,0:T(4,128)(2,1)S(1)}, bf16[4,7168]{1,0:T(4,128)(2,1)S(1)}, u32[]{:S(2)}, u32[]{:S(2)}) collective-permute-start(bf16[4,7168]{1,0:T(4,128)(2,1)S(1)} %fusion.5), channel_id=1, source_target_pairs={{0,32},{32,64},{64,96},{96,128},{128,160},{160,192},{192,224},{224... | collective-permute-start | bytes 172040 | tf_op jit(solution)/shard_map/ppermute | solution.py:153

commit v7 on v5

--- a/solution.py
+++ b/solution.py
@@ -10,16 +10,29 @@
 GROUP = 4
 
 
+def signed_step(index):
+    odd = index % 2
+    return odd * ((index + 1) // 2) - (1 - odd) * (index // 2)
+
+
 def exchange_kernel(count, spread, x_ref, y_ref, send_sem, recv_sem, own_sem):
     me = lax.axis_index("expert")
     seg = lax.axis_index("segment")
+    ring_z = 8
+    ring_y = count // ring_z
+    my_y = me // ring_z
+    my_z = me % ring_z
+
+    def peer_at(d, sign):
+        step_z = signed_step(d % ring_z) * sign
+        step_y = signed_step(d // ring_z) * sign
+        return ((my_y + step_y + ring_y) % ring_y) * ring_z + (my_z + step_z + ring_z) % ring_z
 
     barrier = pltpu.get_barrier_semaphore()
 
     def greet(d, carry):
-        peer = lax.rem(me + d, count)
         pl.semaphore_signal(
-            barrier, inc=1, device_id=(seg, peer), device_id_type=pl.DeviceIdType.MESH
+            barrier, inc=1, device_id=(seg, peer_at(d, 1)), device_id_type=pl.DeviceIdType.MESH
         )
         return carry
 
@@ -50,14 +63,14 @@
         )
 
     def send(d, carry):
-        outgoing(lax.rem(me + d, count)).start()
+        outgoing(peer_at(d, 1)).start()
         return carry
 
     lax.fori_loop(1, count, send, 0)
 
     def finish(d, carry):
-        outgoing(lax.rem(me + d, count)).wait_send()
-        incoming(lax.rem(me + count - d, count)).wait_recv()
+        outgoing(peer_at(d, 1)).wait_send()
+        incoming(peer_at(d, -1)).wait_recv()
         return carry
 
     lax.fori_loop(1, count, finish, 0)

time: 155 us -> 162 us (1.045)
  Pallas kernels: 134 us -> 141 us
    pallas_call x4, Pallas kernels: 112 us -> 119 us  [exchange(): pl.pallas_call(functools.partial(exchange_kernel, count, spread), out_sha...]
where the time goes in v7:
time: 162 us
  Pallas kernels  141 us (87%)
  waiting for transfers between devices  8.48 us (5%)
  local copies, waits for them, and re-layouts  5.12 us (3%)
  matrix products  4.31 us (3%)
  other arithmetic  2.34 us (1%)
    pallas_call x4, Pallas kernels, exchange(): pl.pallas_call(functools.partial(exchange_kernel, count, spread), out_sha...  119 us
    pallas_call x2, Pallas kernels, expert_ffn(): pl.pallas_call(ffn_kernel, grid=(model_dim // chunk,), in_specs=[pl.Block...  21.9 us
    ppermute x2, waiting for transfers between devices, shifted(): return lax.ppermute(value, axis, pairs)  8.48 us
  transfers between devices with their start and end apart: 2, of which 2 were waited for; matrix products, arithmetic and copies ran while one was open for 1% of the time, Pallas kernels for 0%

profile of v7, /device:TPU:32, one launch (start us, length us, event | category | flops | bytes accessed | tf_op | source)
XLA Modules:
  0.0 161.6 jit_solution(12279822120125910857)
XLA Ops:
  0.0 1.0 fusion.13
  1.0 0.7 slice_bitcast_fusion
  2.0 0.7 bitcast_convert_fusion
  3.0 0.6 gather_fusion
  3.6 0.1 copy.43
  3.7 1.1 fusion.17
  4.8 0.9 copy.65.x_ref
  5.7 32.6 %shard_map.73.x_ref = bf16[32,2,7168]{2,1,0:T(2,128)(2,1)} custom-call(bf16[8,2,7168]{2,1,0:T(2,128)(2,1)} %copy.65.x_ref), custom_call_target="tpu_custom_call" | custom-call | tf_op jit(solution)/shard_map/pallas_call | solution.py:82
  38.3 10.9 %shard_map.74.x_ref = bf16[32,2,7168]{2,1,0:T(2,128)(2,1)} custom-call(bf16[32,2,7168]{2,1,0:T(2,128)(2,1)} %shard_map.73.x_ref, bf16[7168,256]{1,0:T(8,128)(2,1)} %bitcast.53, bf16[7168,256]{1,0:T(8,128)(2,1)} %bitcast.55, bf16[256,7168]{1,0:T(8,128)(2,1)} %bitcast.57), custom_call_target="tpu_custom_call" | custom-call | flops 704643072 | bytes 12845056 | tf_op jit(solution)/shard_map/pallas_call | solution.py:124
  49.2 29.3 %shard_map.75 = bf16[32,2,7168]{2,1,0:T(2,128)(2,1)} custom-call(bf16[32,2,7168]{2,1,0:T(2,128)(2,1)} %shard_map.74.x_ref), custom_call_target="tpu_custom_call" | custom-call | tf_op jit(solution)/shard_map/pallas_call | solution.py:82
  78.6 1.5 fusion.4
  80.1 0.1 copy.47
  80.5 0.6 gather_fusion.1
  81.1 0.1 copy.50
  81.2 3.7 %collective-permute-done = bf16[4,7168]{1,0:T(4,128)(2,1)S(1)} collective-permute-done((bf16[4,7168]{1,0:T(4,128)(2,1)S(1)}, bf16[4,7168]{1,0:T(4,128)(2,1)S(1)}, u32[]{:S(2)}, u32[]{:S(2)}) %collective-permute-start) | collective-permute-done | bytes 57376 | tf_op jit(solution)/shard_map/ppermute | solution.py:150
  84.9 0.2 fusion.10
  85.1 0.3 fusion.20
  85.4 0.9 copy.64.x_ref
  86.3 28.5 %shard_map.76.x_ref = bf16[32,2,7168]{2,1,0:T(2,128)(2,1)} custom-call(bf16[8,2,7168]{2,1,0:T(2,128)(2,1)} %copy.64.x_ref), custom_call_target="tpu_custom_call" | custom-call | tf_op jit(solution)/shard_map/pallas_call | solution.py:82
  114.8 10.9 %shard_map.77.x_ref = bf16[32,2,7168]{2,1,0:T(2,128)(2,1)} custom-call(bf16[32,2,7168]{2,1,0:T(2,128)(2,1)} %shard_map.76.x_ref, bf16[7168,256]{1,0:T(8,128)(2,1)} %bitcast.54, bf16[7168,256]{1,0:T(8,128)(2,1)} %bitcast.56, bf16[256,7168]{1,0:T(8,128)(2,1)} %bitcast.58), custom_call_target="tpu_custom_call" | custom-call | flops 704643072 | bytes 12845056 | tf_op jit(solution)/shard_map/pallas_call | solution.py:124
  125.7 29.0 %shard_map.78 = bf16[32,2,7168]{2,1,0:T(2,128)(2,1)} custom-call(bf16[32,2,7168]{2,1,0:T(2,128)(2,1)} %shard_map.77.x_ref), custom_call_target="tpu_custom_call" | custom-call | tf_op jit(solution)/shard_map/pallas_call | solution.py:82
  154.7 1.5 fusion.5
  156.2 4.8 %collective-permute-done.1 = bf16[4,7168]{1,0:T(4,128)(2,1)S(1)} collective-permute-done((bf16[4,7168]{1,0:T(4,128)(2,1)S(1)}, bf16[4,7168]{1,0:T(4,128)(2,1)S(1)}, u32[]{:S(2)}, u32[]{:S(2)}) %collective-permute-start.1) | collective-permute-done | bytes 57376 | tf_op jit(solution)/shard_map/ppermute | solution.py:150
  161.0 0.6 copy.67
  (27 shorter events, 1.0 us)
Async XLA Ops:
  38.3 40.3 %copy-start = (bf16[1,4,7168]{2,1,0:T(4,128)(2,1)S(1)}, bf16[1,4,7168]{2,1,0:T(4,128)(2,1)}, u32[]{:S(2)}) copy-start(bf16[1,4,7168]{2,1,0:T(4,128)(2,1)} %param.7) | copy-start | bytes 172036
  38.3 46.8 %copy-start.1 = (f32[1,7168]{1,0:T(1,128)S(1)}, f32[1,7168]{1,0:T(1,128)}, u32[]{:S(2)}) copy-start(f32[1,7168]{1,0:T(1,128)} %param.10) | copy-start | bytes 86020
  80.1 4.8 %collective-permute-start = (bf16[4,7168]{1,0:T(4,128)(2,1)S(1)}, bf16[4,7168]{1,0:T(4,128)(2,1)S(1)}, u32[]{:S(2)}, u32[]{:S(2)}) collective-permute-start(bf16[4,7168]{1,0:T(4,128)(2,1)S(1)} %fusion.4), channel_id=1, source_target_pairs={{0,32},{32,64},{64,96},{96,128},{128,160},{160,192},{192,224},{224... | collective-permute-start | bytes 172040 | tf_op jit(solution)/shard_map/ppermute | solution.py:150
  156.2 4.8 %collective-permute-start.1 = (bf16[4,7168]{1,0:T(4,128)(2,1)S(1)}, bf16[4,7168]{1,0:T(4,128)(2,1)S(1)}, u32[]{:S(2)}, u32[]{:S(2)}) collective-permute-start(bf16[4,7168]{1,0:T(4,128)(2,1)S(1)} %fusion.5), channel_id=1, source_target_pairs={{0,32},{32,64},{64,96},{96,128},{128,160},{160,192},{192,224},{224... | collective-permute-start | bytes 172040 | tf_op jit(solution)/shard_map/ppermute | solution.py:150

commit v8 on v5

--- a/solution.py
+++ b/solution.py
@@ -72,6 +72,164 @@
         in_specs=[pl.BlockSpec(memory_space=pl.ANY)],
         out_specs=pl.BlockSpec(memory_space=pl.ANY),
         scratch_shapes=[
+            pltpu.SemaphoreType.DMA((count,)),
+            pltpu.SemaphoreType.DMA((count,)),
+            pltpu.SemaphoreType.DMA,
+        ],
+        compiler_params=pltpu.CompilerParams(collective_id=collective_id, has_side_effects=True),
+    )(x)
+
+
+def entry_z(z_from, half, line):
+    ring = 2 * line
+    inside = (z_from // line) == half
+    r = z_from % line
+    low = (z_from - 1 - r + ring) % ring
+    high = (z_from + line - r) % ring
+    return jnp.where(inside, z_from, jnp.where(r < line // 2, low, high))
+
+
+def dispatch_kernel(count, x_ref, y_ref, send_sem, recv_sem, right_sem, left_sem, own_sem):
+    me = lax.axis_index("expert")
+    seg = lax.axis_index("segment")
+    line = GROUP
+    ring_z = 2 * line
+    my_y = me // ring_z
+    my_z = me % ring_z
+    my_half = my_z // line
+    pos = my_z % line
+    group = me // GROUP
+    groups = count // GROUP
+
+    barrier = pltpu.get_barrier_semaphore()
+
+    def greet(d, carry):
+        pl.semaphore_signal(
+            barrier, inc=1, device_id=(seg, lax.rem(me + d, count)),
+            device_id_type=pl.DeviceIdType.MESH,
+        )
+        return carry
+
+    lax.fori_loop(1, count, greet, 0)
+    pl.semaphore_wait(barrier, count - 1)
+
+    own = pltpu.make_async_copy(x_ref.at[group], y_ref.at[me], own_sem)
+    own.start()
+
+    def first_hop(g):
+        target = (g // 2) * ring_z + entry_z(my_z, g % 2, line)
+        return pltpu.make_async_remote_copy(
+            src_ref=x_ref.at[g],
+            dst_ref=y_ref.at[me],
+            send_sem=send_sem.at[g],
+            recv_sem=recv_sem.at[me],
+            device_id=(seg, target),
+            device_id_type=pl.DeviceIdType.MESH,
+        )
+
+    def send(i, carry):
+        g = lax.rem(group + i, groups)
+        first_hop(g).start()
+        return carry
+
+    lax.fori_loop(1, groups, send, 0)
+
+    def relay(p, step, sem):
+        source = x_ref.at[group] if p is None else y_ref.at[p]
+        slot = me if p is None else p
+        return pltpu.make_async_remote_copy(
+            src_ref=source,
+            dst_ref=y_ref.at[slot],
+            send_sem=sem.at[slot],
+            recv_sem=recv_sem.at[slot],
+            device_id=(seg, me + step),
+            device_id_type=pl.DeviceIdType.MESH,
+        )
+
+    def arrival(p):
+        return pltpu.make_async_remote_copy(
+            src_ref=x_ref.at[group],
+            dst_ref=y_ref.at[p],
+            send_sem=send_sem.at[0],
+            recv_sem=recv_sem.at[p],
+            device_id=(seg, p),
+            device_id_type=pl.DeviceIdType.MESH,
+        )
+
+    def entry_pos(p):
+        return entry_z(p % ring_z, my_half, line) % line
+
+    @pl.when(pos < line - 1)
+    def _():
+        relay(None, 1, right_sem).start()
+
+    @pl.when(pos > 0)
+    def _():
+        relay(None, -1, left_sem).start()
+
+    for delta in range(line):
+        def forward(i, carry):
+            p = lax.rem(me + i, count)
+            e = entry_pos(p)
+            far = jnp.abs(e - pos)
+
+            @pl.when(far == delta)
+            def _():
+                arrival(p).wait_recv()
+
+                @pl.when((e <= pos) & (pos < line - 1))
+                def _():
+                    relay(p, 1, right_sem).start()
+
+                @pl.when((e >= pos) & (pos > 0))
+                def _():
+                    relay(p, -1, left_sem).start()
+
+            return carry
+
+        lax.fori_loop(1, count, forward, 0)
+
+    def drain(i, carry):
+        p = lax.rem(me + i, count)
+        e = entry_pos(p)
+
+        @pl.when((e <= pos) & (pos < line - 1))
+        def _():
+            relay(p, 1, right_sem).wait_send()
+
+        @pl.when((e >= pos) & (pos > 0))
+        def _():
+            relay(p, -1, left_sem).wait_send()
+
+        return carry
+
+    lax.fori_loop(1, count, drain, 0)
+
+    @pl.when(pos < line - 1)
+    def _():
+        relay(None, 1, right_sem).wait_send()
+
+    @pl.when(pos > 0)
+    def _():
+        relay(None, -1, left_sem).wait_send()
+
+    def sent(i, carry):
+        first_hop(lax.rem(group + i, groups)).wait_send()
+        return carry
+
+    lax.fori_loop(1, groups, sent, 0)
+    own.wait()
+
+
+def dispatch(x, count, collective_id):
+    return pl.pallas_call(
+        functools.partial(dispatch_kernel, count),
+        out_shape=jax.ShapeDtypeStruct((count,) + x.shape[1:], x.dtype),
+        in_specs=[pl.BlockSpec(memory_space=pl.ANY)],
+        out_specs=pl.BlockSpec(memory_space=pl.ANY),
+        scratch_shapes=[
+            pltpu.SemaphoreType.DMA((x.shape[0],)),
+            pltpu.SemaphoreType.DMA((count,)),
             pltpu.SemaphoreType.DMA((count,)),
             pltpu.SemaphoreType.DMA((count,)),
             pltpu.SemaphoreType.DMA,
@@ -174,7 +332,7 @@
         packed_weight = jnp.sum(
             jnp.where(placer, dense_weight.T[:, None, :], jnp.float32(0.0)), axis=2
         )
-        got = exchange(packed, owners, 0)
+        got = dispatch(packed, owners, 2)
         terms = expert_ffn(got, gate_mat, up_mat, down_mat)
 
         back = exchange(terms, owners, 1)

time: 155 us -> 158 us (1.019)
  the two profiles are of different devices: /device:TPU:32 before, /device:TPU:1 now
where the time goes in v8:
time: 158 us
  Pallas kernels  130 us (82%)
  starting transfers between devices  14.3 us (9%)
  local copies, waits for them, and re-layouts  5.12 us (3%)
  matrix products  4.31 us (3%)
  other arithmetic  2.34 us (1%)
    pallas_call x2, Pallas kernels, dispatch(): pl.pallas_call(functools.partial(dispatch_kernel, count), out_shape=jax.S...  59.5 us
    pallas_call x2, Pallas kernels, exchange(): pl.pallas_call(functools.partial(exchange_kernel, count, spread), out_sha...  48.7 us
    pallas_call x2, Pallas kernels, expert_ffn(): pl.pallas_call(ffn_kernel, grid=(model_dim // chunk,), in_specs=[pl.Block...  21.9 us
    ppermute x2, starting transfers between devices, shifted(): return lax.ppermute(value, axis, pairs)  14.3 us
  transfers between devices with their start and end apart: 2, of which 2 were waited for; matrix products, arithmetic and copies ran while one was open for 1% of the time, Pallas kernels for 0%

profile of v8, /device:TPU:1, one launch (start us, length us, event | category | flops | bytes accessed | tf_op | source)
XLA Modules:
  0.0 157.7 jit_solution(2128480420408792394)
XLA Ops:
  0.0 1.0 fusion.13
  1.0 0.7 slice_bitcast_fusion
  2.0 0.7 bitcast_convert_fusion
  3.0 0.6 gather_fusion
  3.6 0.1 copy.43
  3.7 1.1 fusion.17
  4.8 0.9 copy.65.x_ref
  5.7 35.2 %shard_map.73.x_ref = bf16[32,2,7168]{2,1,0:T(2,128)(2,1)} custom-call(bf16[8,2,7168]{2,1,0:T(2,128)(2,1)} %copy.65.x_ref), custom_call_target="tpu_custom_call" | custom-call | tf_op jit(solution)/shard_map/pallas_call | solution.py:225
  40.9 10.9 %shard_map.74.x_ref = bf16[32,2,7168]{2,1,0:T(2,128)(2,1)} custom-call(bf16[32,2,7168]{2,1,0:T(2,128)(2,1)} %shard_map.73.x_ref, bf16[7168,256]{1,0:T(8,128)(2,1)} %bitcast.53, bf16[7168,256]{1,0:T(8,128)(2,1)} %bitcast.55, bf16[256,7168]{1,0:T(8,128)(2,1)} %bitcast.57), custom_call_target="tpu_custom_call" | custom-call | flops 704643072 | bytes 12845056 | tf_op jit(solution)/shard_map/pallas_call | solution.py:269
  51.9 24.6 %shard_map.75 = bf16[32,2,7168]{2,1,0:T(2,128)(2,1)} custom-call(bf16[32,2,7168]{2,1,0:T(2,128)(2,1)} %shard_map.74.x_ref), custom_call_target="tpu_custom_call" | custom-call | tf_op jit(solution)/shard_map/pallas_call | solution.py:69
  76.5 1.5 fusion.4
  78.0 4.5 %collective-permute-start = (bf16[4,7168]{1,0:T(4,128)(2,1)S(1)}, bf16[4,7168]{1,0:T(4,128)(2,1)S(1)}, u32[]{:S(2)}, u32[]{:S(2)}) collective-permute-start(bf16[4,7168]{1,0:T(4,128)(2,1)S(1)} %fusion.4), channel_id=1, source_target_pairs={{0,32},{32,64},{64,96},{96,128},{128,160},{160,192},{192,224},{224... | collective-permute-start | bytes 172040 | tf_op jit(solution)/shard_map/ppermute | solution.py:295
  82.9 0.6 gather_fusion.1
  83.6 0.1 collective-permute-done
  83.8 0.2 fusion.10
  84.0 0.3 fusion.20
  84.2 0.9 copy.64.x_ref
  85.2 24.3 %shard_map.76.x_ref = bf16[32,2,7168]{2,1,0:T(2,128)(2,1)} custom-call(bf16[8,2,7168]{2,1,0:T(2,128)(2,1)} %copy.64.x_ref), custom_call_target="tpu_custom_call" | custom-call | tf_op jit(solution)/shard_map/pallas_call | solution.py:225
  109.5 10.9 %shard_map.77.x_ref = bf16[32,2,7168]{2,1,0:T(2,128)(2,1)} custom-call(bf16[32,2,7168]{2,1,0:T(2,128)(2,1)} %shard_map.76.x_ref, bf16[7168,256]{1,0:T(8,128)(2,1)} %bitcast.54, bf16[7168,256]{1,0:T(8,128)(2,1)} %bitcast.56, bf16[256,7168]{1,0:T(8,128)(2,1)} %bitcast.58), custom_call_target="tpu_custom_call" | custom-call | flops 704643072 | bytes 12845056 | tf_op jit(solution)/shard_map/pallas_call | solution.py:269
  120.4 24.1 %shard_map.78 = bf16[32,2,7168]{2,1,0:T(2,128)(2,1)} custom-call(bf16[32,2,7168]{2,1,0:T(2,128)(2,1)} %shard_map.77.x_ref), custom_call_target="tpu_custom_call" | custom-call | tf_op jit(solution)/shard_map/pallas_call | solution.py:69
  144.5 1.5 fusion.5
  146.0 9.8 %collective-permute-start.1 = (bf16[4,7168]{1,0:T(4,128)(2,1)S(1)}, bf16[4,7168]{1,0:T(4,128)(2,1)S(1)}, u32[]{:S(2)}, u32[]{:S(2)}) collective-permute-start(bf16[4,7168]{1,0:T(4,128)(2,1)S(1)} %fusion.5), channel_id=1, source_target_pairs={{0,32},{32,64},{64,96},{96,128},{128,160},{160,192},{192,224},{224... | collective-permute-start | bytes 172040 | tf_op jit(solution)/shard_map/ppermute | solution.py:295
  155.8 1.3 collective-permute-done.1
  157.1 0.6 copy.67
  (27 shorter events, 1.1 us)
Async XLA Ops:
  40.9 35.6 %copy-start = (bf16[1,4,7168]{2,1,0:T(4,128)(2,1)S(1)}, bf16[1,4,7168]{2,1,0:T(4,128)(2,1)}, u32[]{:S(2)}) copy-start(bf16[1,4,7168]{2,1,0:T(4,128)(2,1)} %param.7) | copy-start | bytes 172036
  40.9 43.0 %copy-start.1 = (f32[1,7168]{1,0:T(1,128)S(1)}, f32[1,7168]{1,0:T(1,128)}, u32[]{:S(2)}) copy-start(f32[1,7168]{1,0:T(1,128)} %param.10) | copy-start | bytes 86020
  78.0 5.8 %collective-permute-start = (bf16[4,7168]{1,0:T(4,128)(2,1)S(1)}, bf16[4,7168]{1,0:T(4,128)(2,1)S(1)}, u32[]{:S(2)}, u32[]{:S(2)}) collective-permute-start(bf16[4,7168]{1,0:T(4,128)(2,1)S(1)} %fusion.4), channel_id=1, source_target_pairs={{0,32},{32,64},{64,96},{96,128},{128,160},{160,192},{192,224},{224... | collective-permute-start | bytes 172040 | tf_op jit(solution)/shard_map/ppermute | solution.py:295
  146.0 11.0 %collective-permute-start.1 = (bf16[4,7168]{1,0:T(4,128)(2,1)S(1)}, bf16[4,7168]{1,0:T(4,128)(2,1)S(1)}, u32[]{:S(2)}, u32[]{:S(2)}) collective-permute-start(bf16[4,7168]{1,0:T(4,128)(2,1)S(1)} %fusion.5), channel_id=1, source_target_pairs={{0,32},{32,64},{64,96},{96,128},{128,160},{160,192},{192,224},{224... | collective-permute-start | bytes 172040 | tf_op jit(solution)/shard_map/ppermute | solution.py:295

commit v9 on v5

--- a/solution.py
+++ b/solution.py
@@ -131,6 +131,127 @@
     )(x, gate_mat, up_mat, down_mat)
 
 
+def ffn_combine_kernel(count, steps, chunk, x_hbm, g_hbm, u_hbm, d_hbm, y_ref, terms_ref,
+                       acc_g, acc_u, inner, send_sem, recv_sem, own_sem):
+    me = lax.axis_index("expert")
+    seg = lax.axis_index("segment")
+    sources, slots = x_hbm.shape[0], x_hbm.shape[1]
+    hidden = g_hbm.shape[1]
+    model_dim = x_hbm.shape[2]
+
+    barrier = pltpu.get_barrier_semaphore()
+
+    def greet(d, carry):
+        pl.semaphore_signal(
+            barrier, inc=1, device_id=(seg, lax.rem(me + d, count)),
+            device_id_type=pl.DeviceIdType.MESH,
+        )
+        return carry
+
+    lax.fori_loop(1, count, greet, 0)
+
+    acc_g[...] = jnp.zeros_like(acc_g)
+    acc_u[...] = jnp.zeros_like(acc_u)
+
+    def gate_up(x_v, g_v, u_v):
+        for c in range(slots):
+            xc = x_v[:, c, :]
+            acc_g[c] += jnp.dot(xc, g_v[...], preferred_element_type=jnp.float32)
+            acc_u[c] += jnp.dot(xc, u_v[...], preferred_element_type=jnp.float32)
+
+    pltpu.emit_pipeline(
+        gate_up,
+        grid=(steps,),
+        in_specs=[
+            pl.BlockSpec((sources, slots, chunk), lambda k: (0, 0, k)),
+            pl.BlockSpec((chunk, hidden), lambda k: (k, 0)),
+            pl.BlockSpec((chunk, hidden), lambda k: (k, 0)),
+        ],
+    )(x_hbm, g_hbm, u_hbm)
+
+    for c in range(slots):
+        g = acc_g[c]
+        inner[c] = (g / (1.0 + jnp.exp(-g)) * acc_u[c]).astype(jnp.bfloat16)
+
+    def down(d_v, o_v):
+        for c in range(slots):
+            o_v[:, c, :] = jnp.dot(
+                inner[c], d_v[...], preferred_element_type=jnp.float32
+            ).astype(o_v.dtype)
+
+    pltpu.emit_pipeline(
+        down,
+        grid=(1,),
+        in_specs=[pl.BlockSpec((hidden, model_dim), lambda k: (0, 0))],
+        out_specs=[pl.BlockSpec((sources, slots, model_dim), lambda k: (0, 0, 0))],
+    )(d_hbm, terms_ref)
+
+    pl.semaphore_wait(barrier, count - 1)
+
+    own = pltpu.make_async_copy(terms_ref.at[me], y_ref.at[me], own_sem)
+    own.start()
+
+    def outgoing(peer):
+        return pltpu.make_async_remote_copy(
+            src_ref=terms_ref.at[peer],
+            dst_ref=y_ref.at[me],
+            send_sem=send_sem.at[peer],
+            recv_sem=recv_sem.at[me],
+            device_id=(seg, peer),
+            device_id_type=pl.DeviceIdType.MESH,
+        )
+
+    def incoming(peer):
+        return pltpu.make_async_remote_copy(
+            src_ref=terms_ref.at[me],
+            dst_ref=y_ref.at[peer],
+            send_sem=send_sem.at[peer],
+            recv_sem=recv_sem.at[peer],
+            device_id=(seg, peer),
+            device_id_type=pl.DeviceIdType.MESH,
+        )
+
+    def send(d, carry):
+        outgoing(lax.rem(me + d, count)).start()
+        return carry
+
+    lax.fori_loop(1, count, send, 0)
+
+    def finish(d, carry):
+        outgoing(lax.rem(me + d, count)).wait_send()
+        incoming(lax.rem(me + count - d, count)).wait_recv()
+        return carry
+
+    lax.fori_loop(1, count, finish, 0)
+    own.wait()
+
+
+def ffn_combine(x, gate_mat, up_mat, down_mat, collective_id):
+    count, slots, model_dim = x.shape
+    hidden = gate_mat.shape[1]
+    chunk = 1024
+    steps = model_dim // chunk
+    back, _ = pl.pallas_call(
+        functools.partial(ffn_combine_kernel, count, steps, chunk),
+        out_shape=(
+            jax.ShapeDtypeStruct(x.shape, jnp.bfloat16),
+            jax.ShapeDtypeStruct(x.shape, jnp.bfloat16),
+        ),
+        in_specs=[pl.BlockSpec(memory_space=pl.ANY)] * 4,
+        out_specs=(pl.BlockSpec(memory_space=pl.ANY), pl.BlockSpec(memory_space=pl.ANY)),
+        scratch_shapes=[
+            pltpu.VMEM((slots, count, hidden), jnp.float32),
+            pltpu.VMEM((slots, count, hidden), jnp.float32),
+            pltpu.VMEM((slots, count, hidden), jnp.bfloat16),
+            pltpu.SemaphoreType.DMA((count,)),
+            pltpu.SemaphoreType.DMA((count,)),
+            pltpu.SemaphoreType.DMA,
+        ],
+        compiler_params=pltpu.CompilerParams(collective_id=collective_id, has_side_effects=True),
+    )(x, gate_mat, up_mat, down_mat)
+    return back
+
+
 def shifted(value, axis, steps):
     count = lax.axis_size(axis)
     pairs = [(source, (source + steps) % count) for source in range(count)]
@@ -175,9 +296,7 @@
             jnp.where(placer, dense_weight.T[:, None, :], jnp.float32(0.0)), axis=2
         )
         got = exchange(packed, owners, 0)
-        terms = expert_ffn(got, gate_mat, up_mat, down_mat)
-
-        back = exchange(terms, owners, 1)
+        back = ffn_combine(got, gate_mat, up_mat, down_mat, 1)
         slot_weight = jnp.where(placer, packed_weight[:, :, None], jnp.float32(0.0))
         back_weight = slot_weight[owner_expert].astype(jnp.bfloat16)
         summed = jnp.einsum(

time: 155 us -> 148 us (0.955)
  Pallas kernels: 134 us -> 127 us
    pallas_call x4 -> x2, Pallas kernels: 112 us -> 58.4 us  [exchange(): pl.pallas_call(functools.partial(exchange_kernel, count, spread), out_sha...]
    pallas_call x2, Pallas kernels: 21.9 us -> 68.8 us  [ffn_combine(): pl.pallas_call(functools.partial(ffn_combine_kernel, count, steps, chunk)...]
where the time goes in v9:
time: 148 us
  Pallas kernels  127 us (86%)
  waiting for transfers between devices  8.48 us (6%)
  local copies, waits for them, and re-layouts  5.12 us (3%)
  matrix products  4.31 us (3%)
  other arithmetic  2.34 us (2%)
    pallas_call x2, Pallas kernels, ffn_combine(): pl.pallas_call(functools.partial(ffn_combine_kernel, count, steps, chunk)...  68.8 us
    pallas_call x2, Pallas kernels, exchange(): pl.pallas_call(functools.partial(exchange_kernel, count, spread), out_sha...  58.4 us
    ppermute x2, waiting for transfers between devices, shifted(): return lax.ppermute(value, axis, pairs)  8.48 us
    dot_general x2, matrix products, on_device(): jnp.einsum('ocr,ocd->rd', back_weight, back, preferred_element_type=jnp.f...  2.96 us
  transfers between devices with their start and end apart: 2, of which 2 were waited for; matrix products, arithmetic and copies ran while one was open for 1% of the time, Pallas kernels for 0%

profile of v9, /device:TPU:32, one launch (start us, length us, event | category | flops | bytes accessed | tf_op | source)
XLA Modules:
  0.0 147.6 jit_solution(7670454843294354034)
XLA Ops:
  0.0 1.0 fusion.13
  1.0 0.7 slice_bitcast_fusion
  1.8 0.1 copy.40
  2.0 0.7 bitcast_convert_fusion
  2.9 0.1 fusion.6
  3.0 0.6 gather_fusion
  3.6 0.1 copy.43
  3.7 1.1 fusion.17
  4.8 0.9 copy.65.x_ref
  5.7 31.1 %shard_map.73.x_hbm = bf16[32,2,7168]{2,1,0:T(2,128)(2,1)} custom-call(bf16[8,2,7168]{2,1,0:T(2,128)(2,1)} %copy.65.x_ref), custom_call_target="tpu_custom_call" | custom-call | tf_op jit(solution)/shard_map/pallas_call | solution.py:69
  36.8 34.2 %shard_map.74 = (bf16[32,2,7168]{2,1,0:T(2,128)(2,1)}, bf16[32,2,7168]{2,1,0:T(2,128)(2,1)}) custom-call(bf16[32,2,7168]{2,1,0:T(2,128)(2,1)} %shard_map.73.x_hbm, bf16[7168,256]{1,0:T(8,128)(2,1)} %bitcast.53, bf16[7168,256]{1,0:T(8,128)(2,1)} %bitcast.55, bf16[256,7168]{1,0:T(8,128)(2,1)} %bitcast.57), custom_call_target="tpu_custom_call" | custom-call | tf_op jit(solution)/shard_map/pallas_call | solution.py:234
  71.1 1.5 %fusion.4 = bf16[4,7168]{1,0:T(4,128)(2,1)S(1)} fusion(bf16[32,2,7168]{2,1,0:T(2,128)(2,1)} %get-tuple-element.7, bf16[1,4,7168]{2,1,0:T(4,128)(2,1)S(1)} %copy-done, bf16[32,2,4]{0,2,1:T(4,128)(2,1)S(1)} %copy.43), kind=kOutput, calls=%fused_computation.8 | convolution fusion | flops 3756032 | bytes 1032704 | tf_op jit(solution)/shard_map/ocr,ocd->rd/dot_general | solution.py:302
  72.6 0.1 copy.47
  73.0 0.6 gather_fusion.1
  73.6 0.1 copy.50
  73.7 3.7 %collective-permute-done = bf16[4,7168]{1,0:T(4,128)(2,1)S(1)} collective-permute-done((bf16[4,7168]{1,0:T(4,128)(2,1)S(1)}, bf16[4,7168]{1,0:T(4,128)(2,1)S(1)}, u32[]{:S(2)}, u32[]{:S(2)}) %collective-permute-start) | collective-permute-done | bytes 57376 | tf_op jit(solution)/shard_map/ppermute | solution.py:258
  77.4 0.2 fusion.10
  77.6 0.3 fusion.20
  77.8 0.9 copy.64.x_ref
  78.8 27.3 %shard_map.75.x_hbm = bf16[32,2,7168]{2,1,0:T(2,128)(2,1)} custom-call(bf16[8,2,7168]{2,1,0:T(2,128)(2,1)} %copy.64.x_ref), custom_call_target="tpu_custom_call" | custom-call | tf_op jit(solution)/shard_map/pallas_call | solution.py:69
  106.1 34.5 %shard_map.76 = (bf16[32,2,7168]{2,1,0:T(2,128)(2,1)}, bf16[32,2,7168]{2,1,0:T(2,128)(2,1)}) custom-call(bf16[32,2,7168]{2,1,0:T(2,128)(2,1)} %shard_map.75.x_hbm, bf16[7168,256]{1,0:T(8,128)(2,1)} %bitcast.54, bf16[7168,256]{1,0:T(8,128)(2,1)} %bitcast.56, bf16[256,7168]{1,0:T(8,128)(2,1)} %bitcast.58), custom_call_target="tpu_custom_call" | custom-call | tf_op jit(solution)/shard_map/pallas_call | solution.py:234
  140.7 1.5 %fusion.5 = bf16[4,7168]{1,0:T(4,128)(2,1)S(1)} fusion(bf16[32,2,7168]{2,1,0:T(2,128)(2,1)} %get-tuple-element.8, bf16[4,7168]{1,0:T(4,128)(2,1)S(1)} %collective-permute-done, bf16[32,2,4]{0,2,1:T(4,128)(2,1)S(1)} %copy.50), kind=kOutput, calls=%fused_computation.9 | convolution fusion | flops 3756032 | bytes 1032704 | tf_op jit(solution)/shard_map/ocr,ocd->rd/dot_general | solution.py:302
  142.2 4.8 %collective-permute-done.1 = bf16[4,7168]{1,0:T(4,128)(2,1)S(1)} collective-permute-done((bf16[4,7168]{1,0:T(4,128)(2,1)S(1)}, bf16[4,7168]{1,0:T(4,128)(2,1)S(1)}, u32[]{:S(2)}, u32[]{:S(2)}) %collective-permute-start.1) | collective-permute-done | bytes 57376 | tf_op jit(solution)/shard_map/ppermute | solution.py:258
  147.0 0.6 copy.67
  (25 shorter events, 0.8 us)
Async XLA Ops:
  36.8 34.3 %copy-start = (bf16[1,4,7168]{2,1,0:T(4,128)(2,1)S(1)}, bf16[1,4,7168]{2,1,0:T(4,128)(2,1)}, u32[]{:S(2)}) copy-start(bf16[1,4,7168]{2,1,0:T(4,128)(2,1)} %param.7) | copy-start | bytes 172036
  36.8 40.7 %copy-start.1 = (f32[1,7168]{1,0:T(1,128)S(1)}, f32[1,7168]{1,0:T(1,128)}, u32[]{:S(2)}) copy-start(f32[1,7168]{1,0:T(1,128)} %param.10) | copy-start | bytes 86020
  72.6 4.8 %collective-permute-start = (bf16[4,7168]{1,0:T(4,128)(2,1)S(1)}, bf16[4,7168]{1,0:T(4,128)(2,1)S(1)}, u32[]{:S(2)}, u32[]{:S(2)}) collective-permute-start(bf16[4,7168]{1,0:T(4,128)(2,1)S(1)} %fusion.4), channel_id=1, source_target_pairs={{0,32},{32,64},{64,96},{96,128},{128,160},{160,192},{192,224},{224... | collective-permute-start | bytes 172040 | tf_op jit(solution)/shard_map/ppermute | solution.py:258
  142.1 4.8 %collective-permute-start.1 = (bf16[4,7168]{1,0:T(4,128)(2,1)S(1)}, bf16[4,7168]{1,0:T(4,128)(2,1)S(1)}, u32[]{:S(2)}, u32[]{:S(2)}) collective-permute-start(bf16[4,7168]{1,0:T(4,128)(2,1)S(1)} %fusion.5), channel_id=1, source_target_pairs={{0,32},{32,64},{64,96},{96,128},{128,160},{160,192},{192,224},{224... | collective-permute-start | bytes 172040 | tf_op jit(solution)/shard_map/ppermute | solution.py:258

commit v10 on v9

--- a/solution.py
+++ b/solution.py
@@ -129,6 +129,89 @@
             bytes_accessed=3 * model_dim * hidden * 2 + 2 * rows * model_dim * 2,
         ),
     )(x, gate_mat, up_mat, down_mat)
+
+
+def pack_dispatch_kernel(count, normed_ref, placer_ref, y_ref, send_buf, send_sem, recv_sem, own_sem):
+    me = lax.axis_index("expert")
+    seg = lax.axis_index("segment")
+    slots = y_ref.shape[1]
+
+    barrier = pltpu.get_barrier_semaphore()
+
+    def greet(d, carry):
+        pl.semaphore_signal(
+            barrier, inc=1, device_id=(seg, lax.rem(me + d, count)),
+            device_id_type=pl.DeviceIdType.MESH,
+        )
+        return carry
+
+    lax.fori_loop(1, count, greet, 0)
+
+    send_buf[...] = jnp.dot(
+        placer_ref[...], normed_ref[...], preferred_element_type=jnp.float32
+    ).astype(send_buf.dtype)
+
+    pl.semaphore_wait(barrier, count - 1)
+
+    def rows_of(peer):
+        return send_buf.at[pl.ds((peer // GROUP) * slots, slots)]
+
+    own = pltpu.make_async_copy(rows_of(me), y_ref.at[me], own_sem)
+    own.start()
+
+    def outgoing(peer):
+        return pltpu.make_async_remote_copy(
+            src_ref=rows_of(peer),
+            dst_ref=y_ref.at[me],
+            send_sem=send_sem.at[peer],
+            recv_sem=recv_sem.at[me],
+            device_id=(seg, peer),
+            device_id_type=pl.DeviceIdType.MESH,
+        )
+
+    def incoming(peer):
+        return pltpu.make_async_remote_copy(
+            src_ref=rows_of(me),
+            dst_ref=y_ref.at[peer],
+            send_sem=send_sem.at[peer],
+            recv_sem=recv_sem.at[peer],
+            device_id=(seg, peer),
+            device_id_type=pl.DeviceIdType.MESH,
+        )
+
+    def send(d, carry):
+        outgoing(lax.rem(me + d, count)).start()
+        return carry
+
+    lax.fori_loop(1, count, send, 0)
+
+    def finish(d, carry):
+        outgoing(lax.rem(me + d, count)).wait_send()
+        incoming(lax.rem(me + count - d, count)).wait_recv()
+        return carry
+
+    lax.fori_loop(1, count, finish, 0)
+    own.wait()
+
+
+def pack_dispatch(normed, placer_rows, count, slots, collective_id):
+    model_dim = normed.shape[1]
+    return pl.pallas_call(
+        functools.partial(pack_dispatch_kernel, count),
+        out_shape=jax.ShapeDtypeStruct((count, slots, model_dim), normed.dtype),
+        in_specs=[
+            pl.BlockSpec(memory_space=pltpu.VMEM),
+            pl.BlockSpec(memory_space=pltpu.VMEM),
+        ],
+        out_specs=pl.BlockSpec(memory_space=pl.ANY),
+        scratch_shapes=[
+            pltpu.VMEM((placer_rows.shape[0], model_dim), normed.dtype),
+            pltpu.SemaphoreType.DMA((count,)),
+            pltpu.SemaphoreType.DMA((count,)),
+            pltpu.SemaphoreType.DMA,
+        ],
+        compiler_params=pltpu.CompilerParams(collective_id=collective_id, has_side_effects=True),
+    )(normed, placer_rows)
 
 
 def ffn_combine_kernel(count, steps, chunk, x_hbm, g_hbm, u_hbm, d_hbm, y_ref, terms_ref,
@@ -289,13 +372,10 @@
         inv_rms = lax.rsqrt(jnp.mean(current_f * current_f, axis=1, keepdims=True) + 1e-06)
         normed = (current_f * inv_rms * gain_row).astype(jnp.bfloat16)
 
-        packed = jnp.einsum(
-            "jcr,rd->jcd", placer_f, normed, preferred_element_type=jnp.float32
-        ).astype(jnp.bfloat16)
         packed_weight = jnp.sum(
             jnp.where(placer, dense_weight.T[:, None, :], jnp.float32(0.0)), axis=2
         )
-        got = exchange(packed, owners, 0)
+        got = pack_dispatch(normed, placer_f.reshape(experts * capacity, -1), owners, capacity, 0)
         back = ffn_combine(got, gate_mat, up_mat, down_mat, 1)
         slot_weight = jnp.where(placer, packed_weight[:, :, None], jnp.float32(0.0))
         back_weight = slot_weight[owner_expert].astype(jnp.bfloat16)

time: 148 us -> 150 us (1.014)
  other arithmetic: 2.34 us -> 5.25 us
  local copies, waits for them, and re-layouts: 5.12 us -> 3.41 us
    convert_element_type x0 -> x3, other arithmetic: none -> 2.93 us  [the longest x2 2.26 us: on_device(): normed = (current_f * inv_rms * gain_row).astype(jnp.bfloat16)]
    dot_general x2 -> x0, local copies, waits for them, and re-layouts: 1.86 us -> none  [on_device(): jnp.einsum('jcr,rd->jcd', placer_f, normed, preferred_element_type=jnp.fl...]
where the time goes in v10:
time: 150 us; the launch traced here: 149 us
  Pallas kernels  128 us (85%)
  waiting for transfers between devices  8.72 us (6%)
  other arithmetic  5.25 us (4%)
  local copies, waits for them, and re-layouts  3.41 us (2%)
  matrix products  2.96 us (2%)
    pallas_call x2, Pallas kernels, ffn_combine(): pl.pallas_call(functools.partial(ffn_combine_kernel, count, steps, chunk)...  68.7 us
    pallas_call x2, Pallas kernels, pack_dispatch(): pl.pallas_call(functools.partial(pack_dispatch_kernel, count), out_shape=...  59.6 us
    ppermute x2, waiting for transfers between devices, shifted(): return lax.ppermute(value, axis, pairs)  8.72 us
  transfers between devices with their start and end apart: 2, of which 2 were waited for; matrix products, arithmetic and copies ran while one was open for 1% of the time, Pallas kernels for 0%

profile of v10, /device:TPU:32, one launch (start us, length us, event | category | flops | bytes accessed | tf_op | source)
XLA Modules:
  0.0 148.8 jit_solution(4336111832009054168)
XLA Ops:
  0.0 1.0 fusion.13
  1.0 0.7 slice_bitcast_fusion
  1.8 0.1 copy.58
  1.9 0.1 copy.65
  2.3 0.7 bitcast_convert_fusion
  3.3 0.1 fusion.6
  3.4 0.6 gather_fusion
  4.0 0.1 copy.61
  4.1 1.5 %fusion.15.normed_ref = bf16[4,7168]{1,0:T(4,128)(2,1)} fusion(bf16[1,4,7168]{2,1,0:T(4,128)(2,1)} %param.7, f32[7168]{0:T(1024)} %bitcast.52, f32[4]{0:T(128)S(1)} %add_rsqrt_fusion.1), kind=kLoop, calls=%fused_computation.23 | loop fusion | flops 114688 | bytes 143376 | tf_op jit(solution)/shard_map/convert_element_type | solution.py:373
  5.6 0.7 and_convert_fusion
  6.3 31.7 %shard_map.73.x_hbm = bf16[32,2,7168]{2,1,0:T(2,128)(2,1)} custom-call(bf16[4,7168]{1,0:T(4,128)(2,1)} %fusion.15.normed_ref, bf16[16,4]{1,0:T(8,128)(2,1)} %get-tuple-element.14.placer_ref), custom_call_target="tpu_custom_call" | custom-call | tf_op jit(solution)/shard_map/pallas_call | solution.py:199
  38.0 34.2 %shard_map.74 = (bf16[32,2,7168]{2,1,0:T(2,128)(2,1)}, bf16[32,2,7168]{2,1,0:T(2,128)(2,1)}) custom-call(bf16[32,2,7168]{2,1,0:T(2,128)(2,1)} %shard_map.73.x_hbm, bf16[7168,256]{1,0:T(8,128)(2,1)} %bitcast.46, bf16[7168,256]{1,0:T(8,128)(2,1)} %bitcast.48, bf16[256,7168]{1,0:T(8,128)(2,1)} %bitcast.50), custom_call_target="tpu_custom_call" | custom-call | tf_op jit(solution)/shard_map/pallas_call | solution.py:317
  72.2 1.5 fusion.4
  73.8 0.1 fusion.7
  73.9 0.6 gather_fusion.1
  74.5 0.1 copy.68
  74.6 3.9 %collective-permute-done = bf16[4,7168]{1,0:T(4,128)(2,1)S(1)} collective-permute-done((bf16[4,7168]{1,0:T(4,128)(2,1)S(1)}, bf16[4,7168]{1,0:T(4,128)(2,1)S(1)}, u32[]{:S(2)}, u32[]{:S(2)}) %collective-permute-start) | collective-permute-done | bytes 57376 | tf_op jit(solution)/shard_map/ppermute | solution.py:341
  78.6 0.2 fusion.10
  78.7 0.7 fusion.12.normed_ref
  79.5 27.9 %shard_map.75.x_hbm = bf16[32,2,7168]{2,1,0:T(2,128)(2,1)} custom-call(bf16[4,7168]{1,0:T(4,128)(2,1)} %fusion.12.normed_ref, bf16[16,4]{1,0:T(8,128)(2,1)} %get-tuple-element.13.placer_ref), custom_call_target="tpu_custom_call" | custom-call | tf_op jit(solution)/shard_map/pallas_call | solution.py:199
  107.4 34.5 %shard_map.76 = (bf16[32,2,7168]{2,1,0:T(2,128)(2,1)}, bf16[32,2,7168]{2,1,0:T(2,128)(2,1)}) custom-call(bf16[32,2,7168]{2,1,0:T(2,128)(2,1)} %shard_map.75.x_hbm, bf16[7168,256]{1,0:T(8,128)(2,1)} %bitcast.47, bf16[7168,256]{1,0:T(8,128)(2,1)} %bitcast.49, bf16[256,7168]{1,0:T(8,128)(2,1)} %bitcast.51), custom_call_target="tpu_custom_call" | custom-call | tf_op jit(solution)/shard_map/pallas_call | solution.py:317
  141.9 1.5 fusion.5
  143.4 4.8 %collective-permute-done.1 = bf16[4,7168]{1,0:T(4,128)(2,1)S(1)} collective-permute-done((bf16[4,7168]{1,0:T(4,128)(2,1)S(1)}, bf16[4,7168]{1,0:T(4,128)(2,1)S(1)}, u32[]{:S(2)}, u32[]{:S(2)}) %collective-permute-start.1) | collective-permute-done | bytes 57376 | tf_op jit(solution)/shard_map/ppermute | solution.py:341
  148.2 0.6 copy.79
  (30 shorter events, 0.8 us)
Async XLA Ops:
  38.0 34.3 %copy-start = (bf16[1,4,7168]{2,1,0:T(4,128)(2,1)S(1)}, bf16[1,4,7168]{2,1,0:T(4,128)(2,1)}, u32[]{:S(2)}) copy-start(bf16[1,4,7168]{2,1,0:T(4,128)(2,1)} %param.7) | copy-start | bytes 172036
  38.0 40.8 %copy-start.1 = (f32[1,7168]{1,0:T(1,128)S(1)}, f32[1,7168]{1,0:T(1,128)}, u32[]{:S(2)}) copy-start(f32[1,7168]{1,0:T(1,128)} %param.10) | copy-start | bytes 86020
  73.7 4.8 %collective-permute-start = (bf16[4,7168]{1,0:T(4,128)(2,1)S(1)}, bf16[4,7168]{1,0:T(4,128)(2,1)S(1)}, u32[]{:S(2)}, u32[]{:S(2)}) collective-permute-start(bf16[4,7168]{1,0:T(4,128)(2,1)S(1)} %fusion.4), channel_id=1, source_target_pairs={{0,32},{32,64},{64,96},{96,128},{128,160},{160,192},{192,224},{224... | collective-permute-start | bytes 172040 | tf_op jit(solution)/shard_map/ppermute | solution.py:341
  143.4 4.8 %collective-permute-start.1 = (bf16[4,7168]{1,0:T(4,128)(2,1)S(1)}, bf16[4,7168]{1,0:T(4,128)(2,1)S(1)}, u32[]{:S(2)}, u32[]{:S(2)}) collective-permute-start(bf16[4,7168]{1,0:T(4,128)(2,1)S(1)} %fusion.5), channel_id=1, source_target_pairs={{0,32},{32,64},{64,96},{96,128},{128,160},{160,192},{192,224},{224... | collective-permute-start | bytes 172040 | tf_op jit(solution)/shard_map/ppermute | solution.py:341

commit v11 on v9

--- a/solution.py
+++ b/solution.py
@@ -132,7 +132,7 @@
 
 
 def ffn_combine_kernel(count, steps, chunk, x_hbm, g_hbm, u_hbm, d_hbm, y_ref, terms_ref,
-                       acc_g, acc_u, inner, send_sem, recv_sem, own_sem):
+                       acc_g, acc_u, inner, down_v, send_sem, recv_sem, own_sem, down_sem):
     me = lax.axis_index("expert")
     seg = lax.axis_index("segment")
     sources, slots = x_hbm.shape[0], x_hbm.shape[1]
@@ -149,6 +149,9 @@
         return carry
 
     lax.fori_loop(1, count, greet, 0)
+
+    down_copy = pltpu.make_async_copy(d_hbm, down_v, down_sem)
+    down_copy.start()
 
     acc_g[...] = jnp.zeros_like(acc_g)
     acc_u[...] = jnp.zeros_like(acc_u)
@@ -173,18 +176,19 @@
         g = acc_g[c]
         inner[c] = (g / (1.0 + jnp.exp(-g)) * acc_u[c]).astype(jnp.bfloat16)
 
-    def down(d_v, o_v):
+    down_copy.wait()
+
+    def down(o_v):
         for c in range(slots):
             o_v[:, c, :] = jnp.dot(
-                inner[c], d_v[...], preferred_element_type=jnp.float32
+                inner[c], down_v[...], preferred_element_type=jnp.float32
             ).astype(o_v.dtype)
 
     pltpu.emit_pipeline(
         down,
         grid=(1,),
-        in_specs=[pl.BlockSpec((hidden, model_dim), lambda k: (0, 0))],
         out_specs=[pl.BlockSpec((sources, slots, model_dim), lambda k: (0, 0, 0))],
-    )(d_hbm, terms_ref)
+    )(terms_ref)
 
     pl.semaphore_wait(barrier, count - 1)
 
@@ -243,8 +247,10 @@
             pltpu.VMEM((slots, count, hidden), jnp.float32),
             pltpu.VMEM((slots, count, hidden), jnp.float32),
             pltpu.VMEM((slots, count, hidden), jnp.bfloat16),
+            pltpu.VMEM((hidden, model_dim), down_mat.dtype),
             pltpu.SemaphoreType.DMA((count,)),
             pltpu.SemaphoreType.DMA((count,)),
+            pltpu.SemaphoreType.DMA,
             pltpu.SemaphoreType.DMA,
         ],
         compiler_params=pltpu.CompilerParams(collective_id=collective_id, has_side_effects=True),
@@ -298,7 +304,9 @@
         got = exchange(packed, owners, 0)
         back = ffn_combine(got, gate_mat, up_mat, down_mat, 1)
         slot_weight = jnp.where(placer, packed_weight[:, :, None], jnp.float32(0.0))
-        back_weight = slot_weight[owner_expert].astype(jnp.bfloat16)
+        back_weight = jnp.broadcast_to(
+            slot_weight[:, None], (experts, GROUP) + slot_weight.shape[1:]
+        ).reshape((owners,) + slot_weight.shape[1:]).astype(jnp.bfloat16)
         summed = jnp.einsum(
             "ocr,ocd->rd", back_weight, back, preferred_element_type=jnp.float32
         )

time: 148 us -> 145 us (0.980)
  Pallas kernels: 127 us -> 125 us
  local copies, waits for them, and re-layouts: 5.12 us -> 3.53 us
    pallas_call x2, Pallas kernels: 68.8 us -> 66.9 us  [ffn_combine(): pl.pallas_call(functools.partial(ffn_combine_kernel, count, steps, chunk)...]
  transfers between devices with their start and end apart: 2 -> 2, of which waited for: 2 -> 2; matrix products, arithmetic and copies ran while one was open for 1% -> 0% of each run, Pallas kernels for 0% -> 0%
where the time goes in v11:
time: 145 us
  Pallas kernels  125 us (86%)
  waiting for transfers between devices  9.34 us (6%)
  matrix products  4.32 us (3%)
  local copies, waits for them, and re-layouts  3.53 us (2%)
  other arithmetic  2.19 us (2%)
    pallas_call x2, Pallas kernels, ffn_combine(): pl.pallas_call(functools.partial(ffn_combine_kernel, count, steps, chunk)...  66.9 us
    pallas_call x2, Pallas kernels, exchange(): pl.pallas_call(functools.partial(exchange_kernel, count, spread), out_sha...  58.4 us
    ppermute x2, waiting for transfers between devices, shifted(): return lax.ppermute(value, axis, pairs)  9.34 us
    dot_general x2, matrix products, on_device(): jnp.einsum('ocr,ocd->rd', back_weight, back, preferred_element_type=jnp.f...  2.96 us
  transfers between devices with their start and end apart: 2, of which 2 were waited for; matrix products, arithmetic and copies ran while one was open for 0% of the time, Pallas kernels for 0%

profile of v11, /device:TPU:32, one launch (start us, length us, event | category | flops | bytes accessed | tf_op | source)
XLA Modules:
  0.0 144.8 jit_solution(12646190548429228528)
XLA Ops:
  0.0 0.7 slice_bitcast_fusion.1
  0.7 0.7 bitcast_convert_fusion.1
  1.4 0.1 fusion.23
  1.5 0.1 select_reduce_fusion.1
  1.6 0.1 broadcast_in_dim.86
  1.7 0.1 convert_element_type.77
  1.8 1.0 fusion.9
  2.8 1.1 fusion.13
  3.9 0.9 copy.31.x_ref
  4.8 31.1 %shard_map.73.x_hbm = bf16[32,2,7168]{2,1,0:T(2,128)(2,1)} custom-call(bf16[8,2,7168]{2,1,0:T(2,128)(2,1)} %copy.31.x_ref), custom_call_target="tpu_custom_call" | custom-call | tf_op jit(solution)/shard_map/pallas_call | solution.py:69
  36.0 33.3 %shard_map.74 = (bf16[32,2,7168]{2,1,0:T(2,128)(2,1)}, bf16[32,2,7168]{2,1,0:T(2,128)(2,1)}) custom-call(bf16[32,2,7168]{2,1,0:T(2,128)(2,1)} %shard_map.73.x_hbm, bf16[7168,256]{1,0:T(8,128)(2,1)} %bitcast.61, bf16[7168,256]{1,0:T(8,128)(2,1)} %bitcast.63, bf16[256,7168]{1,0:T(8,128)(2,1)} %bitcast.65), custom_call_target="tpu_custom_call" | custom-call | tf_op jit(solution)/shard_map/pallas_call | solution.py:238
  69.3 1.5 %fusion.2 = bf16[4,7168]{1,0:T(4,128)(2,1)S(1)} fusion(bf16[32,2,4]{0,2,1:T(4,128)(2,1)S(1)} %convert_element_type.77, bf16[32,2,7168]{2,1,0:T(2,128)(2,1)} %get-tuple-element.7, bf16[1,4,7168]{2,1,0:T(4,128)(2,1)S(1)} %copy-done), kind=kOutput, calls=%fused_computation.4 | convolution fusion | flops 3756032 | bytes 1032704 | tf_op jit(solution)/shard_map/ocr,ocd->rd/dot_general | solution.py:310
  70.7 0.0 collective-permute-start
  70.9 0.1 broadcast_in_dim.90
  70.9 0.1 convert_element_type.86
  71.0 4.5 %collective-permute-done = bf16[4,7168]{1,0:T(4,128)(2,1)S(1)} collective-permute-done((bf16[4,7168]{1,0:T(4,128)(2,1)S(1)}, bf16[4,7168]{1,0:T(4,128)(2,1)S(1)}, u32[]{:S(2)}, u32[]{:S(2)}) %collective-permute-start) | collective-permute-done | bytes 57376 | tf_op jit(solution)/shard_map/ppermute | solution.py:264
  75.6 0.2 fusion.6
  75.8 0.3 fusion.16
  76.0 0.9 copy.30.x_ref
  77.0 27.3 %shard_map.75.x_hbm = bf16[32,2,7168]{2,1,0:T(2,128)(2,1)} custom-call(bf16[8,2,7168]{2,1,0:T(2,128)(2,1)} %copy.30.x_ref), custom_call_target="tpu_custom_call" | custom-call | tf_op jit(solution)/shard_map/pallas_call | solution.py:69
  104.3 33.6 %shard_map.76 = (bf16[32,2,7168]{2,1,0:T(2,128)(2,1)}, bf16[32,2,7168]{2,1,0:T(2,128)(2,1)}) custom-call(bf16[32,2,7168]{2,1,0:T(2,128)(2,1)} %shard_map.75.x_hbm, bf16[7168,256]{1,0:T(8,128)(2,1)} %bitcast.62, bf16[7168,256]{1,0:T(8,128)(2,1)} %bitcast.64, bf16[256,7168]{1,0:T(8,128)(2,1)} %bitcast.66), custom_call_target="tpu_custom_call" | custom-call | tf_op jit(solution)/shard_map/pallas_call | solution.py:238
  137.9 1.5 %fusion.3 = bf16[4,7168]{1,0:T(4,128)(2,1)S(1)} fusion(bf16[32,2,4]{0,2,1:T(4,128)(2,1)S(1)} %convert_element_type.86, bf16[32,2,7168]{2,1,0:T(2,128)(2,1)} %get-tuple-element.8, bf16[4,7168]{1,0:T(4,128)(2,1)S(1)} %collective-permute-done), kind=kOutput, calls=%fused_computation.5 | convolution fusion | flops 3756032 | bytes 1032704 | tf_op jit(solution)/shard_map/ocr,ocd->rd/dot_general | solution.py:310
  139.4 4.8 %collective-permute-done.1 = bf16[4,7168]{1,0:T(4,128)(2,1)S(1)} collective-permute-done((bf16[4,7168]{1,0:T(4,128)(2,1)S(1)}, bf16[4,7168]{1,0:T(4,128)(2,1)S(1)}, u32[]{:S(2)}, u32[]{:S(2)}) %collective-permute-start.1) | collective-permute-done | bytes 57376 | tf_op jit(solution)/shard_map/ppermute | solution.py:264
  144.2 0.6 copy.33
  (17 shorter events, 0.2 us)
Async XLA Ops:
  35.9 33.3 %copy-start = (bf16[1,4,7168]{2,1,0:T(4,128)(2,1)S(1)}, bf16[1,4,7168]{2,1,0:T(4,128)(2,1)}, u32[]{:S(2)}) copy-start(bf16[1,4,7168]{2,1,0:T(4,128)(2,1)} %param.7) | copy-start | bytes 172036
  35.9 39.8 %copy-start.1 = (f32[1,7168]{1,0:T(1,128)S(1)}, f32[1,7168]{1,0:T(1,128)}, u32[]{:S(2)}) copy-start(f32[1,7168]{1,0:T(1,128)} %param.10) | copy-start | bytes 86020
  70.7 4.8 %collective-permute-start = (bf16[4,7168]{1,0:T(4,128)(2,1)S(1)}, bf16[4,7168]{1,0:T(4,128)(2,1)S(1)}, u32[]{:S(2)}, u32[]{:S(2)}) collective-permute-start(bf16[4,7168]{1,0:T(4,128)(2,1)S(1)} %fusion.2), channel_id=1, source_target_pairs={{0,32},{32,64},{64,96},{96,128},{128,160},{160,192},{192,224},{224... | collective-permute-start | bytes 172040 | tf_op jit(solution)/shard_map/ppermute | solution.py:264
  139.4 4.8 %collective-permute-start.1 = (bf16[4,7168]{1,0:T(4,128)(2,1)S(1)}, bf16[4,7168]{1,0:T(4,128)(2,1)S(1)}, u32[]{:S(2)}, u32[]{:S(2)}) collective-permute-start(bf16[4,7168]{1,0:T(4,128)(2,1)S(1)} %fusion.3), channel_id=1, source_target_pairs={{0,32},{32,64},{64,96},{96,128},{128,160},{160,192},{192,224},{224... | collective-permute-start | bytes 172040 | tf_op jit(solution)/shard_map/ppermute | solution.py:264

commit v12 on v11

--- a/solution.py
+++ b/solution.py
@@ -177,56 +177,63 @@
         inner[c] = (g / (1.0 + jnp.exp(-g)) * acc_u[c]).astype(jnp.bfloat16)
 
     down_copy.wait()
-
-    def down(o_v):
-        for c in range(slots):
-            o_v[:, c, :] = jnp.dot(
-                inner[c], down_v[...], preferred_element_type=jnp.float32
-            ).astype(o_v.dtype)
-
-    pltpu.emit_pipeline(
-        down,
-        grid=(1,),
-        out_specs=[pl.BlockSpec((sources, slots, model_dim), lambda k: (0, 0, 0))],
-    )(terms_ref)
-
     pl.semaphore_wait(barrier, count - 1)
+
+    parts = 2
+    width = model_dim // parts
+
+    def columns(part):
+        return pl.ds(part * width, width)
+
+    def outgoing(peer, part):
+        return pltpu.make_async_remote_copy(
+            src_ref=terms_ref.at[peer, :, columns(part)],
+            dst_ref=y_ref.at[me, :, columns(part)],
+            send_sem=send_sem.at[part, peer],
+            recv_sem=recv_sem.at[part, me],
+            device_id=(seg, peer),
+            device_id_type=pl.DeviceIdType.MESH,
+        )
+
+    def incoming(peer, part):
+        return pltpu.make_async_remote_copy(
+            src_ref=terms_ref.at[me, :, columns(part)],
+            dst_ref=y_ref.at[peer, :, columns(part)],
+            send_sem=send_sem.at[part, peer],
+            recv_sem=recv_sem.at[part, peer],
+            device_id=(seg, peer),
+            device_id_type=pl.DeviceIdType.MESH,
+        )
+
+    for part in range(parts):
+        def down(o_v, part=part):
+            for c in range(slots):
+                o_v[:, c, :] = jnp.dot(
+                    inner[c], down_v[:, columns(part)], preferred_element_type=jnp.float32
+                ).astype(o_v.dtype)
+
+        pltpu.emit_pipeline(
+            down,
+            grid=(1,),
+            out_specs=[pl.BlockSpec((sources, slots, width), lambda k, part=part: (0, 0, part))],
+        )(terms_ref)
+
+        def send(d, carry, part=part):
+            outgoing(lax.rem(me + d, count), part).start()
+            return carry
+
+        lax.fori_loop(1, count, send, 0)
 
     own = pltpu.make_async_copy(terms_ref.at[me], y_ref.at[me], own_sem)
     own.start()
 
-    def outgoing(peer):
-        return pltpu.make_async_remote_copy(
-            src_ref=terms_ref.at[peer],
-            dst_ref=y_ref.at[me],
-            send_sem=send_sem.at[peer],
-            recv_sem=recv_sem.at[me],
-            device_id=(seg, peer),
-            device_id_type=pl.DeviceIdType.MESH,
-        )
-
-    def incoming(peer):
-        return pltpu.make_async_remote_copy(
-            src_ref=terms_ref.at[me],
-            dst_ref=y_ref.at[peer],
-            send_sem=send_sem.at[peer],
-            recv_sem=recv_sem.at[peer],
-            device_id=(seg, peer),
-            device_id_type=pl.DeviceIdType.MESH,
-        )
-
-    def send(d, carry):
-        outgoing(lax.rem(me + d, count)).start()
-        return carry
-
-    lax.fori_loop(1, count, send, 0)
-
-    def finish(d, carry):
-        outgoing(lax.rem(me + d, count)).wait_send()
-        incoming(lax.rem(me + count - d, count)).wait_recv()
-        return carry
-
-    lax.fori_loop(1, count, finish, 0)
+    for part in range(parts):
+        def finish(d, carry, part=part):
+            outgoing(lax.rem(me + d, count), part).wait_send()
+            incoming(lax.rem(me + count - d, count), part).wait_recv()
+            return carry
+
+        lax.fori_loop(1, count, finish, 0)
     own.wait()
 
 
@@ -248,8 +255,8 @@
             pltpu.VMEM((slots, count, hidden), jnp.float32),
             pltpu.VMEM((slots, count, hidden), jnp.bfloat16),
             pltpu.VMEM((hidden, model_dim), down_mat.dtype),
-            pltpu.SemaphoreType.DMA((count,)),
-            pltpu.SemaphoreType.DMA((count,)),
+            pltpu.SemaphoreType.DMA((2, count)),
+            pltpu.SemaphoreType.DMA((2, count)),
             pltpu.SemaphoreType.DMA,
             pltpu.SemaphoreType.DMA,
         ],

time: 145 us -> 146 us (level); the launches traced: 145 us -> 144 us
  no operation moved by 1% of the time
where the time goes in v12:
time: 146 us; the launch traced here: 144 us
  Pallas kernels  124 us (85%)
  waiting for transfers between devices  9.34 us (6%)
  matrix products  4.32 us (3%)
  local copies, waits for them, and re-layouts  3.53 us (2%)
  other arithmetic  2.19 us (2%)
    pallas_call x2, Pallas kernels, ffn_combine(): pl.pallas_call(functools.partial(ffn_combine_kernel, count, steps, chunk)...  65.6 us
    pallas_call x2, Pallas kernels, exchange(): pl.pallas_call(functools.partial(exchange_kernel, count, spread), out_sha...  58.4 us
    ppermute x2, waiting for transfers between devices, shifted(): return lax.ppermute(value, axis, pairs)  9.34 us
    dot_general x2, matrix products, on_device(): jnp.einsum('ocr,ocd->rd', back_weight, back, preferred_element_type=jnp.f...  2.96 us
  transfers between devices with their start and end apart: 2, of which 2 were waited for; matrix products, arithmetic and copies ran while one was open for 0% of the time, Pallas kernels for 0%

profile of v12, /device:TPU:32, one launch (start us, length us, event | category | flops | bytes accessed | tf_op | source)
XLA Modules:
  0.0 143.6 jit_solution(5617440308911063559)
XLA Ops:
  0.0 0.7 slice_bitcast_fusion.1
  0.7 0.7 bitcast_convert_fusion.1
  1.4 0.1 fusion.23
  1.5 0.1 select_reduce_fusion.1
  1.6 0.1 broadcast_in_dim.86
  1.7 0.1 convert_element_type.77
  1.8 1.0 fusion.9
  2.8 1.1 fusion.13
  3.9 0.9 copy.31.x_ref
  4.8 31.1 %shard_map.73.x_hbm = bf16[32,2,7168]{2,1,0:T(2,128)(2,1)} custom-call(bf16[8,2,7168]{2,1,0:T(2,128)(2,1)} %copy.31.x_ref), custom_call_target="tpu_custom_call" | custom-call | tf_op jit(solution)/shard_map/pallas_call | solution.py:69
  36.0 33.1 %shard_map.74 = (bf16[32,2,7168]{2,1,0:T(2,128)(2,1)}, bf16[32,2,7168]{2,1,0:T(2,128)(2,1)}) custom-call(bf16[32,2,7168]{2,1,0:T(2,128)(2,1)} %shard_map.73.x_hbm, bf16[7168,256]{1,0:T(8,128)(2,1)} %bitcast.61, bf16[7168,256]{1,0:T(8,128)(2,1)} %bitcast.63, bf16[256,7168]{1,0:T(8,128)(2,1)} %bitcast.65), custom_call_target="tpu_custom_call" | custom-call | tf_op jit(solution)/shard_map/pallas_call | solution.py:245
  69.1 1.5 %fusion.2 = bf16[4,7168]{1,0:T(4,128)(2,1)S(1)} fusion(bf16[32,2,4]{0,2,1:T(4,128)(2,1)S(1)} %convert_element_type.77, bf16[32,2,7168]{2,1,0:T(2,128)(2,1)} %get-tuple-element.7, bf16[1,4,7168]{2,1,0:T(4,128)(2,1)S(1)} %copy-done), kind=kOutput, calls=%fused_computation.4 | convolution fusion | flops 3756032 | bytes 1032704 | tf_op jit(solution)/shard_map/ocr,ocd->rd/dot_general | solution.py:317
  70.6 0.0 collective-permute-start
  70.7 0.1 broadcast_in_dim.90
  70.8 0.1 convert_element_type.86
  70.9 4.5 %collective-permute-done = bf16[4,7168]{1,0:T(4,128)(2,1)S(1)} collective-permute-done((bf16[4,7168]{1,0:T(4,128)(2,1)S(1)}, bf16[4,7168]{1,0:T(4,128)(2,1)S(1)}, u32[]{:S(2)}, u32[]{:S(2)}) %collective-permute-start) | collective-permute-done | bytes 57376 | tf_op jit(solution)/shard_map/ppermute | solution.py:271
  75.4 0.2 fusion.6
  75.6 0.3 fusion.16
  75.9 0.9 copy.30.x_ref
  76.8 27.3 %shard_map.75.x_hbm = bf16[32,2,7168]{2,1,0:T(2,128)(2,1)} custom-call(bf16[8,2,7168]{2,1,0:T(2,128)(2,1)} %copy.30.x_ref), custom_call_target="tpu_custom_call" | custom-call | tf_op jit(solution)/shard_map/pallas_call | solution.py:69
  104.1 32.5 %shard_map.76 = (bf16[32,2,7168]{2,1,0:T(2,128)(2,1)}, bf16[32,2,7168]{2,1,0:T(2,128)(2,1)}) custom-call(bf16[32,2,7168]{2,1,0:T(2,128)(2,1)} %shard_map.75.x_hbm, bf16[7168,256]{1,0:T(8,128)(2,1)} %bitcast.62, bf16[7168,256]{1,0:T(8,128)(2,1)} %bitcast.64, bf16[256,7168]{1,0:T(8,128)(2,1)} %bitcast.66), custom_call_target="tpu_custom_call" | custom-call | tf_op jit(solution)/shard_map/pallas_call | solution.py:245
  136.6 1.5 %fusion.3 = bf16[4,7168]{1,0:T(4,128)(2,1)S(1)} fusion(bf16[32,2,4]{0,2,1:T(4,128)(2,1)S(1)} %convert_element_type.86, bf16[32,2,7168]{2,1,0:T(2,128)(2,1)} %get-tuple-element.8, bf16[4,7168]{1,0:T(4,128)(2,1)S(1)} %collective-permute-done), kind=kOutput, calls=%fused_computation.5 | convolution fusion | flops 3756032 | bytes 1032704 | tf_op jit(solution)/shard_map/ocr,ocd->rd/dot_general | solution.py:317
  138.2 4.8 %collective-permute-done.1 = bf16[4,7168]{1,0:T(4,128)(2,1)S(1)} collective-permute-done((bf16[4,7168]{1,0:T(4,128)(2,1)S(1)}, bf16[4,7168]{1,0:T(4,128)(2,1)S(1)}, u32[]{:S(2)}, u32[]{:S(2)}) %collective-permute-start.1) | collective-permute-done | bytes 57376 | tf_op jit(solution)/shard_map/ppermute | solution.py:271
  143.0 0.6 copy.33
  (17 shorter events, 0.2 us)
Async XLA Ops:
  35.9 33.2 %copy-start = (bf16[1,4,7168]{2,1,0:T(4,128)(2,1)S(1)}, bf16[1,4,7168]{2,1,0:T(4,128)(2,1)}, u32[]{:S(2)}) copy-start(bf16[1,4,7168]{2,1,0:T(4,128)(2,1)} %param.7) | copy-start | bytes 172036
  35.9 39.7 %copy-start.1 = (f32[1,7168]{1,0:T(1,128)S(1)}, f32[1,7168]{1,0:T(1,128)}, u32[]{:S(2)}) copy-start(f32[1,7168]{1,0:T(1,128)} %param.10) | copy-start | bytes 86020
  70.6 4.8 %collective-permute-start = (bf16[4,7168]{1,0:T(4,128)(2,1)S(1)}, bf16[4,7168]{1,0:T(4,128)(2,1)S(1)}, u32[]{:S(2)}, u32[]{:S(2)}) collective-permute-start(bf16[4,7168]{1,0:T(4,128)(2,1)S(1)} %fusion.2), channel_id=1, source_target_pairs={{0,32},{32,64},{64,96},{96,128},{128,160},{160,192},{192,224},{224... | collective-permute-start | bytes 172040 | tf_op jit(solution)/shard_map/ppermute | solution.py:271
  138.1 4.8 %collective-permute-start.1 = (bf16[4,7168]{1,0:T(4,128)(2,1)S(1)}, bf16[4,7168]{1,0:T(4,128)(2,1)S(1)}, u32[]{:S(2)}, u32[]{:S(2)}) collective-permute-start(bf16[4,7168]{1,0:T(4,128)(2,1)S(1)} %fusion.3), channel_id=1, source_target_pairs={{0,32},{32,64},{64,96},{96,128},{128,160},{160,192},{192,224},{224... | collective-permute-start | bytes 172040 | tf_op jit(solution)/shard_map/ppermute | solution.py:271

commit v13 on v11

--- a/solution.py
+++ b/solution.py
@@ -131,10 +131,15 @@
     )(x, gate_mat, up_mat, down_mat)
 
 
-def ffn_combine_kernel(count, steps, chunk, x_hbm, g_hbm, u_hbm, d_hbm, y_ref, terms_ref,
-                       acc_g, acc_u, inner, down_v, send_sem, recv_sem, own_sem, down_sem):
+def ffn_combine_kernel(count, steps, chunk, x_hbm, g_hbm, u_hbm, d_hbm, h_ref, w_ref,
+                       y_ref, terms_ref, next_ref, stage_ref,
+                       acc_g, acc_u, inner, down_v, y_v, h_v,
+                       send_sem, recv_sem, own_sem, down_sem, y_sem, stage_sem, h_send_sem, h_recv_sem):
     me = lax.axis_index("expert")
     seg = lax.axis_index("segment")
+    sections = lax.axis_size("segment")
+    ahead = lax.rem(seg + 1, sections)
+    behind = lax.rem(seg + sections - 1, sections)
     sources, slots = x_hbm.shape[0], x_hbm.shape[1]
     hidden = g_hbm.shape[1]
     model_dim = x_hbm.shape[2]
@@ -149,6 +154,10 @@
         return carry
 
     lax.fori_loop(1, count, greet, 0)
+    for section in (ahead, behind):
+        pl.semaphore_signal(
+            barrier, inc=1, device_id=(section, me), device_id_type=pl.DeviceIdType.MESH
+        )
 
     down_copy = pltpu.make_async_copy(d_hbm, down_v, down_sem)
     down_copy.start()
@@ -190,7 +199,7 @@
         out_specs=[pl.BlockSpec((sources, slots, model_dim), lambda k: (0, 0, 0))],
     )(terms_ref)
 
-    pl.semaphore_wait(barrier, count - 1)
+    pl.semaphore_wait(barrier, count + 1)
 
     own = pltpu.make_async_copy(terms_ref.at[me], y_ref.at[me], own_sem)
     own.start()
@@ -229,34 +238,75 @@
     lax.fori_loop(1, count, finish, 0)
     own.wait()
 
-
-def ffn_combine(x, gate_mat, up_mat, down_mat, collective_id):
+    y_copy = pltpu.make_async_copy(y_ref, y_v, y_sem)
+    y_copy.start()
+    y_copy.wait()
+    for k in range(steps):
+        cols = pl.ds(k * chunk, chunk)
+        total = h_ref[:, cols].astype(jnp.float32)
+        for c in range(slots):
+            total = total + jnp.dot(w_ref[c], y_v[:, c, cols], preferred_element_type=jnp.float32)
+        h_v[:, cols] = total.astype(h_v.dtype)
+
+    stage = pltpu.make_async_copy(h_v, stage_ref, stage_sem)
+    stage.start()
+    stage.wait()
+    moved = pltpu.make_async_remote_copy(
+        src_ref=stage_ref,
+        dst_ref=next_ref,
+        send_sem=h_send_sem,
+        recv_sem=h_recv_sem,
+        device_id=(ahead, me),
+        device_id_type=pl.DeviceIdType.MESH,
+    )
+    moved.start()
+    moved.wait_send()
+    arrived = pltpu.make_async_remote_copy(
+        src_ref=stage_ref,
+        dst_ref=next_ref,
+        send_sem=h_send_sem,
+        recv_sem=h_recv_sem,
+        device_id=(behind, me),
+        device_id_type=pl.DeviceIdType.MESH,
+    )
+    arrived.wait_recv()
+
+
+def ffn_combine(x, gate_mat, up_mat, down_mat, h, weights, collective_id):
     count, slots, model_dim = x.shape
     hidden = gate_mat.shape[1]
     chunk = 1024
     steps = model_dim // chunk
-    back, _ = pl.pallas_call(
+    _, _, moved, _ = pl.pallas_call(
         functools.partial(ffn_combine_kernel, count, steps, chunk),
         out_shape=(
             jax.ShapeDtypeStruct(x.shape, jnp.bfloat16),
             jax.ShapeDtypeStruct(x.shape, jnp.bfloat16),
+            jax.ShapeDtypeStruct(h.shape, h.dtype),
+            jax.ShapeDtypeStruct(h.shape, h.dtype),
         ),
-        in_specs=[pl.BlockSpec(memory_space=pl.ANY)] * 4,
-        out_specs=(pl.BlockSpec(memory_space=pl.ANY), pl.BlockSpec(memory_space=pl.ANY)),
+        in_specs=[pl.BlockSpec(memory_space=pl.ANY)] * 4
+        + [pl.BlockSpec(memory_space=pltpu.VMEM)] * 2,
+        out_specs=tuple(pl.BlockSpec(memory_space=pl.ANY) for _ in range(4)),
         scratch_shapes=[
             pltpu.VMEM((slots, count, hidden), jnp.float32),
             pltpu.VMEM((slots, count, hidden), jnp.float32),
             pltpu.VMEM((slots, count, hidden), jnp.bfloat16),
             pltpu.VMEM((hidden, model_dim), down_mat.dtype),
+            pltpu.VMEM(x.shape, jnp.bfloat16),
+            pltpu.VMEM(h.shape, h.dtype),
             pltpu.SemaphoreType.DMA((count,)),
             pltpu.SemaphoreType.DMA((count,)),
             pltpu.SemaphoreType.DMA,
             pltpu.SemaphoreType.DMA,
+            pltpu.SemaphoreType.DMA,
+            pltpu.SemaphoreType.DMA,
+            pltpu.SemaphoreType.DMA,
+            pltpu.SemaphoreType.DMA,
         ],
         compiler_params=pltpu.CompilerParams(collective_id=collective_id, has_side_effects=True),
-    )(x, gate_mat, up_mat, down_mat)
-    return back
-
+    )(x, gate_mat, up_mat, down_mat, h, weights)
+    return moved
 
 def shifted(value, axis, steps):
     count = lax.axis_size(axis)
@@ -302,16 +352,11 @@
             jnp.where(placer, dense_weight.T[:, None, :], jnp.float32(0.0)), axis=2
         )
         got = exchange(packed, owners, 0)
-        back = ffn_combine(got, gate_mat, up_mat, down_mat, 1)
         slot_weight = jnp.where(placer, packed_weight[:, :, None], jnp.float32(0.0))
-        back_weight = jnp.broadcast_to(
-            slot_weight[:, None], (experts, GROUP) + slot_weight.shape[1:]
-        ).reshape((owners,) + slot_weight.shape[1:]).astype(jnp.bfloat16)
-        summed = jnp.einsum(
-            "ocr,ocd->rd", back_weight, back, preferred_element_type=jnp.float32
-        )
-        updated = (current_f + summed).astype(jnp.bfloat16)
-        current = shifted(updated, "segment", 1)
+        weights = jnp.broadcast_to(
+            slot_weight.transpose(1, 2, 0)[:, :, :, None], (capacity, row_dev, experts, GROUP)
+        ).reshape(capacity, row_dev, owners).astype(jnp.bfloat16)
+        current = ffn_combine(got, gate_mat, up_mat, down_mat, current, weights, 1 + step_no)
     return current[None]
 
 

time: 145 us -> 156 us (1.076); the launches traced: 145 us -> 153 us
  Pallas kernels: 125 us -> 143 us
  waiting for transfers between devices: 9.34 us -> 0 us
  matrix products: 4.32 us -> 2.19 us
  local copies, waits for them, and re-layouts: 3.53 us -> 5.5 us
    pallas_call x2, Pallas kernels: 66.9 us -> 84.3 us  [ffn_combine(): pl.pallas_call(functools.partial(ffn_combine_kernel, count, steps, chunk)...]
    ppermute x2 -> x0, waiting for transfers between devices: 9.34 us -> none  [shifted(): return lax.ppermute(value, axis, pairs)]
    dot_general x2 -> x0, matrix products: 2.96 us -> none  [on_device(): jnp.einsum('ocr,ocd->rd', back_weight, back, preferred_element_type=jnp.f...]
  transfers between devices with their start and end apart: 2 -> 0, of which waited for: 2 -> 0; matrix products, arithmetic and copies ran while one was open for 0% -> 0% of each run, Pallas kernels for 0% -> 0%
where the time goes in v13:
time: 156 us; the launch traced here: 153 us
  Pallas kernels  143 us (92%)
  local copies, waits for them, and re-layouts  5.5 us (4%)
  other arithmetic  3 us (2%)
  matrix products  2.19 us (1%)
    pallas_call x2, Pallas kernels, ffn_combine(): pl.pallas_call(functools.partial(ffn_combine_kernel, count, steps, chunk)...  84.3 us
    pallas_call x2, Pallas kernels, exchange(): pl.pallas_call(functools.partial(exchange_kernel, count, spread), out_sha...  58.3 us

profile of v13, /device:TPU:32, one launch (start us, length us, event | category | flops | bytes accessed | tf_op | source)
XLA Modules:
  0.0 153.3 jit_solution(4502873159756155711)
XLA Ops:
  0.0 1.0 fusion
  1.0 0.7 slice_bitcast_fusion.1
  1.7 0.1 fusion.16
  1.9 0.7 bitcast_convert_fusion
  2.6 0.1 select_reduce_fusion.1
  2.7 0.1 broadcast_in_dim.94
  2.8 0.7 convert_element_type.66.w_ref
  3.5 0.1 broadcast_in_dim.99
  3.5 0.6 convert_element_type.73.w_ref
  4.2 1.1 fusion.10
  5.3 0.9 copy.25.x_ref
  6.2 31.1 %shard_map.73.x_hbm = bf16[32,2,7168]{2,1,0:T(2,128)(2,1)} custom-call(bf16[8,2,7168]{2,1,0:T(2,128)(2,1)} %copy.25.x_ref), custom_call_target="tpu_custom_call" | custom-call | tf_op jit(solution)/shard_map/pallas_call | solution.py:69
  37.3 0.0 copy-start
  37.3 41.6 %shard_map.74 = (bf16[32,2,7168]{2,1,0:T(2,128)(2,1)}, bf16[32,2,7168]{2,1,0:T(2,128)(2,1)}, bf16[4,7168]{1,0:T(4,128)(2,1)}, bf16[4,7168]{1,0:T(4,128)(2,1)}) custom-call(bf16[32,2,7168]{2,1,0:T(2,128)(2,1)} %shard_map.73.x_hbm, bf16[7168,256]{1,0:T(8,128)(2,1)} %bitcast.41, bf16[7168,256]{1,0:T(8,128)(2,1)} %bitcast.43, bf16[256,7168]{1,0:T(8,128)(2,1)} %bitcast.45, ...), custom_call_target="tpu_custom_call" | custom-call | tf_op jit(solution)/shard_map/pallas_call | solution.py:280
  78.9 1.0 fusion.3
  79.9 0.0 copy-done
  79.9 1.1 fusion.7
  81.0 0.9 copy.24.x_ref
  82.0 27.2 %shard_map.75.x_hbm = bf16[32,2,7168]{2,1,0:T(2,128)(2,1)} custom-call(bf16[8,2,7168]{2,1,0:T(2,128)(2,1)} %copy.24.x_ref), custom_call_target="tpu_custom_call" | custom-call | tf_op jit(solution)/shard_map/pallas_call | solution.py:69
  109.2 42.7 %shard_map.76 = (bf16[32,2,7168]{2,1,0:T(2,128)(2,1)}, bf16[32,2,7168]{2,1,0:T(2,128)(2,1)}, bf16[4,7168]{1,0:T(4,128)(2,1)}, bf16[4,7168]{1,0:T(4,128)(2,1)}) custom-call(bf16[32,2,7168]{2,1,0:T(2,128)(2,1)} %shard_map.75.x_hbm, bf16[7168,256]{1,0:T(8,128)(2,1)} %bitcast.42, bf16[7168,256]{1,0:T(8,128)(2,1)} %bitcast.44, bf16[256,7168]{1,0:T(8,128)(2,1)} %bitcast.46, ...), custom_call_target="tpu_custom_call" | custom-call | tf_op jit(solution)/shard_map/pallas_call | solution.py:280
  151.9 1.5 copy.27
  (12 shorter events, 0.2 us)
Async XLA Ops:
  37.3 42.6 %copy-start = (f32[1,7168]{1,0:T(1,128)S(1)}, f32[1,7168]{1,0:T(1,128)}, u32[]{:S(2)}) copy-start(f32[1,7168]{1,0:T(1,128)} %param.10) | copy-start | bytes 86020

commit v14 on v11

--- a/solution.py
+++ b/solution.py
@@ -233,7 +233,7 @@
 def ffn_combine(x, gate_mat, up_mat, down_mat, collective_id):
     count, slots, model_dim = x.shape
     hidden = gate_mat.shape[1]
-    chunk = 1024
+    chunk = 1792
     steps = model_dim // chunk
     back, _ = pl.pallas_call(
         functools.partial(ffn_combine_kernel, count, steps, chunk),

time: 145 us -> 142 us (0.979)
  Pallas kernels: 125 us -> 122 us
    pallas_call x2, Pallas kernels: 66.9 us -> 63.9 us  [ffn_combine(): pl.pallas_call(functools.partial(ffn_combine_kernel, count, steps, chunk)...]
where the time goes in v14:
time: 142 us
  Pallas kernels  122 us (86%)
  waiting for transfers between devices  9.34 us (7%)
  matrix products  4.32 us (3%)
  local copies, waits for them, and re-layouts  3.53 us (2%)
  other arithmetic  2.19 us (2%)
    pallas_call x2, Pallas kernels, ffn_combine(): pl.pallas_call(functools.partial(ffn_combine_kernel, count, steps, chunk)...  63.9 us
    pallas_call x2, Pallas kernels, exchange(): pl.pallas_call(functools.partial(exchange_kernel, count, spread), out_sha...  58.4 us
    ppermute x2, waiting for transfers between devices, shifted(): return lax.ppermute(value, axis, pairs)  9.34 us
    dot_general x2, matrix products, on_device(): jnp.einsum('ocr,ocd->rd', back_weight, back, preferred_element_type=jnp.f...  2.96 us
  transfers between devices with their start and end apart: 2, of which 2 were waited for; matrix products, arithmetic and copies ran while one was open for 0% of the time, Pallas kernels for 0%

profile of v14, /device:TPU:32, one launch (start us, length us, event | category | flops | bytes accessed | tf_op | source)
XLA Modules:
  0.0 141.9 jit_solution(3126006664106661239)
XLA Ops:
  0.0 0.7 slice_bitcast_fusion.1
  0.7 0.7 bitcast_convert_fusion.1
  1.4 0.1 fusion.23
  1.5 0.1 select_reduce_fusion.1
  1.6 0.1 broadcast_in_dim.86
  1.7 0.1 convert_element_type.77
  1.8 1.0 fusion.9
  2.8 1.1 fusion.13
  3.9 0.9 copy.31.x_ref
  4.8 31.1 %shard_map.73.x_hbm = bf16[32,2,7168]{2,1,0:T(2,128)(2,1)} custom-call(bf16[8,2,7168]{2,1,0:T(2,128)(2,1)} %copy.31.x_ref), custom_call_target="tpu_custom_call" | custom-call | tf_op jit(solution)/shard_map/pallas_call | solution.py:69
  36.0 31.8 %shard_map.74 = (bf16[32,2,7168]{2,1,0:T(2,128)(2,1)}, bf16[32,2,7168]{2,1,0:T(2,128)(2,1)}) custom-call(bf16[32,2,7168]{2,1,0:T(2,128)(2,1)} %shard_map.73.x_hbm, bf16[7168,256]{1,0:T(8,128)(2,1)} %bitcast.61, bf16[7168,256]{1,0:T(8,128)(2,1)} %bitcast.63, bf16[256,7168]{1,0:T(8,128)(2,1)} %bitcast.65), custom_call_target="tpu_custom_call" | custom-call | tf_op jit(solution)/shard_map/pallas_call | solution.py:238
  67.8 1.5 %fusion.2 = bf16[4,7168]{1,0:T(4,128)(2,1)S(1)} fusion(bf16[32,2,4]{0,2,1:T(4,128)(2,1)S(1)} %convert_element_type.77, bf16[32,2,7168]{2,1,0:T(2,128)(2,1)} %get-tuple-element.7, bf16[1,4,7168]{2,1,0:T(4,128)(2,1)S(1)} %copy-done), kind=kOutput, calls=%fused_computation.4 | convolution fusion | flops 3756032 | bytes 1032704 | tf_op jit(solution)/shard_map/ocr,ocd->rd/dot_general | solution.py:310
  69.3 0.0 collective-permute-start
  69.4 0.1 broadcast_in_dim.90
  69.4 0.1 convert_element_type.86
  69.5 4.5 %collective-permute-done = bf16[4,7168]{1,0:T(4,128)(2,1)S(1)} collective-permute-done((bf16[4,7168]{1,0:T(4,128)(2,1)S(1)}, bf16[4,7168]{1,0:T(4,128)(2,1)S(1)}, u32[]{:S(2)}, u32[]{:S(2)}) %collective-permute-start) | collective-permute-done | bytes 57376 | tf_op jit(solution)/shard_map/ppermute | solution.py:264
  74.1 0.2 fusion.6
  74.3 0.3 fusion.16
  74.5 0.9 copy.30.x_ref
  75.5 27.3 %shard_map.75.x_hbm = bf16[32,2,7168]{2,1,0:T(2,128)(2,1)} custom-call(bf16[8,2,7168]{2,1,0:T(2,128)(2,1)} %copy.30.x_ref), custom_call_target="tpu_custom_call" | custom-call | tf_op jit(solution)/shard_map/pallas_call | solution.py:69
  102.8 32.1 %shard_map.76 = (bf16[32,2,7168]{2,1,0:T(2,128)(2,1)}, bf16[32,2,7168]{2,1,0:T(2,128)(2,1)}) custom-call(bf16[32,2,7168]{2,1,0:T(2,128)(2,1)} %shard_map.75.x_hbm, bf16[7168,256]{1,0:T(8,128)(2,1)} %bitcast.62, bf16[7168,256]{1,0:T(8,128)(2,1)} %bitcast.64, bf16[256,7168]{1,0:T(8,128)(2,1)} %bitcast.66), custom_call_target="tpu_custom_call" | custom-call | tf_op jit(solution)/shard_map/pallas_call | solution.py:238
  134.9 1.5 %fusion.3 = bf16[4,7168]{1,0:T(4,128)(2,1)S(1)} fusion(bf16[32,2,4]{0,2,1:T(4,128)(2,1)S(1)} %convert_element_type.86, bf16[32,2,7168]{2,1,0:T(2,128)(2,1)} %get-tuple-element.8, bf16[4,7168]{1,0:T(4,128)(2,1)S(1)} %collective-permute-done), kind=kOutput, calls=%fused_computation.5 | convolution fusion | flops 3756032 | bytes 1032704 | tf_op jit(solution)/shard_map/ocr,ocd->rd/dot_general | solution.py:310
  136.4 4.8 %collective-permute-done.1 = bf16[4,7168]{1,0:T(4,128)(2,1)S(1)} collective-permute-done((bf16[4,7168]{1,0:T(4,128)(2,1)S(1)}, bf16[4,7168]{1,0:T(4,128)(2,1)S(1)}, u32[]{:S(2)}, u32[]{:S(2)}) %collective-permute-start.1) | collective-permute-done | bytes 57376 | tf_op jit(solution)/shard_map/ppermute | solution.py:264
  141.2 0.6 copy.33
  (17 shorter events, 0.2 us)
Async XLA Ops:
  35.9 31.8 %copy-start = (bf16[1,4,7168]{2,1,0:T(4,128)(2,1)S(1)}, bf16[1,4,7168]{2,1,0:T(4,128)(2,1)}, u32[]{:S(2)}) copy-start(bf16[1,4,7168]{2,1,0:T(4,128)(2,1)} %param.7) | copy-start | bytes 172036
  35.9 38.3 %copy-start.1 = (f32[1,7168]{1,0:T(1,128)S(1)}, f32[1,7168]{1,0:T(1,128)}, u32[]{:S(2)}) copy-start(f32[1,7168]{1,0:T(1,128)} %param.10) | copy-start | bytes 86020
  69.3 4.8 %collective-permute-start = (bf16[4,7168]{1,0:T(4,128)(2,1)S(1)}, bf16[4,7168]{1,0:T(4,128)(2,1)S(1)}, u32[]{:S(2)}, u32[]{:S(2)}) collective-permute-start(bf16[4,7168]{1,0:T(4,128)(2,1)S(1)} %fusion.2), channel_id=1, source_target_pairs={{0,32},{32,64},{64,96},{96,128},{128,160},{160,192},{192,224},{224... | collective-permute-start | bytes 172040 | tf_op jit(solution)/shard_map/ppermute | solution.py:264
  136.4 4.8 %collective-permute-start.1 = (bf16[4,7168]{1,0:T(4,128)(2,1)S(1)}, bf16[4,7168]{1,0:T(4,128)(2,1)S(1)}, u32[]{:S(2)}, u32[]{:S(2)}) collective-permute-start(bf16[4,7168]{1,0:T(4,128)(2,1)S(1)} %fusion.3), channel_id=1, source_target_pairs={{0,32},{32,64},{64,96},{96,128},{128,160},{160,192},{192,224},{224... | collective-permute-start | bytes 172040 | tf_op jit(solution)/shard_map/ppermute | solution.py:264

commit v15 on v14

--- a/solution.py
+++ b/solution.py
@@ -233,7 +233,7 @@
 def ffn_combine(x, gate_mat, up_mat, down_mat, collective_id):
     count, slots, model_dim = x.shape
     hidden = gate_mat.shape[1]
-    chunk = 1792
+    chunk = 3584
     steps = model_dim // chunk
     back, _ = pl.pallas_call(
         functools.partial(ffn_combine_kernel, count, steps, chunk),

time: 142 us -> 141 us (level)
  no operation moved by 1% of the time
where the time goes in v15:
time: 141 us
  Pallas kernels  121 us (86%)
  waiting for transfers between devices  9.34 us (7%)
  matrix products  4.32 us (3%)
  local copies, waits for them, and re-layouts  3.53 us (3%)
  other arithmetic  2.19 us (2%)
    pallas_call x2, Pallas kernels, ffn_combine(): pl.pallas_call(functools.partial(ffn_combine_kernel, count, steps, chunk)...  62.9 us
    pallas_call x2, Pallas kernels, exchange(): pl.pallas_call(functools.partial(exchange_kernel, count, spread), out_sha...  58.4 us
    ppermute x2, waiting for transfers between devices, shifted(): return lax.ppermute(value, axis, pairs)  9.34 us
    dot_general x2, matrix products, on_device(): jnp.einsum('ocr,ocd->rd', back_weight, back, preferred_element_type=jnp.f...  2.96 us
  transfers between devices with their start and end apart: 2, of which 2 were waited for; matrix products, arithmetic and copies ran while one was open for 0% of the time, Pallas kernels for 0%

profile of v15, /device:TPU:32, one launch (start us, length us, event | category | flops | bytes accessed | tf_op | source)
XLA Modules:
  0.0 140.8 jit_solution(11207071509573014353)
XLA Ops:
  0.0 0.7 slice_bitcast_fusion.1
  0.7 0.7 bitcast_convert_fusion.1
  1.4 0.1 fusion.23
  1.5 0.1 select_reduce_fusion.1
  1.6 0.1 broadcast_in_dim.86
  1.7 0.1 convert_element_type.77
  1.8 1.0 fusion.9
  2.8 1.1 fusion.13
  3.9 0.9 copy.31.x_ref
  4.8 31.1 %shard_map.73.x_hbm = bf16[32,2,7168]{2,1,0:T(2,128)(2,1)} custom-call(bf16[8,2,7168]{2,1,0:T(2,128)(2,1)} %copy.31.x_ref), custom_call_target="tpu_custom_call" | custom-call | tf_op jit(solution)/shard_map/pallas_call | solution.py:69
  36.0 31.3 %shard_map.74 = (bf16[32,2,7168]{2,1,0:T(2,128)(2,1)}, bf16[32,2,7168]{2,1,0:T(2,128)(2,1)}) custom-call(bf16[32,2,7168]{2,1,0:T(2,128)(2,1)} %shard_map.73.x_hbm, bf16[7168,256]{1,0:T(8,128)(2,1)} %bitcast.61, bf16[7168,256]{1,0:T(8,128)(2,1)} %bitcast.63, bf16[256,7168]{1,0:T(8,128)(2,1)} %bitcast.65), custom_call_target="tpu_custom_call" | custom-call | tf_op jit(solution)/shard_map/pallas_call | solution.py:238
  67.3 1.5 %fusion.2 = bf16[4,7168]{1,0:T(4,128)(2,1)S(1)} fusion(bf16[32,2,4]{0,2,1:T(4,128)(2,1)S(1)} %convert_element_type.77, bf16[32,2,7168]{2,1,0:T(2,128)(2,1)} %get-tuple-element.7, bf16[1,4,7168]{2,1,0:T(4,128)(2,1)S(1)} %copy-done), kind=kOutput, calls=%fused_computation.4 | convolution fusion | flops 3756032 | bytes 1032704 | tf_op jit(solution)/shard_map/ocr,ocd->rd/dot_general | solution.py:310
  68.7 0.0 collective-permute-start
  68.9 0.1 broadcast_in_dim.90
  68.9 0.1 convert_element_type.86
  69.0 4.5 %collective-permute-done = bf16[4,7168]{1,0:T(4,128)(2,1)S(1)} collective-permute-done((bf16[4,7168]{1,0:T(4,128)(2,1)S(1)}, bf16[4,7168]{1,0:T(4,128)(2,1)S(1)}, u32[]{:S(2)}, u32[]{:S(2)}) %collective-permute-start) | collective-permute-done | bytes 57376 | tf_op jit(solution)/shard_map/ppermute | solution.py:264
  73.6 0.2 fusion.6
  73.8 0.3 fusion.16
  74.0 0.9 copy.30.x_ref
  75.0 27.3 %shard_map.75.x_hbm = bf16[32,2,7168]{2,1,0:T(2,128)(2,1)} custom-call(bf16[8,2,7168]{2,1,0:T(2,128)(2,1)} %copy.30.x_ref), custom_call_target="tpu_custom_call" | custom-call | tf_op jit(solution)/shard_map/pallas_call | solution.py:69
  102.3 31.6 %shard_map.76 = (bf16[32,2,7168]{2,1,0:T(2,128)(2,1)}, bf16[32,2,7168]{2,1,0:T(2,128)(2,1)}) custom-call(bf16[32,2,7168]{2,1,0:T(2,128)(2,1)} %shard_map.75.x_hbm, bf16[7168,256]{1,0:T(8,128)(2,1)} %bitcast.62, bf16[7168,256]{1,0:T(8,128)(2,1)} %bitcast.64, bf16[256,7168]{1,0:T(8,128)(2,1)} %bitcast.66), custom_call_target="tpu_custom_call" | custom-call | tf_op jit(solution)/shard_map/pallas_call | solution.py:238
  133.9 1.5 %fusion.3 = bf16[4,7168]{1,0:T(4,128)(2,1)S(1)} fusion(bf16[32,2,4]{0,2,1:T(4,128)(2,1)S(1)} %convert_element_type.86, bf16[32,2,7168]{2,1,0:T(2,128)(2,1)} %get-tuple-element.8, bf16[4,7168]{1,0:T(4,128)(2,1)S(1)} %collective-permute-done), kind=kOutput, calls=%fused_computation.5 | convolution fusion | flops 3756032 | bytes 1032704 | tf_op jit(solution)/shard_map/ocr,ocd->rd/dot_general | solution.py:310
  135.4 4.8 %collective-permute-done.1 = bf16[4,7168]{1,0:T(4,128)(2,1)S(1)} collective-permute-done((bf16[4,7168]{1,0:T(4,128)(2,1)S(1)}, bf16[4,7168]{1,0:T(4,128)(2,1)S(1)}, u32[]{:S(2)}, u32[]{:S(2)}) %collective-permute-start.1) | collective-permute-done | bytes 57376 | tf_op jit(solution)/shard_map/ppermute | solution.py:264
  140.2 0.6 copy.33
  (17 shorter events, 0.2 us)
Async XLA Ops:
  35.9 31.3 %copy-start = (bf16[1,4,7168]{2,1,0:T(4,128)(2,1)S(1)}, bf16[1,4,7168]{2,1,0:T(4,128)(2,1)}, u32[]{:S(2)}) copy-start(bf16[1,4,7168]{2,1,0:T(4,128)(2,1)} %param.7) | copy-start | bytes 172036
  35.9 37.8 %copy-start.1 = (f32[1,7168]{1,0:T(1,128)S(1)}, f32[1,7168]{1,0:T(1,128)}, u32[]{:S(2)}) copy-start(f32[1,7168]{1,0:T(1,128)} %param.10) | copy-start | bytes 86020
  68.7 4.8 %collective-permute-start = (bf16[4,7168]{1,0:T(4,128)(2,1)S(1)}, bf16[4,7168]{1,0:T(4,128)(2,1)S(1)}, u32[]{:S(2)}, u32[]{:S(2)}) collective-permute-start(bf16[4,7168]{1,0:T(4,128)(2,1)S(1)} %fusion.2), channel_id=1, source_target_pairs={{0,32},{32,64},{64,96},{96,128},{128,160},{160,192},{192,224},{224... | collective-permute-start | bytes 172040 | tf_op jit(solution)/shard_map/ppermute | solution.py:264
  135.4 4.8 %collective-permute-start.1 = (bf16[4,7168]{1,0:T(4,128)(2,1)S(1)}, bf16[4,7168]{1,0:T(4,128)(2,1)S(1)}, u32[]{:S(2)}, u32[]{:S(2)}) collective-permute-start(bf16[4,7168]{1,0:T(4,128)(2,1)S(1)} %fusion.3), channel_id=1, source_target_pairs={{0,32},{32,64},{64,96},{96,128},{128,160},{160,192},{192,224},{224... | collective-permute-start | bytes 172040 | tf_op jit(solution)/shard_map/ppermute | solution.py:264

commit v16 on v14

--- a/solution.py
+++ b/solution.py
@@ -132,7 +132,8 @@
 
 
 def ffn_combine_kernel(count, steps, chunk, x_hbm, g_hbm, u_hbm, d_hbm, y_ref, terms_ref,
-                       acc_g, acc_u, inner, down_v, send_sem, recv_sem, own_sem, down_sem):
+                       acc_g, acc_u, inner, down_v, x_v, g_v, u_v,
+                       send_sem, recv_sem, own_sem, down_sem, in_sem):
     me = lax.axis_index("expert")
     seg = lax.axis_index("segment")
     sources, slots = x_hbm.shape[0], x_hbm.shape[1]
@@ -150,27 +151,32 @@
 
     lax.fori_loop(1, count, greet, 0)
 
+    def chunk_copies(k):
+        cols = pl.ds(k * chunk, chunk)
+        return (
+            pltpu.make_async_copy(x_hbm.at[:, :, cols], x_v.at[:, :, cols], in_sem.at[0, k]),
+            pltpu.make_async_copy(g_hbm.at[cols], g_v.at[cols], in_sem.at[1, k]),
+            pltpu.make_async_copy(u_hbm.at[cols], u_v.at[cols], in_sem.at[2, k]),
+        )
+
+    for k in range(steps):
+        for copy in chunk_copies(k):
+            copy.start()
+
     down_copy = pltpu.make_async_copy(d_hbm, down_v, down_sem)
     down_copy.start()
 
     acc_g[...] = jnp.zeros_like(acc_g)
     acc_u[...] = jnp.zeros_like(acc_u)
 
-    def gate_up(x_v, g_v, u_v):
+    for k in range(steps):
+        for copy in chunk_copies(k):
+            copy.wait()
+        cols = pl.ds(k * chunk, chunk)
         for c in range(slots):
-            xc = x_v[:, c, :]
-            acc_g[c] += jnp.dot(xc, g_v[...], preferred_element_type=jnp.float32)
-            acc_u[c] += jnp.dot(xc, u_v[...], preferred_element_type=jnp.float32)
-
-    pltpu.emit_pipeline(
-        gate_up,
-        grid=(steps,),
-        in_specs=[
-            pl.BlockSpec((sources, slots, chunk), lambda k: (0, 0, k)),
-            pl.BlockSpec((chunk, hidden), lambda k: (k, 0)),
-            pl.BlockSpec((chunk, hidden), lambda k: (k, 0)),
-        ],
-    )(x_hbm, g_hbm, u_hbm)
+            xc = x_v[:, c, cols]
+            acc_g[c] += jnp.dot(xc, g_v[cols, :], preferred_element_type=jnp.float32)
+            acc_u[c] += jnp.dot(xc, u_v[cols, :], preferred_element_type=jnp.float32)
 
     for c in range(slots):
         g = acc_g[c]
@@ -248,10 +254,14 @@
             pltpu.VMEM((slots, count, hidden), jnp.float32),
             pltpu.VMEM((slots, count, hidden), jnp.bfloat16),
             pltpu.VMEM((hidden, model_dim), down_mat.dtype),
+            pltpu.VMEM(x.shape, x.dtype),
+            pltpu.VMEM(gate_mat.shape, gate_mat.dtype),
+            pltpu.VMEM(up_mat.shape, up_mat.dtype),
             pltpu.SemaphoreType.DMA((count,)),
             pltpu.SemaphoreType.DMA((count,)),
             pltpu.SemaphoreType.DMA,
             pltpu.SemaphoreType.DMA,
+            pltpu.SemaphoreType.DMA((3, steps)),
         ],
         compiler_params=pltpu.CompilerParams(collective_id=collective_id, has_side_effects=True),
     )(x, gate_mat, up_mat, down_mat)

time: 142 us -> 138 us (0.972)
  Pallas kernels: 122 us -> 118 us
    pallas_call x2, Pallas kernels: 63.9 us -> 59.7 us  [ffn_combine(): pl.pallas_call(functools.partial(ffn_combine_kernel, count, steps, chunk)...]
where the time goes in v16:
time: 138 us
  Pallas kernels  118 us (86%)
  waiting for transfers between devices  9.34 us (7%)
  matrix products  4.32 us (3%)
  local copies, waits for them, and re-layouts  3.53 us (3%)
  other arithmetic  2.19 us (2%)
    pallas_call x2, Pallas kernels, ffn_combine(): pl.pallas_call(functools.partial(ffn_combine_kernel, count, steps, chunk)...  59.7 us
    pallas_call x2, Pallas kernels, exchange(): pl.pallas_call(functools.partial(exchange_kernel, count, spread), out_sha...  58.4 us
    ppermute x2, waiting for transfers between devices, shifted(): return lax.ppermute(value, axis, pairs)  9.34 us
    dot_general x2, matrix products, on_device(): jnp.einsum('ocr,ocd->rd', back_weight, back, preferred_element_type=jnp.f...  2.96 us
  transfers between devices with their start and end apart: 2, of which 2 were waited for; matrix products, arithmetic and copies ran while one was open for 0% of the time, Pallas kernels for 0%

profile of v16, /device:TPU:32, one launch (start us, length us, event | category | flops | bytes accessed | tf_op | source)
XLA Modules:
  0.0 137.6 jit_solution(11964321536136570609)
XLA Ops:
  0.0 0.7 slice_bitcast_fusion.1
  0.7 0.7 bitcast_convert_fusion.1
  1.4 0.1 fusion.23
  1.5 0.1 select_reduce_fusion.1
  1.6 0.1 broadcast_in_dim.86
  1.7 0.1 convert_element_type.77
  1.8 1.0 fusion.9
  2.8 1.1 fusion.13
  3.9 0.9 copy.31.x_ref
  4.8 31.1 %shard_map.73.x_hbm = bf16[32,2,7168]{2,1,0:T(2,128)(2,1)} custom-call(bf16[8,2,7168]{2,1,0:T(2,128)(2,1)} %copy.31.x_ref), custom_call_target="tpu_custom_call" | custom-call | tf_op jit(solution)/shard_map/pallas_call | solution.py:69
  36.0 29.7 %shard_map.74 = (bf16[32,2,7168]{2,1,0:T(2,128)(2,1)}, bf16[32,2,7168]{2,1,0:T(2,128)(2,1)}) custom-call(bf16[32,2,7168]{2,1,0:T(2,128)(2,1)} %shard_map.73.x_hbm, bf16[7168,256]{1,0:T(8,128)(2,1)} %bitcast.61, bf16[7168,256]{1,0:T(8,128)(2,1)} %bitcast.63, bf16[256,7168]{1,0:T(8,128)(2,1)} %bitcast.65), custom_call_target="tpu_custom_call" | custom-call | tf_op jit(solution)/shard_map/pallas_call | solution.py:244
  65.7 1.5 %fusion.2 = bf16[4,7168]{1,0:T(4,128)(2,1)S(1)} fusion(bf16[32,2,4]{0,2,1:T(4,128)(2,1)S(1)} %convert_element_type.77, bf16[32,2,7168]{2,1,0:T(2,128)(2,1)} %get-tuple-element.7, bf16[1,4,7168]{2,1,0:T(4,128)(2,1)S(1)} %copy-done), kind=kOutput, calls=%fused_computation.4 | convolution fusion | flops 3756032 | bytes 1032704 | tf_op jit(solution)/shard_map/ocr,ocd->rd/dot_general | solution.py:320
  67.3 0.1 broadcast_in_dim.90
  67.3 0.1 convert_element_type.86
  67.4 4.5 %collective-permute-done = bf16[4,7168]{1,0:T(4,128)(2,1)S(1)} collective-permute-done((bf16[4,7168]{1,0:T(4,128)(2,1)S(1)}, bf16[4,7168]{1,0:T(4,128)(2,1)S(1)}, u32[]{:S(2)}, u32[]{:S(2)}) %collective-permute-start) | collective-permute-done | bytes 57376 | tf_op jit(solution)/shard_map/ppermute | solution.py:274
  72.0 0.2 fusion.6
  72.2 0.3 fusion.16
  72.4 0.9 copy.30.x_ref
  73.4 27.3 %shard_map.75.x_hbm = bf16[32,2,7168]{2,1,0:T(2,128)(2,1)} custom-call(bf16[8,2,7168]{2,1,0:T(2,128)(2,1)} %copy.30.x_ref), custom_call_target="tpu_custom_call" | custom-call | tf_op jit(solution)/shard_map/pallas_call | solution.py:69
  100.7 30.0 %shard_map.76 = (bf16[32,2,7168]{2,1,0:T(2,128)(2,1)}, bf16[32,2,7168]{2,1,0:T(2,128)(2,1)}) custom-call(bf16[32,2,7168]{2,1,0:T(2,128)(2,1)} %shard_map.75.x_hbm, bf16[7168,256]{1,0:T(8,128)(2,1)} %bitcast.62, bf16[7168,256]{1,0:T(8,128)(2,1)} %bitcast.64, bf16[256,7168]{1,0:T(8,128)(2,1)} %bitcast.66), custom_call_target="tpu_custom_call" | custom-call | tf_op jit(solution)/shard_map/pallas_call | solution.py:244
  130.7 1.5 %fusion.3 = bf16[4,7168]{1,0:T(4,128)(2,1)S(1)} fusion(bf16[32,2,4]{0,2,1:T(4,128)(2,1)S(1)} %convert_element_type.86, bf16[32,2,7168]{2,1,0:T(2,128)(2,1)} %get-tuple-element.8, bf16[4,7168]{1,0:T(4,128)(2,1)S(1)} %collective-permute-done), kind=kOutput, calls=%fused_computation.5 | convolution fusion | flops 3756032 | bytes 1032704 | tf_op jit(solution)/shard_map/ocr,ocd->rd/dot_general | solution.py:320
  132.2 0.0 collective-permute-start.1
  132.2 4.8 %collective-permute-done.1 = bf16[4,7168]{1,0:T(4,128)(2,1)S(1)} collective-permute-done((bf16[4,7168]{1,0:T(4,128)(2,1)S(1)}, bf16[4,7168]{1,0:T(4,128)(2,1)S(1)}, u32[]{:S(2)}, u32[]{:S(2)}) %collective-permute-start.1) | collective-permute-done | bytes 57376 | tf_op jit(solution)/shard_map/ppermute | solution.py:274
  137.0 0.6 copy.33
  (17 shorter events, 0.2 us)
Async XLA Ops:
  35.9 29.7 %copy-start = (bf16[1,4,7168]{2,1,0:T(4,128)(2,1)S(1)}, bf16[1,4,7168]{2,1,0:T(4,128)(2,1)}, u32[]{:S(2)}) copy-start(bf16[1,4,7168]{2,1,0:T(4,128)(2,1)} %param.7) | copy-start | bytes 172036
  35.9 36.2 %copy-start.1 = (f32[1,7168]{1,0:T(1,128)S(1)}, f32[1,7168]{1,0:T(1,128)}, u32[]{:S(2)}) copy-start(f32[1,7168]{1,0:T(1,128)} %param.10) | copy-start | bytes 86020
  67.1 4.8 %collective-permute-start = (bf16[4,7168]{1,0:T(4,128)(2,1)S(1)}, bf16[4,7168]{1,0:T(4,128)(2,1)S(1)}, u32[]{:S(2)}, u32[]{:S(2)}) collective-permute-start(bf16[4,7168]{1,0:T(4,128)(2,1)S(1)} %fusion.2), channel_id=1, source_target_pairs={{0,32},{32,64},{64,96},{96,128},{128,160},{160,192},{192,224},{224... | collective-permute-start | bytes 172040 | tf_op jit(solution)/shard_map/ppermute | solution.py:274
  132.2 4.8 %collective-permute-start.1 = (bf16[4,7168]{1,0:T(4,128)(2,1)S(1)}, bf16[4,7168]{1,0:T(4,128)(2,1)S(1)}, u32[]{:S(2)}, u32[]{:S(2)}) collective-permute-start(bf16[4,7168]{1,0:T(4,128)(2,1)S(1)} %fusion.3), channel_id=1, source_target_pairs={{0,32},{32,64},{64,96},{96,128},{128,160},{160,192},{192,224},{224... | collective-permute-start | bytes 172040 | tf_op jit(solution)/shard_map/ppermute | solution.py:274

commit v17 on v16

--- a/solution.py
+++ b/solution.py
@@ -239,7 +239,7 @@
 def ffn_combine(x, gate_mat, up_mat, down_mat, collective_id):
     count, slots, model_dim = x.shape
     hidden = gate_mat.shape[1]
-    chunk = 1792
+    chunk = 1024
     steps = model_dim // chunk
     back, _ = pl.pallas_call(
         functools.partial(ffn_combine_kernel, count, steps, chunk),

time: 138 us -> 138 us (level)
  no operation moved by 1% of the time
where the time goes in v17:
time: 138 us
  Pallas kernels  118 us (86%)
  waiting for transfers between devices  9.34 us (7%)
  matrix products  4.32 us (3%)
  local copies, waits for them, and re-layouts  3.53 us (3%)
  other arithmetic  2.19 us (2%)
    pallas_call x2, Pallas kernels, ffn_combine(): pl.pallas_call(functools.partial(ffn_combine_kernel, count, steps, chunk)...  59.8 us
    pallas_call x2, Pallas kernels, exchange(): pl.pallas_call(functools.partial(exchange_kernel, count, spread), out_sha...  58.4 us
    ppermute x2, waiting for transfers between devices, shifted(): return lax.ppermute(value, axis, pairs)  9.34 us
    dot_general x2, matrix products, on_device(): jnp.einsum('ocr,ocd->rd', back_weight, back, preferred_element_type=jnp.f...  2.96 us
  transfers between devices with their start and end apart: 2, of which 2 were waited for; matrix products, arithmetic and copies ran while one was open for 0% of the time, Pallas kernels for 0%

profile of v17, /device:TPU:32, one launch (start us, length us, event | category | flops | bytes accessed | tf_op | source)
XLA Modules:
  0.0 137.8 jit_solution(1453521852609441080)
XLA Ops:
  0.0 0.7 slice_bitcast_fusion.1
  0.7 0.7 bitcast_convert_fusion.1
  1.4 0.1 fusion.23
  1.5 0.1 select_reduce_fusion.1
  1.6 0.1 broadcast_in_dim.86
  1.7 0.1 convert_element_type.77
  1.8 1.0 fusion.9
  2.8 1.1 fusion.13
  3.9 0.9 copy.31.x_ref
  4.8 31.1 %shard_map.73.x_hbm = bf16[32,2,7168]{2,1,0:T(2,128)(2,1)} custom-call(bf16[8,2,7168]{2,1,0:T(2,128)(2,1)} %copy.31.x_ref), custom_call_target="tpu_custom_call" | custom-call | tf_op jit(solution)/shard_map/pallas_call | solution.py:69
  36.0 29.8 %shard_map.74 = (bf16[32,2,7168]{2,1,0:T(2,128)(2,1)}, bf16[32,2,7168]{2,1,0:T(2,128)(2,1)}) custom-call(bf16[32,2,7168]{2,1,0:T(2,128)(2,1)} %shard_map.73.x_hbm, bf16[7168,256]{1,0:T(8,128)(2,1)} %bitcast.61, bf16[7168,256]{1,0:T(8,128)(2,1)} %bitcast.63, bf16[256,7168]{1,0:T(8,128)(2,1)} %bitcast.65), custom_call_target="tpu_custom_call" | custom-call | tf_op jit(solution)/shard_map/pallas_call | solution.py:244
  65.7 1.5 %fusion.2 = bf16[4,7168]{1,0:T(4,128)(2,1)S(1)} fusion(bf16[32,2,4]{0,2,1:T(4,128)(2,1)S(1)} %convert_element_type.77, bf16[32,2,7168]{2,1,0:T(2,128)(2,1)} %get-tuple-element.7, bf16[1,4,7168]{2,1,0:T(4,128)(2,1)S(1)} %copy-done), kind=kOutput, calls=%fused_computation.4 | convolution fusion | flops 3756032 | bytes 1032704 | tf_op jit(solution)/shard_map/ocr,ocd->rd/dot_general | solution.py:320
  67.2 0.0 collective-permute-start
  67.3 0.1 broadcast_in_dim.90
  67.4 0.1 convert_element_type.86
  67.5 4.5 %collective-permute-done = bf16[4,7168]{1,0:T(4,128)(2,1)S(1)} collective-permute-done((bf16[4,7168]{1,0:T(4,128)(2,1)S(1)}, bf16[4,7168]{1,0:T(4,128)(2,1)S(1)}, u32[]{:S(2)}, u32[]{:S(2)}) %collective-permute-start) | collective-permute-done | bytes 57376 | tf_op jit(solution)/shard_map/ppermute | solution.py:274
  72.0 0.2 fusion.6
  72.2 0.3 fusion.16
  72.5 0.9 copy.30.x_ref
  73.4 27.3 %shard_map.75.x_hbm = bf16[32,2,7168]{2,1,0:T(2,128)(2,1)} custom-call(bf16[8,2,7168]{2,1,0:T(2,128)(2,1)} %copy.30.x_ref), custom_call_target="tpu_custom_call" | custom-call | tf_op jit(solution)/shard_map/pallas_call | solution.py:69
  100.8 30.1 %shard_map.76 = (bf16[32,2,7168]{2,1,0:T(2,128)(2,1)}, bf16[32,2,7168]{2,1,0:T(2,128)(2,1)}) custom-call(bf16[32,2,7168]{2,1,0:T(2,128)(2,1)} %shard_map.75.x_hbm, bf16[7168,256]{1,0:T(8,128)(2,1)} %bitcast.62, bf16[7168,256]{1,0:T(8,128)(2,1)} %bitcast.64, bf16[256,7168]{1,0:T(8,128)(2,1)} %bitcast.66), custom_call_target="tpu_custom_call" | custom-call | tf_op jit(solution)/shard_map/pallas_call | solution.py:244
  130.8 1.5 %fusion.3 = bf16[4,7168]{1,0:T(4,128)(2,1)S(1)} fusion(bf16[32,2,4]{0,2,1:T(4,128)(2,1)S(1)} %convert_element_type.86, bf16[32,2,7168]{2,1,0:T(2,128)(2,1)} %get-tuple-element.8, bf16[4,7168]{1,0:T(4,128)(2,1)S(1)} %collective-permute-done), kind=kOutput, calls=%fused_computation.5 | convolution fusion | flops 3756032 | bytes 1032704 | tf_op jit(solution)/shard_map/ocr,ocd->rd/dot_general | solution.py:320
  132.3 4.8 %collective-permute-done.1 = bf16[4,7168]{1,0:T(4,128)(2,1)S(1)} collective-permute-done((bf16[4,7168]{1,0:T(4,128)(2,1)S(1)}, bf16[4,7168]{1,0:T(4,128)(2,1)S(1)}, u32[]{:S(2)}, u32[]{:S(2)}) %collective-permute-start.1) | collective-permute-done | bytes 57376 | tf_op jit(solution)/shard_map/ppermute | solution.py:274
  137.2 0.6 copy.33
  (17 shorter events, 0.2 us)
Async XLA Ops:
  35.9 29.8 %copy-start = (bf16[1,4,7168]{2,1,0:T(4,128)(2,1)S(1)}, bf16[1,4,7168]{2,1,0:T(4,128)(2,1)}, u32[]{:S(2)}) copy-start(bf16[1,4,7168]{2,1,0:T(4,128)(2,1)} %param.7) | copy-start | bytes 172036
  35.9 36.3 %copy-start.1 = (f32[1,7168]{1,0:T(1,128)S(1)}, f32[1,7168]{1,0:T(1,128)}, u32[]{:S(2)}) copy-start(f32[1,7168]{1,0:T(1,128)} %param.10) | copy-start | bytes 86020
  67.2 4.8 %collective-permute-start = (bf16[4,7168]{1,0:T(4,128)(2,1)S(1)}, bf16[4,7168]{1,0:T(4,128)(2,1)S(1)}, u32[]{:S(2)}, u32[]{:S(2)}) collective-permute-start(bf16[4,7168]{1,0:T(4,128)(2,1)S(1)} %fusion.2), channel_id=1, source_target_pairs={{0,32},{32,64},{64,96},{96,128},{128,160},{160,192},{192,224},{224... | collective-permute-start | bytes 172040 | tf_op jit(solution)/shard_map/ppermute | solution.py:274
  132.3 4.8 %collective-permute-start.1 = (bf16[4,7168]{1,0:T(4,128)(2,1)S(1)}, bf16[4,7168]{1,0:T(4,128)(2,1)S(1)}, u32[]{:S(2)}, u32[]{:S(2)}) collective-permute-start(bf16[4,7168]{1,0:T(4,128)(2,1)S(1)} %fusion.3), channel_id=1, source_target_pairs={{0,32},{32,64},{64,96},{96,128},{128,160},{160,192},{192,224},{224... | collective-permute-start | bytes 172040 | tf_op jit(solution)/shard_map/ppermute | solution.py:274

commit v18 on v16

--- a/solution.py
+++ b/solution.py
@@ -132,7 +132,7 @@
 
 
 def ffn_combine_kernel(count, steps, chunk, x_hbm, g_hbm, u_hbm, d_hbm, y_ref, terms_ref,
-                       acc_g, acc_u, inner, down_v, x_v, g_v, u_v,
+                       acc_g, acc_u, inner, down_v, x_v, g_v, u_v, t_v,
                        send_sem, recv_sem, own_sem, down_sem, in_sem):
     me = lax.axis_index("expert")
     seg = lax.axis_index("segment")
@@ -184,17 +184,13 @@
 
     down_copy.wait()
 
-    def down(o_v):
-        for c in range(slots):
-            o_v[:, c, :] = jnp.dot(
-                inner[c], down_v[...], preferred_element_type=jnp.float32
-            ).astype(o_v.dtype)
-
-    pltpu.emit_pipeline(
-        down,
-        grid=(1,),
-        out_specs=[pl.BlockSpec((sources, slots, model_dim), lambda k: (0, 0, 0))],
-    )(terms_ref)
+    for c in range(slots):
+        t_v[:, c, :] = jnp.dot(
+            inner[c], down_v[...], preferred_element_type=jnp.float32
+        ).astype(t_v.dtype)
+    terms_out = pltpu.make_async_copy(t_v, terms_ref, down_sem)
+    terms_out.start()
+    terms_out.wait()
 
     pl.semaphore_wait(barrier, count - 1)
 
@@ -257,6 +253,7 @@
             pltpu.VMEM(x.shape, x.dtype),
             pltpu.VMEM(gate_mat.shape, gate_mat.dtype),
             pltpu.VMEM(up_mat.shape, up_mat.dtype),
+            pltpu.VMEM(x.shape, jnp.bfloat16),
             pltpu.SemaphoreType.DMA((count,)),
             pltpu.SemaphoreType.DMA((count,)),
             pltpu.SemaphoreType.DMA,

time: 138 us -> 138 us (level)
  no operation moved by 1% of the time
where the time goes in v18:
time: 138 us
  Pallas kernels  118 us (86%)
  waiting for transfers between devices  9.34 us (7%)
  matrix products  4.32 us (3%)
  local copies, waits for them, and re-layouts  3.53 us (3%)
  other arithmetic  2.19 us (2%)
    pallas_call x2, Pallas kernels, ffn_combine(): pl.pallas_call(functools.partial(ffn_combine_kernel, count, steps, chunk)...  59.7 us
    pallas_call x2, Pallas kernels, exchange(): pl.pallas_call(functools.partial(exchange_kernel, count, spread), out_sha...  58.4 us
    ppermute x2, waiting for transfers between devices, shifted(): return lax.ppermute(value, axis, pairs)  9.34 us
    dot_general x2, matrix products, on_device(): jnp.einsum('ocr,ocd->rd', back_weight, back, preferred_element_type=jnp.f...  2.96 us
  transfers between devices with their start and end apart: 2, of which 2 were waited for; matrix products, arithmetic and copies ran while one was open for 0% of the time, Pallas kernels for 0%

profile of v18, /device:TPU:32, one launch (start us, length us, event | category | flops | bytes accessed | tf_op | source)
XLA Modules:
  0.0 137.6 jit_solution(3410602841780840063)
XLA Ops:
  0.0 0.7 slice_bitcast_fusion.1
  0.7 0.7 bitcast_convert_fusion.1
  1.4 0.1 fusion.23
  1.5 0.1 select_reduce_fusion.1
  1.6 0.1 broadcast_in_dim.86
  1.7 0.1 convert_element_type.77
  1.8 1.0 fusion.9
  2.8 1.1 fusion.13
  3.9 0.9 copy.31.x_ref
  4.8 31.1 %shard_map.73.x_hbm = bf16[32,2,7168]{2,1,0:T(2,128)(2,1)} custom-call(bf16[8,2,7168]{2,1,0:T(2,128)(2,1)} %copy.31.x_ref), custom_call_target="tpu_custom_call" | custom-call | tf_op jit(solution)/shard_map/pallas_call | solution.py:69
  36.0 29.7 %shard_map.74 = (bf16[32,2,7168]{2,1,0:T(2,128)(2,1)}, bf16[32,2,7168]{2,1,0:T(2,128)(2,1)}) custom-call(bf16[32,2,7168]{2,1,0:T(2,128)(2,1)} %shard_map.73.x_hbm, bf16[7168,256]{1,0:T(8,128)(2,1)} %bitcast.61, bf16[7168,256]{1,0:T(8,128)(2,1)} %bitcast.63, bf16[256,7168]{1,0:T(8,128)(2,1)} %bitcast.65), custom_call_target="tpu_custom_call" | custom-call | tf_op jit(solution)/shard_map/pallas_call | solution.py:240
  65.7 1.5 %fusion.2 = bf16[4,7168]{1,0:T(4,128)(2,1)S(1)} fusion(bf16[32,2,4]{0,2,1:T(4,128)(2,1)S(1)} %convert_element_type.77, bf16[32,2,7168]{2,1,0:T(2,128)(2,1)} %get-tuple-element.7, bf16[1,4,7168]{2,1,0:T(4,128)(2,1)S(1)} %copy-done), kind=kOutput, calls=%fused_computation.4 | convolution fusion | flops 3756032 | bytes 1032704 | tf_op jit(solution)/shard_map/ocr,ocd->rd/dot_general | solution.py:317
  67.1 0.0 collective-permute-start
  67.3 0.1 broadcast_in_dim.90
  67.3 0.1 convert_element_type.86
  67.4 4.5 %collective-permute-done = bf16[4,7168]{1,0:T(4,128)(2,1)S(1)} collective-permute-done((bf16[4,7168]{1,0:T(4,128)(2,1)S(1)}, bf16[4,7168]{1,0:T(4,128)(2,1)S(1)}, u32[]{:S(2)}, u32[]{:S(2)}) %collective-permute-start) | collective-permute-done | bytes 57376 | tf_op jit(solution)/shard_map/ppermute | solution.py:271
  72.0 0.2 fusion.6
  72.2 0.3 fusion.16
  72.4 0.9 copy.30.x_ref
  73.4 27.3 %shard_map.75.x_hbm = bf16[32,2,7168]{2,1,0:T(2,128)(2,1)} custom-call(bf16[8,2,7168]{2,1,0:T(2,128)(2,1)} %copy.30.x_ref), custom_call_target="tpu_custom_call" | custom-call | tf_op jit(solution)/shard_map/pallas_call | solution.py:69
  100.7 30.0 %shard_map.76 = (bf16[32,2,7168]{2,1,0:T(2,128)(2,1)}, bf16[32,2,7168]{2,1,0:T(2,128)(2,1)}) custom-call(bf16[32,2,7168]{2,1,0:T(2,128)(2,1)} %shard_map.75.x_hbm, bf16[7168,256]{1,0:T(8,128)(2,1)} %bitcast.62, bf16[7168,256]{1,0:T(8,128)(2,1)} %bitcast.64, bf16[256,7168]{1,0:T(8,128)(2,1)} %bitcast.66), custom_call_target="tpu_custom_call" | custom-call | tf_op jit(solution)/shard_map/pallas_call | solution.py:240
  130.7 1.5 %fusion.3 = bf16[4,7168]{1,0:T(4,128)(2,1)S(1)} fusion(bf16[32,2,4]{0,2,1:T(4,128)(2,1)S(1)} %convert_element_type.86, bf16[32,2,7168]{2,1,0:T(2,128)(2,1)} %get-tuple-element.8, bf16[4,7168]{1,0:T(4,128)(2,1)S(1)} %collective-permute-done), kind=kOutput, calls=%fused_computation.5 | convolution fusion | flops 3756032 | bytes 1032704 | tf_op jit(solution)/shard_map/ocr,ocd->rd/dot_general | solution.py:317
  132.2 4.8 %collective-permute-done.1 = bf16[4,7168]{1,0:T(4,128)(2,1)S(1)} collective-permute-done((bf16[4,7168]{1,0:T(4,128)(2,1)S(1)}, bf16[4,7168]{1,0:T(4,128)(2,1)S(1)}, u32[]{:S(2)}, u32[]{:S(2)}) %collective-permute-start.1) | collective-permute-done | bytes 57376 | tf_op jit(solution)/shard_map/ppermute | solution.py:271
  137.0 0.6 copy.33
  (17 shorter events, 0.2 us)
Async XLA Ops:
  35.9 29.7 %copy-start = (bf16[1,4,7168]{2,1,0:T(4,128)(2,1)S(1)}, bf16[1,4,7168]{2,1,0:T(4,128)(2,1)}, u32[]{:S(2)}) copy-start(bf16[1,4,7168]{2,1,0:T(4,128)(2,1)} %param.7) | copy-start | bytes 172036
  35.9 36.2 %copy-start.1 = (f32[1,7168]{1,0:T(1,128)S(1)}, f32[1,7168]{1,0:T(1,128)}, u32[]{:S(2)}) copy-start(f32[1,7168]{1,0:T(1,128)} %param.10) | copy-start | bytes 86020
  67.1 4.8 %collective-permute-start = (bf16[4,7168]{1,0:T(4,128)(2,1)S(1)}, bf16[4,7168]{1,0:T(4,128)(2,1)S(1)}, u32[]{:S(2)}, u32[]{:S(2)}) collective-permute-start(bf16[4,7168]{1,0:T(4,128)(2,1)S(1)} %fusion.2), channel_id=1, source_target_pairs={{0,32},{32,64},{64,96},{96,128},{128,160},{160,192},{192,224},{224... | collective-permute-start | bytes 172040 | tf_op jit(solution)/shard_map/ppermute | solution.py:271
  132.2 4.8 %collective-permute-start.1 = (bf16[4,7168]{1,0:T(4,128)(2,1)S(1)}, bf16[4,7168]{1,0:T(4,128)(2,1)S(1)}, u32[]{:S(2)}, u32[]{:S(2)}) collective-permute-start(bf16[4,7168]{1,0:T(4,128)(2,1)S(1)} %fusion.3), channel_id=1, source_target_pairs={{0,32},{32,64},{64,96},{96,128},{128,160},{160,192},{192,224},{224... | collective-permute-start | bytes 172040 | tf_op jit(solution)/shard_map/ppermute | solution.py:271
